TPU v7x, 128 devices: a whole 4x4x4 slice. The times are simulated.
128 devices in a mesh: tm: 16 (over z, x), mp: 8 (over y, core).
Axes of the slice: x: 4, y: 4, z: 4, core: 2. Of those that a mesh axis runs over, the one named last changes fastest.
Arguments:
- frames: bfloat16 [1536, 8192], P('mp', 'tm'), may hold values from -40 to 40
- norm_gain: float32 [1536], replicated, may hold values from 0.1 to 1.9
- w_qkv: bfloat16 [3, 1536, 1536], P(None, 'mp'), may hold values from -0.76546554 to 0.76546554
- w_out: bfloat16 [1536, 1536], P('mp'), may hold values from -0.15625 to 0.15625
- conv_kernel: float32 [31, 1536], P(None, 'mp'), may hold values from -1 to 1
- grad_out: bfloat16 [1536, 8192], P('mp', 'tm'), may hold values from -6 to 6
Outputs:
- block_out: bfloat16 [1536, 8192], P('mp', 'tm')
- grad_frames: bfloat16 [1536, 8192], P('mp', 'tm')
- grad_gain: float32 [1536], P('mp')
- grad_qkv: float32 [3, 1536, 1536], P(None, 'mp')
- grad_out_proj: float32 [1536, 1536], P('mp')
- grad_kernel: float32 [31, 1536], P(None, 'mp')
All inputs are finite; a program needn't handle non-finite values.
Results may differ from a plain program's by a relative error of at most 0.023.
The roundings to bfloat16 on the way count: a program that leaves them out, or rounds other values in their place, can miss the bound.
Values may be sent and summed in bfloat16 or wider, within the bound.
No kernel may reach another device: no remote copies, remote signals or barrier semaphores. Data moves between devices by JAX's collectives and lax.ppermute only.
A program may use at most 128 MiB of HBM per device.

v0:
```python
import functools

import jax
import jax.numpy as jnp
from jax import lax
from jax.experimental import pallas as pl
from jax.experimental.pallas import tpu as pltpu
from jax.sharding import PartitionSpec as P


HEAD_DIM = 64
SIDE = 4
PAD = 16
F32 = jnp.float32
BF16 = jnp.bfloat16


def nn(a, b):
    return jnp.dot(a, b, preferred_element_type=F32)


def nt(a, b):
    return lax.dot_general(a, b, (((1,), (1,)), ((), ())), preferred_element_type=F32)


VM = pl.BlockSpec(memory_space=pltpu.VMEM)


STEP = 64


def fill(pad_ref, left_ref, own_ref, right_ref):
    count = own_ref.shape[1]
    slab = left_ref.shape[1]
    pad_ref[PAD : PAD + count, :] = own_ref[...].astype(F32).T
    pad_ref[:PAD, :] = left_ref[...].astype(F32).T[slab - PAD :, :]
    pad_ref[PAD + count :, :] = right_ref[...].astype(F32).T[:PAD, :]


def back_kernel(left_ref, own_ref, right_ref, taps_ref, sum_ref, cast_ref, pad_ref, acc_ref, near):
    count = own_ref.shape[1]
    fill(pad_ref, left_ref, own_ref, right_ref)
    taps = taps_ref.shape[0]
    half = taps // 2

    def step(i, carry):
        base = pl.multiple_of(i * STEP, STEP)
        near[...] = pad_ref[pl.ds(base, STEP + 2 * PAD), :]
        acc = near[PAD : PAD + STEP, :]
        for j in range(taps):
            start = PAD + half - j
            acc = acc + taps_ref[j : j + 1, :] * near[start : start + STEP, :]
        acc_ref[pl.ds(base, STEP), :] = acc
        return carry

    lax.fori_loop(0, count // STEP, step, 0)
    acc = acc_ref[...].T
    sum_ref[...] = acc
    cast_ref[...] = acc.astype(BF16)


def conv_body(left_ref, own_ref, right_ref, up_ref, taps_ref, out_ref, grad_ref, pad_ref, upt_ref, sums, near):
    count = own_ref.shape[1]
    fill(pad_ref, left_ref, own_ref, right_ref)
    upt_ref[...] = up_ref[...].astype(F32).T
    taps = taps_ref.shape[0]
    half = taps // 2
    sums[...] = jnp.zeros_like(sums)

    def step(i, carry):
        base = pl.multiple_of(i * STEP, STEP)
        near[...] = pad_ref[pl.ds(base, STEP + 2 * PAD), :]
        acc = near[PAD : PAD + STEP, :]
        up = upt_ref[pl.ds(base, STEP), :]
        for j in range(taps):
            start = PAD + j - half
            part = near[start : start + STEP, :]
            acc = acc + taps_ref[j : j + 1, :] * part
            prod = up * part
            sums[j] += sum(prod[8 * s : 8 * s + 8] for s in range(STEP // 8))
        upt_ref[pl.ds(base, STEP), :] = acc
        return carry

    lax.fori_loop(0, count // STEP, step, 0)
    for j in range(taps):
        grad_ref[j : j + 1, :] = jnp.sum(sums[j], axis=0, keepdims=True)
    out_ref[...] = upt_ref[...].T.astype(BF16)


def shift_x(a, by):
    pairs = [
        (z * SIDE + x, z * SIDE + (x + by) % SIDE) for z in range(SIDE) for x in range(SIDE)
    ]
    return lax.ppermute(a, "tm", pairs)


def shift_z(a, by):
    pairs = [
        (z * SIDE + x, ((z + by) % SIDE) * SIDE + x) for z in range(SIDE) for x in range(SIDE)
    ]
    return lax.ppermute(a, "tm", pairs)


def halos(a, slab=128):
    count = lax.axis_size("tm")
    ends = count - 1
    left = lax.ppermute(a[:, a.shape[1] - slab :], "tm", [(i, i + 1) for i in range(ends)])
    right = lax.ppermute(a[:, :slab], "tm", [(i + 1, i) for i in range(ends)])
    return left, right


SM = pl.BlockSpec(memory_space=pltpu.SMEM)


def shift_y(a, by):
    count = lax.axis_size("mp") // 2
    pairs = [(y * 2 + c, ((y + by) % count) * 2 + c) for y in range(count) for c in range(2)]
    return lax.ppermute(a, "mp", pairs)


def swap_core(a):
    count = lax.axis_size("mp")
    return lax.ppermute(a, "mp", [(i, i ^ 1) for i in range(count)])


def call(body, outs, args, specs=None, scratch=(), flops=0, exps=0):
    out_shape = tuple(jax.ShapeDtypeStruct(s, t) for s, t in outs)
    moved = sum(a.size * a.dtype.itemsize for a in args)
    moved += sum(o.size * o.dtype.itemsize for o in out_shape)
    return pl.pallas_call(
        body,
        out_shape=out_shape,
        in_specs=specs or [VM] * len(args),
        out_specs=[VM] * len(outs),
        scratch_shapes=list(scratch),
        cost_estimate=pl.CostEstimate(flops=flops, bytes_accessed=moved, transcendentals=exps),
    )(*args)


def ring(shift, blocks, sign):
    return [blocks[0]] + [shift(blocks[r], sign * r) for r in range(1, SIDE)]


def head_rows(h):
    return slice(h * HEAD_DIM, (h + 1) * HEAD_DIM)


def prep_body(pos_ref, w_ref, wo_ref, wq_out, wo_out, mixed, turned, turned_out):
    head_cols, width = wo_ref.shape
    heads = head_cols // HEAD_DIM
    for h in range(heads):
        for j in range(3):
            at = (h * 3 + j) * HEAD_DIM
            mixed[at : at + HEAD_DIM, :] = w_ref[j, head_rows(h), :]
    turned[...] = mixed[...].T
    turned_out[...] = wo_ref[...].T
    chunk = width // 8
    for r in range(8):
        rows = pl.ds(pl.multiple_of(pos_ref[r] * chunk, chunk), chunk)
        wq_out[r * chunk : (r + 1) * chunk, :] = turned[rows, :]
        wo_out[r * chunk : (r + 1) * chunk, :] = turned_out[rows, :]


def norm_body(pos_ref, b0, b1, b2, b3, other, gain_ref, w_ref, normed_out, inv_out, q_out, kv_out):
    own = [b0, b1, b2, b3]
    chunk, rows = b0.shape
    width = normed_out.shape[0]

    def block(r):
        part = own[r][...] if r < 4 else other[(r - 4) * chunk : (r - 3) * chunk, :]
        return part.astype(F32)

    total = jnp.zeros((1, rows), F32)
    for r in range(8):
        x = block(r)
        total = total + jnp.sum(x * x, axis=0, keepdims=True)
    inverse = lax.rsqrt(total / width + 1e-06)
    inv_out[...] = inverse
    for r in range(8):
        at = pl.ds(pl.multiple_of(pos_ref[r] * chunk, chunk), chunk)
        normed_out[at, :] = (block(r) * inverse * gain_ref[at, :]).astype(BF16)
    normed = normed_out[...]
    q_out[...] = nn(w_ref[0], normed).astype(BF16) * jnp.asarray(HEAD_DIM ** (-0.5), BF16)
    head_cols = q_out.shape[0]
    for j in (1, 2):
        kv_out[(j - 1) * head_cols : j * head_cols, :] = nn(w_ref[j], normed).astype(BF16)


def back_arrange_body(pos_ref, b0, b1, b2, b3, other, wo_ref, full_out, grad_out):
    own = [b0, b1, b2, b3]
    chunk = b0.shape[0]
    for r in range(8):
        at = pl.ds(pl.multiple_of(pos_ref[r] * chunk, chunk), chunk)
        full_out[at, :] = own[r][...] if r < 4 else other[(r - 4) * chunk : (r - 3) * chunk, :]
    grad_out[...] = nn(wo_ref[...], full_out[...]).astype(BF16)


def fwd_loop_body(heads, *refs):
    q_refs, kv_refs = refs[:SIDE], refs[SIDE : 2 * SIDE]
    o_ref, lse_ref, keys, vals, queries = refs[2 * SIDE :]
    rows = q_refs[0].shape[1]
    width = heads * HEAD_DIM
    for r in range(SIDE):
        cols = slice(r * rows, (r + 1) * rows)
        vals[:, cols] = kv_refs[r][width:, :]
        queries[:, cols] = q_refs[r][...]
        for h in range(heads):
            keys[h, cols, :] = kv_refs[r][head_rows(h), :].T

    def step(r, carry):
        cols = pl.ds(pl.multiple_of(r * rows, rows), rows)
        for h in range(heads):
            at = head_rows(h)
            scores = nn(keys[h], queries[at, cols])
            top = jnp.max(scores, axis=0, keepdims=True)
            weights = jnp.exp(scores - top)
            total = jnp.sum(weights, axis=0, keepdims=True)
            out = nn(vals[at, :], weights.astype(BF16)) / total
            o_ref[at, cols] = out.astype(BF16)
            lse_ref[h : h + 1, cols] = top + jnp.log(total)
        return carry

    lax.fori_loop(0, SIDE, step, 0)


def stats_body(heads, o_ref, lse_ref, *refs):
    g_refs, out_ref = refs[:SIDE], refs[SIDE]
    rows = g_refs[0].shape[1]
    out_ref[...] = jnp.zeros_like(out_ref)
    out_ref[:heads, :] = lse_ref[...]
    for r in range(SIDE):
        cols = slice(r * rows, (r + 1) * rows)
        for h in range(heads):
            at = head_rows(h)
            out_ref[heads + h : heads + h + 1, cols] = jnp.sum(
                o_ref[at, cols].astype(F32) * g_refs[r][at, :].astype(F32), axis=0, keepdims=True
            )


def combine_body(heads, o_ref, *refs):
    peers, outs = refs[:SIDE], refs[SIDE:]
    lse_out, off_out, blocks = outs[0], outs[1], outs[2:]
    rows = o_ref.shape[1] // SIDE
    for r in range(SIDE):
        cols = slice(r * rows, (r + 1) * rows)
        theirs = []
        for s in range(SIDE):
            at = (r - s) % SIDE
            theirs.append(peers[s][:, at * rows : (at + 1) * rows])
        lse = [t[:heads] for t in theirs]
        off = [t[heads : 2 * heads] for t in theirs]
        top = jnp.maximum(jnp.maximum(lse[0], lse[1]), jnp.maximum(lse[2], lse[3]))
        logsum = top + jnp.log(sum(jnp.exp(v - top) for v in lse))
        shares = [jnp.exp(v - logsum) for v in lse]
        lse_out[:heads, cols] = logsum
        off_out[:heads, cols] = sum(w * v for w, v in zip(shares, off))
        for h in range(heads):
            at = head_rows(h)
            blocks[r][at, :] = (o_ref[at, cols].astype(F32) * shares[0][h : h + 1]).astype(BF16)


def bwd_body(first, last, heads, q_block, k_block, *refs):
    q_refs, kv_refs, g_refs = refs[:SIDE], refs[SIDE : 2 * SIDE], refs[2 * SIDE : 3 * SIDE]
    lse_ref, off_ref = refs[3 * SIDE : 3 * SIDE + 2]
    refs = refs[3 * SIDE + 2 :]
    carried = refs[: 2 * SIDE] if first else ()
    refs = refs[len(carried) :]
    dq_refs, dkv_refs = refs[:SIDE], refs[SIDE : 2 * SIDE]
    keys, vals, kt, qt, gt, stat, dq, dk, dv = refs[2 * SIDE :]
    count = last - first
    rows = q_refs[0].shape[1]
    span = SIDE * rows
    mine = slice(first * HEAD_DIM, last * HEAD_DIM)
    for r in range(SIDE):
        cols = slice(r * rows, (r + 1) * rows)
        qt[:, cols] = q_refs[r][mine, :]
        gt[:, cols] = g_refs[r][mine, :]
        kt[:, cols] = kv_refs[r][mine, :]
        for h in range(count):
            keys[h, cols, :] = kv_refs[r][head_rows(first + h), :].T
            vals[h, cols, :] = kv_refs[r][head_rows(heads + first + h), :].T
    for h in range(count):
        stat[h : h + 1, :] = lse_ref[first + h : first + h + 1, :]
        stat[count + h : count + h + 1, :] = off_ref[first + h : first + h + 1, :]
    dk[...] = jnp.zeros_like(dk)
    dv[...] = jnp.zeros_like(dv)
    dq[...] = jnp.zeros_like(dq)

    def q_step(qi, carry):
        q_cols = pl.ds(pl.multiple_of(qi * q_block, q_block), q_block)

        def k_step(ki, carry):
            k_rows = pl.ds(pl.multiple_of(ki * k_block, k_block), k_block)
            for h in range(count):
                at = head_rows(h)
                q = qt[at, q_cols]
                g = gt[at, q_cols]
                scores = nn(keys[h, k_rows, :], q)
                prob = jnp.exp(scores - stat[h : h + 1, q_cols])
                grad_prob = nn(vals[h, k_rows, :], g)
                off = stat[count + h : count + h + 1, q_cols]
                grad_score = (prob * (grad_prob - off)).astype(BF16)
                dq[at, q_cols] += nn(kt[at, k_rows], grad_score)
                dk[at, k_rows] += nt(q, grad_score)
                dv[at, k_rows] += nt(g, prob.astype(BF16))
            return carry

        lax.fori_loop(0, span // k_block, k_step, 0)
        return carry

    lax.fori_loop(0, span // q_block, q_step, 0)
    done = first * HEAD_DIM
    for r in range(SIDE):
        cols = slice(r * rows, (r + 1) * rows)
        dq_refs[r][done:, :] = (dq[:, cols] * HEAD_DIM ** (-0.5)).astype(BF16)
        half = last * HEAD_DIM
        dkv_refs[r][done:half, :] = dk[:, cols].astype(BF16)
        dkv_refs[r][half + done :, :] = dv[:, cols].astype(BF16)
        if first:
            dq_refs[r][:done, :] = carried[r][...]
            dkv_refs[r][:done, :] = carried[SIDE + r][:done, :]
            dkv_refs[r][half : half + done, :] = carried[SIDE + r][done:, :]


def sum_terms(refs):
    return sum(t[...].astype(F32) for t in refs)


def proj_body(*refs):
    terms, wo_ref = refs[:SIDE], refs[SIDE]
    att_out, own_out, other_out = refs[SIDE + 1 :]
    attended = sum_terms(terms).astype(BF16)
    half = own_out.shape[0]
    other_out[...] = nn(wo_ref[half:, :], attended).astype(BF16)
    own_out[...] = nn(wo_ref[:half, :], attended)
    att_out[...] = attended


def out_weights_body(att_ref, full_ref, part_out):
    part_out[...] = nt(att_ref[...], full_ref[...]).astype(BF16)


def pair_body(own_ref, got_ref, *outs):
    chunk = outs[0].shape[0]
    for d in range(SIDE):
        at = slice(d * chunk, (d + 1) * chunk)
        outs[d][...] = (own_ref[at, :] + got_ref[at, :].astype(F32)).astype(BF16)


def weights_body(heads, *refs):
    dq, dkv = refs[:SIDE], refs[SIDE : 2 * SIDE]
    normed_ref, out_part_ref, gp_out, part_out = refs[2 * SIDE :]
    width = heads * HEAD_DIM
    grad_q = sum_terms(dq).astype(BF16)
    grad_kv = sum_terms(dkv).astype(BF16)
    for h in range(heads):
        at = h * 3 * HEAD_DIM
        gp_out[at : at + HEAD_DIM, :] = grad_q[head_rows(h)]
        gp_out[at + HEAD_DIM : at + 2 * HEAD_DIM, :] = grad_kv[head_rows(h)]
        gp_out[at + 2 * HEAD_DIM : at + 3 * HEAD_DIM, :] = grad_kv[head_rows(heads + h)]
    part_out[: 3 * width, :] = nt(gp_out[...], normed_ref[...]).astype(BF16)
    part_out[3 * width :, :] = out_part_ref[...]


def split(v):
    high = v.astype(BF16)
    return high, (v - high.astype(F32)).astype(BF16)


def grads_body(heads, width, all_gp, q_ref, kv_ref, wq_ref, own_out, other_out):
    size = 3 * HEAD_DIM
    dots = jnp.zeros((1, q_ref.shape[1]), F32)
    for h in range(heads):
        at = h * size
        gp = all_gp[at : at + size, :].astype(F32)
        q = q_ref[head_rows(h), :].astype(F32) * HEAD_DIM**0.5
        k = kv_ref[head_rows(h), :].astype(F32)
        v = kv_ref[head_rows(heads + h), :].astype(F32)
        for j, held in enumerate((q, k, v)):
            dots = dots + jnp.sum(
                gp[j * HEAD_DIM : (j + 1) * HEAD_DIM] * held, axis=0, keepdims=True
            )
    dots = dots / width
    half = wq_ref.shape[0] // 2
    other_out[:half, :] = nn(wq_ref[half:, :], all_gp[...]).astype(BF16)
    high, low = split(dots)
    other_out[half:, :] = jnp.concatenate(
        [high, low, jnp.zeros((PAD - 2, dots.shape[1]), BF16)], axis=0
    )
    own_out[:half, :] = nn(wq_ref[:half, :], all_gp[...])
    own_out[half:, :] = jnp.broadcast_to(dots, (8, dots.shape[1]))


def grads_pair_body(own_ref, got_ref, *outs):
    chunk = outs[0].shape[0] - PAD
    half = SIDE * chunk
    got = got_ref[half:, :].astype(F32)
    dots = own_ref[half : half + 1, :] + got[0:1] + got[1:2]
    high, low = split(dots)
    tail = jnp.concatenate([high, low, jnp.zeros((PAD - 2, dots.shape[1]), BF16)], axis=0)
    for d in range(SIDE):
        at = slice(d * chunk, (d + 1) * chunk)
        outs[d][:chunk, :] = (own_ref[at, :] + got_ref[at, :].astype(F32)).astype(BF16)
        outs[d][chunk:, :] = tail


def spread_small_body(in_ref, small_ref, out_ref):
    members, _, width = in_ref.shape
    total = sum(in_ref[i].astype(F32) for i in range(members)).astype(BF16)
    small = small_ref[...]
    for i in range(members):
        out_ref[i, :, :width] = total
        out_ref[i, :, width:] = small


def finish_body(heads, all_ref, qkv_out, proj_out, small_out):
    members, each, _ = all_ref.shape
    width = qkv_out.shape[2]
    step = 8

    def rows_of(row):
        m, k = divmod(row, each)
        return all_ref[m, k : k + step, :width].astype(F32)

    for i in range(0, HEAD_DIM, step):
        for h in range(heads):
            for j in range(3):
                at = h * HEAD_DIM + i
                qkv_out[j, at : at + step, :] = rows_of((h * 3 + j) * HEAD_DIM + i)
    for i in range(0, heads * HEAD_DIM, step):
        proj_out[i : i + step, :] = rows_of(3 * heads * HEAD_DIM + i)
    small_out[...] = sum(all_ref[m, :, width:].astype(F32) for m in range(members))


def tie(value, *others):
    return lax.optimization_barrier((value, *others))[0]


def shards(frames, norm_gain, w_qkv, w_out, conv_kernel, grad_out):
    own_width, rows = frames.shape
    head_cols, width = w_qkv.shape[1:]
    heads = head_cols // HEAD_DIM
    members = lax.axis_size("tm")
    taps = conv_kernel.shape[0]
    span = SIDE * rows
    y, core = lax.axis_index("mp") // 2, lax.axis_index("mp") % 2
    steps = jnp.arange(SIDE, dtype=jnp.int32)
    cores = jnp.stack([core, 1 - core]).astype(jnp.int32)
    came = ((((y - steps + SIDE) % SIDE) * 2)[None, :] + cores[:, None]).reshape(-1)
    goes = ((((y + steps) % SIDE) * 2)[None, :] + cores[:, None]).reshape(-1)

    def with_swap(blocks):
        return blocks + [swap_core(jnp.concatenate(blocks, axis=0))]

    up_left, up_right = halos(grad_out)
    in_blocks = ring(shift_y, [frames] * SIDE, 1)
    back_sum, back_cast = call(
        back_kernel,
        [((own_width, rows), F32), ((own_width, rows), BF16)],
        [up_left, grad_out, up_right, conv_kernel], None,
        [
            pltpu.VMEM((rows + 2 * PAD, own_width), F32),
            pltpu.VMEM((rows, own_width), F32),
            pltpu.VMEM((STEP + 2 * PAD, own_width), F32),
        ],
        flops=8 * own_width * rows * taps,
    )
    in_blocks = list(lax.optimization_barrier((*in_blocks, back_cast)))
    back_cast = in_blocks.pop()
    in_blocks = with_swap(in_blocks)
    back_blocks = ring(shift_y, [back_cast] * SIDE, 1)
    normed, inverse, queries, keys_values = call(
        norm_body,
        [((width, rows), BF16), ((1, rows), F32), ((head_cols, rows), BF16), ((2 * head_cols, rows), BF16)],
        [came, *in_blocks, norm_gain[:, None], w_qkv], [SM] + [VM] * 7,
        flops=2 * 3 * head_cols * width * rows,
    )
    group_kv = ring(shift_z, [keys_values] * SIDE, 1)
    group_q = ring(shift_x, [queries] * SIDE, 1)

    back_blocks = list(lax.optimization_barrier((*back_blocks, keys_values)))[:SIDE]
    back_blocks = with_swap(back_blocks)
    back_full, grad_attn = call(
        back_arrange_body,
        [((width, rows), BF16), ((head_cols, rows), BF16)],
        [came, *back_blocks, w_out], [SM] + [VM] * 6,
        flops=2 * head_cols * width * rows,
    )
    group_g = ring(shift_x, [grad_attn] * SIDE, 1)

    part_out, part_lse = call(
        functools.partial(fwd_loop_body, heads),
        [((head_cols, span), BF16), ((heads, span), F32)],
        [tie(group_q[0], grad_attn), *group_q[1:], *group_kv], None,
        [
            pltpu.VMEM((heads, span, HEAD_DIM), BF16),
            pltpu.VMEM((head_cols, span), BF16),
            pltpu.VMEM((head_cols, span), BF16),
        ],
        flops=16 * head_cols * span * span, exps=heads * span * span,
    )
    (stats,) = call(
        functools.partial(stats_body, heads),
        [((8, span), F32)], [part_out, part_lse, *group_g],
    )
    peers = ring(shift_x, [stats] * SIDE, 1)
    wq_rel, wo_rel = call(
        prep_body,
        [((width, 3 * head_cols), BF16), ((width, head_cols), BF16)],
        [tie(goes, stats), w_qkv, w_out], [SM, VM, VM],
        [
            pltpu.VMEM((3 * head_cols, width), BF16),
            pltpu.VMEM((width, 3 * head_cols), BF16),
            pltpu.VMEM((width, head_cols), BF16),
        ],
    )
    logsum, offset, *out_blocks = call(
        functools.partial(combine_body, heads),
        [((8, span), F32), ((8, span), F32)] + [((head_cols, rows), BF16)] * SIDE,
        [tie(part_out, wo_rel), *peers],
    )
    out_terms = ring(shift_x, out_blocks, -1)

    q_block, k_block = min(1024, span), min(512, span)

    def head_grads(first, last, logsum, carried):
        count = last - first
        size = count * HEAD_DIM
        return call(
            functools.partial(bwd_body, first, last, heads, q_block, k_block),
            [((last * HEAD_DIM, rows), BF16)] * SIDE + [((2 * last * HEAD_DIM, rows), BF16)] * SIDE,
            [*group_q, *group_kv, *group_g, logsum, offset, *carried], None,
            [pltpu.VMEM((count, span, HEAD_DIM), BF16)] * 2
            + [pltpu.VMEM((size, span), BF16)] * 3
            + [pltpu.VMEM((8, span), F32)]
            + [pltpu.VMEM((size, span), F32)] * 3,
            flops=40 * size * span * span, exps=count * span * span,
        )

    early = head_grads(0, 1, logsum, ())
    half = SIDE * own_width
    attended, proj_own, proj_other = call(
        proj_body,
        [((head_cols, rows), BF16), ((half, rows), F32), ((half, rows), BF16)],
        [tie(out_terms[0], early[0]), *out_terms[1:], wo_rel],
        flops=2 * head_cols * width * rows,
    )
    proj_got = swap_core(proj_other)
    proj_blocks = call(pair_body, [((own_width, rows), BF16)] * SIDE, [proj_own, proj_got])
    proj_terms = ring(shift_y, proj_blocks, 1)

    grads = head_grads(1, heads, tie(logsum, *proj_blocks), early)
    dq, dkv = grads[:SIDE], grads[SIDE:]
    dkv_terms = ring(shift_z, dkv, -1)
    dq_terms = ring(shift_x, dq, -1)

    mixed = sum(t.astype(F32) for t in [tie(proj_terms[0], dq[0])] + proj_terms[1:])
    residual = (frames.astype(F32) + mixed).astype(BF16)
    res_left, res_right = halos(residual)
    (out_part,) = call(
        out_weights_body, [((head_cols, width), BF16)],
        [tie(attended, dq[0]), back_full], flops=2 * head_cols * width * rows,
    )
    block_out, kernel_part = call(
        conv_body,
        [((own_width, rows), BF16), ((taps, own_width), F32)],
        [res_left, residual, res_right, grad_out, conv_kernel], None,
        [
            pltpu.VMEM((rows + 2 * PAD, own_width), F32),
            pltpu.VMEM((rows, own_width), F32),
            pltpu.VMEM((taps, 8, own_width), F32),
            pltpu.VMEM((STEP + 2 * PAD, own_width), F32),
        ],
        flops=16 * own_width * rows * taps,
    )

    all_gp, part = call(
        functools.partial(weights_body, heads),
        [((3 * head_cols, rows), BF16), ((4 * head_cols, width), BF16)],
        [*dq_terms, *dkv_terms, normed, tie(out_part, kernel_part)],
        flops=2 * 3 * head_cols * width * rows,
    )
    each = part.shape[0] // members
    got = lax.all_to_all(part.reshape(members, each, width), "tm", 0, 0, tiled=True)

    gn_own, gn_other = call(
        functools.partial(grads_body, heads, width),
        [((half + 8, rows), F32), ((half + PAD, rows), BF16)],
        [tie(all_gp, part), queries, keys_values, wq_rel],
        flops=2 * 3 * head_cols * width * rows,
    )
    gn_got = swap_core(gn_other)
    gn_blocks = call(grads_pair_body, [((own_width + PAD, rows), BF16)] * SIDE, [gn_own, gn_got])
    gn_terms = ring(shift_y, gn_blocks, 1)
    summed = sum(t.astype(F32) for t in gn_terms)
    grad_own = summed[:own_width]
    dots = summed[own_width : own_width + 1] + summed[own_width + 1 : own_width + 2]
    column_start = lax.axis_index("mp") * own_width
    gain_own = lax.dynamic_slice_in_dim(norm_gain, column_start, own_width, 0)[:, None]
    normed_own = frames.astype(F32) * inverse
    grad_frames = (
        back_sum + inverse * (grad_own * gain_own) - normed_own * inverse * dots
    ).astype(BF16)
    gain_part = jnp.sum(grad_own * normed_own, axis=1)
    small = jnp.concatenate([kernel_part.astype(BF16), gain_part.astype(BF16)[None]], axis=0)
    small_cols = small.size // each
    (spread,) = call(
        spread_small_body, [((members, each, width + small_cols), BF16)],
        [got, small.reshape(each, small_cols)],
    )
    everything = lax.all_to_all(spread, "tm", 0, 0, tiled=True)
    qkv_grads, out_grads, small_sum = call(
        functools.partial(finish_body, heads),
        [((3, head_cols, width), F32), ((head_cols, width), F32), ((each, small_cols), F32)],
        [everything],
    )
    small_sum = small_sum.reshape(taps + 1, own_width)
    return block_out, grad_frames, small_sum[taps], qkv_grads, out_grads, small_sum[:taps]


def solution(mesh):
    return jax.shard_map(
        shards,
        mesh=mesh,
        in_specs=(
            P("mp", "tm"),
            P(),
            P(None, "mp", None),
            P("mp", None),
            P(None, "mp"),
            P("mp", "tm"),
        ),
        out_specs=(
            P("mp", "tm"),
            P("mp", "tm"),
            P("mp"),
            P(None, "mp", None),
            P("mp", None),
            P(None, "mp"),
        ),
        check_vma=False,
    )
```

profile of v0, /device:TPU:0, one launch (start us, length us, event | category | flops | bytes accessed | tf_op | source)
XLA Modules:
  0.0 283.5 jit_solution(15959171130129952963)
XLA Ops:
  2.4 2.9 %collective-permute-start.1 = (bf16[192,512]{1,0:T(8,128)(2,1)}, bf16[192,512]{1,0:T(8,128)(2,1)S(1)}, u32[]{:S(2)}, u32[]{:S(2)}) collective-permute-start(bf16[192,512]{1,0:T(8,128)(2,1)} %b0), channel_id=1, source_target_pairs={{0,4},{1,5},{2,6},{3,7},{4,0},{5,1},{6,2},{7,3},{8,12},{9,13},{10,... | collective-permute-start | bytes 589832 | tf_op jit(solution)/shard_map/ppermute | solution.py:118
  7.5 3.4 %collective-permute-start.3 = (bf16[192,128]{1,0:T(8,128)(2,1)S(1)}, bf16[192,128]{1,0:T(8,128)(2,1)S(1)}, u32[]{:S(2)}, u32[]{:S(2)}) collective-permute-start(bf16[192,128]{1,0:T(8,128)(2,1)S(1)} %get-tuple-element.154), channel_id=1, source_target_pairs={{0,8},{8,16},{16,24},{24,32},{32,40},{40,48},{48,56},{56,64},{64,7... | collective-permute-start | bytes 147464 | tf_op jit(solution)/shard_map/ppermute | solution.py:107
  12.6 4.2 %collective-permute-done.4.right_ref = bf16[192,128]{1,0:T(8,128)(2,1)S(1)} collective-permute-done((bf16[192,128]{1,0:T(8,128)(2,1)S(1)}, bf16[192,128]{1,0:T(8,128)(2,1)S(1)}, u32[]{:S(2)}, u32[]{:S(2)}) %collective-permute-start.4) | collective-permute-done | bytes 49184 | tf_op jit(solution)/shard_map/ppermute | solution.py:108
  17.5 4.3 %shard_map.109 = (f32[192,512]{1,0:T(8,128)}, bf16[192,512]{1,0:T(8,128)(2,1)}) custom-call(bf16[192,128]{1,0:T(8,128)(2,1)} %copy-done.33, bf16[192,512]{1,0:T(8,128)(2,1)} %up_ref.1, bf16[192,128]{1,0:T(8,128)(2,1)} %copy-done.34, f32[31,192]{1,0:T(8,128)} %taps_ref.3), custom_call_target="tpu_custom_call" | custom-call | flops 24379392 | bytes 908544 | tf_op jit(solution)/shard_map/pallas_call | solution.py:130
  29.5 4.6 %shard_map.110 = (bf16[1536,512]{1,0:T(8,128)(2,1)}, f32[1,512]{1,0:T(1,128)}, bf16[192,512]{1,0:T(8,128)(2,1)}, bf16[384,512]{1,0:T(8,128)(2,1)}) custom-call(s32[8]{0:T(128)} %add.106.pos_ref, bf16[192,512]{1,0:T(8,128)(2,1)} %b0, bf16[192,512]{1,0:T(8,128)(2,1)} %copy-done.4, bf16[192,512]{1,0:T(8,128)(2,1)} %copy-done.5, bf16[192,512]{1,0:T(8,128)(2,1)} %copy-done.6, ...), custom_call_target="tpu_custom_call" | custom-call | flops 905969664 | bytes 5513248 | tf_op jit(solution)/shard_map/pallas_call | solution.py:130
  40.3 3.6 %collective-permute-start.14 = (bf16[384,512]{1,0:T(8,128)(2,1)S(1)}, bf16[384,512]{1,0:T(8,128)(2,1)S(1)}, u32[]{:S(2)}, u32[]{:S(2)}) collective-permute-start(bf16[384,512]{1,0:T(8,128)(2,1)S(1)} %copy-done.39), channel_id=1, source_target_pairs={{0,64},{8,72},{16,80},{24,88},{32,96},{40,104},{48,112},{56,120},{... | collective-permute-start | bytes 1179656 | tf_op jit(solution)/shard_map/ppermute | solution.py:101
  44.9 2.9 %collective-permute-done.10.refs_1_ = bf16[192,512]{1,0:T(8,128)(2,1)S(1)} collective-permute-done((bf16[192,512]{1,0:T(8,128)(2,1)}, bf16[192,512]{1,0:T(8,128)(2,1)S(1)}, u32[]{:S(2)}, u32[]{:S(2)}) %collective-permute-start.10) | collective-permute-done | bytes 196640 | tf_op jit(solution)/shard_map/ppermute | solution.py:94
  50.7 3.0 %shard_map.111 = (bf16[1536,512]{1,0:T(8,128)(2,1)}, bf16[192,512]{1,0:T(8,128)(2,1)}) custom-call(s32[8]{0:T(128)} %add.106.pos_ref, bf16[192,512]{1,0:T(8,128)(2,1)} %get-tuple-element.86.b0, bf16[192,512]{1,0:T(8,128)(2,1)} %copy-done.9, bf16[192,512]{1,0:T(8,128)(2,1)} %copy-done.10, bf16[192,512]{1,0:T(8,128)(2,1)} %copy-done.11, ...), custom_call_target="tpu_custom_call" | custom-call | flops 301989888 | bytes 3932192 | tf_op jit(solution)/shard_map/pallas_call | solution.py:130
  63.0 23.0 %shard_map.112 = (bf16[192,2048]{1,0:T(8,128)(2,1)}, f32[3,2048]{1,0:T(4,128)}) custom-call(bf16[192,512]{1,0:T(8,128)(2,1)} %get-tuple-element.91.refs_0_.q_ref, bf16[192,512]{1,0:T(8,128)(2,1)} %copy-done.42, bf16[192,512]{1,0:T(8,128)(2,1)} %collective-permute-done.11.refs_2_, bf16[192,512]{1,0:T(8,128)(2,1)} %copy-done.43, ...), custom_call_target="tpu_custom_call" | custom-call | flops 12884901888 | bytes 3170304 | tf_op jit(solution)/shard_map/pallas_call | solution.py:130
  95.0 3.8 %shard_map.114 = (bf16[1536,576]{1,0:T(8,128)(2,1)}, bf16[1536,192]{1,0:T(8,128)(2,1)}) custom-call(s32[8]{0:T(128)} %add.111.pos_ref, bf16[3,192,1536]{2,1,0:T(8,128)(2,1)} %w_ref.3, bf16[192,1536]{1,0:T(8,128)(2,1)} %wo_ref.3), custom_call_target="tpu_custom_call" | custom-call | bytes 4718624 | tf_op jit(solution)/shard_map/pallas_call | solution.py:130
  104.5 15.2 %shard_map.116 = (bf16[64,512]{1,0:T(8,128)(2,1)}, bf16[64,512]{1,0:T(8,128)(2,1)}, bf16[64,512]{1,0:T(8,128)(2,1)}, bf16[64,512]{1,0:T(8,128)(2,1)}, bf16[128,5...) custom-call(bf16[192,512]{1,0:T(8,128)(2,1)} %get-tuple-element.91.refs_0_.q_ref, ...), custom_call_target="tpu_custom_call" | custom-call | flops 10737418240 | bytes 4063232 | tf_op jit(solution)/shard_map/pallas_call | solution.py:130
  121.2 3.5 %shard_map.117 = (bf16[192,512]{1,0:T(8,128)(2,1)}, f32[768,512]{1,0:T(8,128)}, bf16[768,512]{1,0:T(8,128)(2,1)}) custom-call(bf16[192,512]{1,0:T(8,128)(2,1)} %get-tuple-element.101.refs_0_, bf16[192,512]{1,0:T(8,128)(2,1)} %copy-done.25, bf16[192,512]{1,0:T(8,128)(2,1)} %copy-done.26, bf16[192,512]{1,0:T(8,128)(2,1)} %copy-done.27, ...), custom_call_target="tpu_custom_call" | custom-call | flops 301989888 | bytes 3932160 | tf_op jit(solution)/shard_map/pallas_call | solution.py:130
  131.1 3.6 %collective-permute-start.27 = (bf16[192,512]{1,0:T(8,128)(2,1)}, bf16[192,512]{1,0:T(8,128)(2,1)S(1)}, u32[]{:S(2)}, u32[]{:S(2)}) collective-permute-start(bf16[192,512]{1,0:T(8,128)(2,1)} %get-tuple-element.109), channel_id=1, source_target_pairs={{0,4},{1,5},{2,6},{3,7},{4,0},{5,1},{6,2},{7,3},{8,12},{9,13},{10,... | collective-permute-start | bytes 589832 | tf_op jit(solution)/shard_map/ppermute | solution.py:118
  134.7 27.6 %shard_map.119 = (bf16[192,512]{1,0:T(8,128)(2,1)}, bf16[192,512]{1,0:T(8,128)(2,1)}, bf16[192,512]{1,0:T(8,128)(2,1)}, bf16[192,512]{1,0:T(8,128)(2,1)}, bf16[3...) custom-call(bf16[192,512]{1,0:T(8,128)(2,1)} %get-tuple-element.91.refs_0_.q, ...), custom_call_target="tpu_custom_call" | custom-call | flops 21474836480 | bytes 6422528 | tf_op jit(solution)/shard_map/pallas_call | solution.py:130
  175.0 4.3 %collective-permute-start.32 = (bf16[192,512]{1,0:T(8,128)(2,1)}, bf16[192,512]{1,0:T(8,128)(2,1)S(1)}, u32[]{:S(2)}, u32[]{:S(2)}) collective-permute-start(bf16[192,512]{1,0:T(8,128)(2,1)} %get-tuple-element.125), channel_id=1, source_target_pairs={{0,16},{8,24},{16,0},{24,8},{32,48},{40,56},{48,32},{56,40},{64,80... | collective-permute-start | bytes 589832 | tf_op jit(solution)/shard_map/ppermute | solution.py:94
  182.3 3.0 %shard_map.121.refs_9_ = bf16[192,1536]{1,0:T(8,128)(2,1)} custom-call(bf16[192,512]{1,0:T(8,128)(2,1)} %get-tuple-element.133.att_ref, bf16[1536,512]{1,0:T(8,128)(2,1)} %get-tuple-element.134.full_ref), custom_call_target="tpu_custom_call" | custom-call | flops 301989888 | bytes 2359296 | tf_op jit(solution)/shard_map/pallas_call | solution.py:130
  185.3 6.4 %shard_map.120 = (bf16[192,512]{1,0:T(8,128)(2,1)}, f32[31,192]{1,0:T(8,128)}) custom-call(bf16[192,128]{1,0:T(8,128)(2,1)} %copy-done.31, bf16[192,512]{1,0:T(8,128)(2,1)} %copy-done.2, bf16[192,128]{1,0:T(8,128)(2,1)} %copy-done.32, bf16[192,512]{1,0:T(8,128)(2,1)} %up_ref.1, f32[31,192]{1,0:T(8,128)} %taps_ref.3), custom_call_target="tpu_custom_call" | custom-call | flops 48758784 | bytes 735744 | tf_op jit(solution)/shard_map/pallas_call | solution.py:130
  192.8 4.9 %shard_map.122 = (bf16[576,512]{1,0:T(8,128)(2,1)}, bf16[768,1536]{1,0:T(8,128)(2,1)}) custom-call(bf16[192,512]{1,0:T(8,128)(2,1)} %get-tuple-element.119.refs_0_, bf16[192,512]{1,0:T(8,128)(2,1)} %copy-done.18, bf16[192,512]{1,0:T(8,128)(2,1)} %copy-done.19, bf16[192,512]{1,0:T(8,128)(2,1)} %copy-done.20, bf16[384,512]{1,0:T(8,128)(2,1)} %get-tuple-element.127.refs_4_, ...), custom_call_target="tpu_custom_call" | custom-call | flops 905969664 | bytes 7471104 | tf_op jit(solution)/shard_map/pallas_call | solution.py:130
  197.7 8.0 %all-to-all-start = ((bf16[16,48,1536]{2,1,0:T(8,128)(2,1)}), bf16[16,48,1536]{2,1,0:T(8,128)(2,1)S(1)}, u32[]{:S(2)}, u32[]{:S(2)}) async-start(bf16[16,48,1536]{2,1,0:T(8,128)(2,1)} %bitcast.7), calls=%async_computation | async-start | bytes 4718592 | tf_op jit(solution)/shard_map/all_to_all | solution.py:584
  205.7 4.8 %shard_map.123 = (f32[776,512]{1,0:T(8,128)}, bf16[784,512]{1,0:T(8,128)(2,1)}) custom-call(bf16[576,512]{1,0:T(8,128)(2,1)} %get-tuple-element.137.all_gp, bf16[192,512]{1,0:T(8,128)(2,1)} %get-tuple-element.91.refs_0_.q_ref, bf16[384,512]{1,0:T(8,128)(2,1)} %get-tuple-element.85.refs_4_.kv_ref, bf16[1536,576]{1,0:T(8,128)(2,1)} %get-tuple-element.138.wq_ref), custom_call_target="tpu_custom_call" | custom-call | flops 905969664 | bytes 5341184 | tf_op jit(solution)/shard_map/pallas_call | solution.py:130
  221.3 8.4 %collective-permute-done.38 = bf16[208,512]{1,0:T(8,128)(2,1)S(1)} collective-permute-done((bf16[208,512]{1,0:T(8,128)(2,1)}, bf16[208,512]{1,0:T(8,128)(2,1)S(1)}, u32[]{:S(2)}, u32[]{:S(2)}) %collective-permute-start.38) | collective-permute-done | bytes 213024 | tf_op jit(solution)/shard_map/ppermute | solution.py:118
  236.8 3.5 %shard_map.125 = bf16[16,48,1664]{2,1,0:T(8,128)(2,1)} custom-call(bf16[16,48,1536]{2,1,0:T(8,128)(2,1)} %copy-done, bf16[48,128]{1,0:T(8,128)(2,1)} %reshape.73.small_ref), custom_call_target="tpu_custom_call" | custom-call | bytes 4927488 | tf_op jit(solution)/shard_map/pallas_call | solution.py:130
  240.2 37.9 %all_to_all.10.all_ref = bf16[16,48,1664]{2,1,0:T(8,128)(2,1)} all-to-all(bf16[16,48,1664]{2,1,0:T(8,128)(2,1)} %shard_map.125), channel_id=1, replica_groups=mesh['tm'=16,'mp'=8] {'tm'}, dimensions={0} | all-to-all | bytes 5111808 | tf_op jit(solution)/shard_map/all_to_all | solution.py:611
  278.1 4.0 %shard_map.126 = (f32[3,192,1536]{2,1,0:T(8,128)}, f32[192,1536]{1,0:T(8,128)}, f32[48,128]{1,0:T(8,128)}) custom-call(bf16[16,48,1664]{2,1,0:T(8,128)(2,1)} %all_to_all.10.all_ref), custom_call_target="tpu_custom_call" | custom-call | bytes 7299072 | tf_op jit(solution)/shard_map/pallas_call | solution.py:130
  (188 shorter events, 91.7 us)
Async XLA Ops:
  0.6 21.2 %collective-permute-start = (bf16[192,512]{1,0:T(8,128)(2,1)}, bf16[192,512]{1,0:T(8,128)(2,1)S(1)}, u32[]{:S(2)}, u32[]{:S(2)}) collective-permute-start(bf16[192,512]{1,0:T(8,128)(2,1)} %b0), channel_id=1, source_target_pairs={{0,2},{1,3},{2,4},{3,5},{4,6},{5,7},{6,0},{7,1},{8,10},{9,11},{10,... | collective-permute-start | bytes 589832 | tf_op jit(solution)/shard_map/ppermute | solution.py:118
  2.4 19.4 %collective-permute-start.1 = (bf16[192,512]{1,0:T(8,128)(2,1)}, bf16[192,512]{1,0:T(8,128)(2,1)S(1)}, u32[]{:S(2)}, u32[]{:S(2)}) collective-permute-start(bf16[192,512]{1,0:T(8,128)(2,1)} %b0), channel_id=1, source_target_pairs={{0,4},{1,5},{2,6},{3,7},{4,0},{5,1},{6,2},{7,3},{8,12},{9,13},{10,... | collective-permute-start | bytes 589832 | tf_op jit(solution)/shard_map/ppermute | solution.py:118
  5.3 16.6 %collective-permute-start.2 = (bf16[192,512]{1,0:T(8,128)(2,1)}, bf16[192,512]{1,0:T(8,128)(2,1)S(1)}, u32[]{:S(2)}, u32[]{:S(2)}) collective-permute-start(bf16[192,512]{1,0:T(8,128)(2,1)} %b0), channel_id=1, source_target_pairs={{0,6},{1,7},{2,0},{3,1},{4,2},{5,3},{6,4},{7,5},{8,14},{9,15},{10,... | collective-permute-start | bytes 589832 | tf_op jit(solution)/shard_map/ppermute | solution.py:118
  23.3 12.8 %collective-permute-start.6 = (bf16[192,512]{1,0:T(8,128)(2,1)S(1)}, bf16[192,512]{1,0:T(8,128)(2,1)S(1)}, u32[]{:S(2)}, u32[]{:S(2)}) collective-permute-start(bf16[192,512]{1,0:T(8,128)(2,1)S(1)} %copy-done.8), channel_id=1, source_target_pairs={{0,2},{1,3},{2,4},{3,5},{4,6},{5,7},{6,0},{7,1},{8,10},{9,11},{10,... | collective-permute-start | bytes 589832 | tf_op jit(solution)/shard_map/ppermute | solution.py:118
  24.1 12.0 %collective-permute-start.7 = (bf16[192,512]{1,0:T(8,128)(2,1)S(1)}, bf16[192,512]{1,0:T(8,128)(2,1)S(1)}, u32[]{:S(2)}, u32[]{:S(2)}) collective-permute-start(bf16[192,512]{1,0:T(8,128)(2,1)S(1)} %copy-done.8), channel_id=1, source_target_pairs={{0,4},{1,5},{2,6},{3,7},{4,0},{5,1},{6,2},{7,3},{8,12},{9,13},{10,... | collective-permute-start | bytes 589832 | tf_op jit(solution)/shard_map/ppermute | solution.py:118
  36.8 13.1 %collective-permute-start.9 = (bf16[768,512]{1,0:T(8,128)(2,1)S(1)}, bf16[768,512]{1,0:T(8,128)(2,1)S(1)}, u32[]{:S(2)}, u32[]{:S(2)}) collective-permute-start(bf16[768,512]{1,0:T(8,128)(2,1)S(1)} %pad_maximum_fusion.1), channel_id=1, source_target_pairs={{0,1},{1,0},{2,3},{3,2},{4,5},{5,4},{6,7},{7,6},{8,9},{9,8},{10,11... | collective-permute-start | bytes 2359304 | tf_op jit(solution)/shard_map/ppermute | solution.py:123
  38.4 22.3 %collective-permute-start.13 = (bf16[384,512]{1,0:T(8,128)(2,1)S(1)}, bf16[384,512]{1,0:T(8,128)(2,1)S(1)}, u32[]{:S(2)}, u32[]{:S(2)}) collective-permute-start(bf16[384,512]{1,0:T(8,128)(2,1)S(1)} %copy-done.39), channel_id=1, source_target_pairs={{0,32},{8,40},{16,48},{24,56},{32,64},{40,72},{48,80},{56,88},{64,... | collective-permute-start | bytes 1179656 | tf_op jit(solution)/shard_map/ppermute | solution.py:101
  40.3 21.8 %collective-permute-start.14 = (bf16[384,512]{1,0:T(8,128)(2,1)S(1)}, bf16[384,512]{1,0:T(8,128)(2,1)S(1)}, u32[]{:S(2)}, u32[]{:S(2)}) collective-permute-start(bf16[384,512]{1,0:T(8,128)(2,1)S(1)} %copy-done.39), channel_id=1, source_target_pairs={{0,64},{8,72},{16,80},{24,88},{32,96},{40,104},{48,112},{56,120},{... | collective-permute-start | bytes 1179656 | tf_op jit(solution)/shard_map/ppermute | solution.py:101
  43.9 18.3 %collective-permute-start.15 = (bf16[384,512]{1,0:T(8,128)(2,1)S(1)}, bf16[384,512]{1,0:T(8,128)(2,1)}, u32[]{:S(2)}, u32[]{:S(2)}) collective-permute-start(bf16[384,512]{1,0:T(8,128)(2,1)S(1)} %copy-done.39), channel_id=1, source_target_pairs={{0,96},{8,104},{16,112},{24,120},{32,0},{40,8},{48,16},{56,24},{64... | collective-permute-start | bytes 1179656 | tf_op jit(solution)/shard_map/ppermute | solution.py:101
  56.3 29.7 %collective-permute-start.16 = (bf16[192,512]{1,0:T(8,128)(2,1)}, bf16[192,512]{1,0:T(8,128)(2,1)S(1)}, u32[]{:S(2)}, u32[]{:S(2)}) collective-permute-start(bf16[192,512]{1,0:T(8,128)(2,1)} %get-tuple-element.90.refs_0_.refs_8_), channel_id=1, source_target_pairs={{0,8},{8,16},{16,24},{24,0},{32,40},{40,48},{48,56},{56,32},{64,72... | collective-permute-start | bytes 589832 | tf_op jit(solution)/shard_map/ppermute | solution.py:94
  59.3 26.7 %collective-permute-start.17 = (bf16[192,512]{1,0:T(8,128)(2,1)}, bf16[192,512]{1,0:T(8,128)(2,1)S(1)}, u32[]{:S(2)}, u32[]{:S(2)}) collective-permute-start(bf16[192,512]{1,0:T(8,128)(2,1)} %get-tuple-element.90.refs_0_.refs_8_), channel_id=1, source_target_pairs={{0,16},{8,24},{16,0},{24,8},{32,48},{40,56},{48,32},{56,40},{64,80... | collective-permute-start | bytes 589832 | tf_op jit(solution)/shard_map/ppermute | solution.py:94
  60.7 25.3 %collective-permute-start.18 = (bf16[192,512]{1,0:T(8,128)(2,1)}, bf16[192,512]{1,0:T(8,128)(2,1)S(1)}, u32[]{:S(2)}, u32[]{:S(2)}) collective-permute-start(bf16[192,512]{1,0:T(8,128)(2,1)} %get-tuple-element.90.refs_0_.refs_8_), channel_id=1, source_target_pairs={{0,24},{8,0},{16,8},{24,16},{32,56},{40,32},{48,40},{56,48},{64,88... | collective-permute-start | bytes 589832 | tf_op jit(solution)/shard_map/ppermute | solution.py:94
  102.4 17.3 %collective-permute-start.22 = (bf16[192,512]{1,0:T(8,128)(2,1)}, bf16[192,512]{1,0:T(8,128)(2,1)S(1)}, u32[]{:S(2)}, u32[]{:S(2)}) collective-permute-start(bf16[192,512]{1,0:T(8,128)(2,1)} %get-tuple-element.102), channel_id=1, source_target_pairs={{0,24},{8,0},{16,8},{24,16},{32,56},{40,32},{48,40},{56,48},{64,88... | collective-permute-start | bytes 589832 | tf_op jit(solution)/shard_map/ppermute | solution.py:94
  103.0 16.7 %collective-permute-start.23 = (bf16[192,512]{1,0:T(8,128)(2,1)}, bf16[192,512]{1,0:T(8,128)(2,1)S(1)}, u32[]{:S(2)}, u32[]{:S(2)}) collective-permute-start(bf16[192,512]{1,0:T(8,128)(2,1)} %get-tuple-element.103), channel_id=1, source_target_pairs={{0,16},{8,24},{16,0},{24,8},{32,48},{40,56},{48,32},{56,40},{64,80... | collective-permute-start | bytes 589832 | tf_op jit(solution)/shard_map/ppermute | solution.py:94
  104.2 15.6 %collective-permute-start.24 = (bf16[192,512]{1,0:T(8,128)(2,1)}, bf16[192,512]{1,0:T(8,128)(2,1)S(1)}, u32[]{:S(2)}, u32[]{:S(2)}) collective-permute-start(bf16[192,512]{1,0:T(8,128)(2,1)} %get-tuple-element.104), channel_id=1, source_target_pairs={{0,8},{8,16},{16,24},{24,0},{32,40},{40,48},{48,56},{56,32},{64,72... | collective-permute-start | bytes 589832 | tf_op jit(solution)/shard_map/ppermute | solution.py:94
  130.6 35.8 %collective-permute-start.26 = (bf16[192,512]{1,0:T(8,128)(2,1)}, bf16[192,512]{1,0:T(8,128)(2,1)S(1)}, u32[]{:S(2)}, u32[]{:S(2)}) collective-permute-start(bf16[192,512]{1,0:T(8,128)(2,1)} %get-tuple-element.108), channel_id=1, source_target_pairs={{0,2},{1,3},{2,4},{3,5},{4,6},{5,7},{6,0},{7,1},{8,10},{9,11},{10,... | collective-permute-start | bytes 589832 | tf_op jit(solution)/shard_map/ppermute | solution.py:118
  131.1 36.2 %collective-permute-start.27 = (bf16[192,512]{1,0:T(8,128)(2,1)}, bf16[192,512]{1,0:T(8,128)(2,1)S(1)}, u32[]{:S(2)}, u32[]{:S(2)}) collective-permute-start(bf16[192,512]{1,0:T(8,128)(2,1)} %get-tuple-element.109), channel_id=1, source_target_pairs={{0,4},{1,5},{2,6},{3,7},{4,0},{5,1},{6,2},{7,3},{8,12},{9,13},{10,... | collective-permute-start | bytes 589832 | tf_op jit(solution)/shard_map/ppermute | solution.py:118
  134.6 35.5 %collective-permute-start.28 = (bf16[192,512]{1,0:T(8,128)(2,1)}, bf16[192,512]{1,0:T(8,128)(2,1)S(1)}, u32[]{:S(2)}, u32[]{:S(2)}) collective-permute-start(bf16[192,512]{1,0:T(8,128)(2,1)} %get-tuple-element.110), channel_id=1, source_target_pairs={{0,6},{1,7},{2,0},{3,1},{4,2},{5,3},{6,4},{7,5},{8,14},{9,15},{10,... | collective-permute-start | bytes 589832 | tf_op jit(solution)/shard_map/ppermute | solution.py:118
  162.2 29.5 %collective-permute-start.34 = (bf16[384,512]{1,0:T(8,128)(2,1)}, bf16[384,512]{1,0:T(8,128)(2,1)S(1)}, u32[]{:S(2)}, u32[]{:S(2)}) collective-permute-start(bf16[384,512]{1,0:T(8,128)(2,1)} %get-tuple-element.128), channel_id=1, source_target_pairs={{0,96},{8,104},{16,112},{24,120},{32,0},{40,8},{48,16},{56,24},{64... | collective-permute-start | bytes 1179656 | tf_op jit(solution)/shard_map/ppermute | solution.py:101
  165.0 26.7 %collective-permute-start.35 = (bf16[384,512]{1,0:T(8,128)(2,1)}, bf16[384,512]{1,0:T(8,128)(2,1)S(1)}, u32[]{:S(2)}, u32[]{:S(2)}) collective-permute-start(bf16[384,512]{1,0:T(8,128)(2,1)} %get-tuple-element.129), channel_id=1, source_target_pairs={{0,64},{8,72},{16,80},{24,88},{32,96},{40,104},{48,112},{56,120},{... | collective-permute-start | bytes 1179656 | tf_op jit(solution)/shard_map/ppermute | solution.py:101
  166.4 25.3 %collective-permute-start.36 = (bf16[384,512]{1,0:T(8,128)(2,1)}, bf16[384,512]{1,0:T(8,128)(2,1)S(1)}, u32[]{:S(2)}, u32[]{:S(2)}) collective-permute-start(bf16[384,512]{1,0:T(8,128)(2,1)} %get-tuple-element.130), channel_id=1, source_target_pairs={{0,32},{8,40},{16,48},{24,56},{32,64},{40,72},{48,80},{56,88},{64,... | collective-permute-start | bytes 1179656 | tf_op jit(solution)/shard_map/ppermute | solution.py:101
  175.0 16.7 %collective-permute-start.32 = (bf16[192,512]{1,0:T(8,128)(2,1)}, bf16[192,512]{1,0:T(8,128)(2,1)S(1)}, u32[]{:S(2)}, u32[]{:S(2)}) collective-permute-start(bf16[192,512]{1,0:T(8,128)(2,1)} %get-tuple-element.125), channel_id=1, source_target_pairs={{0,16},{8,24},{16,0},{24,8},{32,48},{40,56},{48,32},{56,40},{64,80... | collective-permute-start | bytes 589832 | tf_op jit(solution)/shard_map/ppermute | solution.py:94
  197.7 37.7 %all-to-all-start = ((bf16[16,48,1536]{2,1,0:T(8,128)(2,1)}), bf16[16,48,1536]{2,1,0:T(8,128)(2,1)S(1)}, u32[]{:S(2)}, u32[]{:S(2)}) async-start(bf16[16,48,1536]{2,1,0:T(8,128)(2,1)} %bitcast.7), calls=%async_computation | async-start | bytes 4718592 | tf_op jit(solution)/shard_map/all_to_all | solution.py:584
  216.4 13.3 %collective-permute-start.38 = (bf16[208,512]{1,0:T(8,128)(2,1)}, bf16[208,512]{1,0:T(8,128)(2,1)S(1)}, u32[]{:S(2)}, u32[]{:S(2)}) collective-permute-start(bf16[208,512]{1,0:T(8,128)(2,1)} %get-tuple-element.142), channel_id=1, source_target_pairs={{0,2},{1,3},{2,4},{3,5},{4,6},{5,7},{6,0},{7,1},{8,10},{9,11},{10,... | collective-permute-start | bytes 638984 | tf_op jit(solution)/shard_map/ppermute | solution.py:118
  (62 other events, 426.8 us)
where the time goes:
time: 285 us; the launch traced here: 283 us
  Pallas kernels  121 us (42%)
  starting transfers between devices  69.2 us (24%)
  blocking collectives  37.9 us (13%)
  waiting for transfers between devices  34.8 us (12%)
  local copies, waits for them, and re-layouts  15.8 us (6%)
  other arithmetic  3.63 us (1%)
    pallas_call x18, Pallas kernels, call(): pl.pallas_call(body, out_shape=out_shape, in_specs=specs or [VM] * len(ar...  121 us
    all_to_all x1, blocking collectives, shards(): everything = lax.all_to_all(spread, 'tm', 0, 0, tiled=True)  37.9 us
    ppermute x15, starting transfers between devices, shift_x(): return lax.ppermute(a, 'tm', pairs)  23.9 us
    ppermute x12, starting transfers between devices, shift_y(): return lax.ppermute(a, 'mp', pairs)  18.3 us
    ppermute x12, waiting for transfers between devices, shift_y(): return lax.ppermute(a, 'mp', pairs)  11.7 us
    ppermute x6, starting transfers between devices, shift_z(): return lax.ppermute(a, 'tm', pairs)  11.6 us
    unnamed x88, local copies, waits for them, and re-layouts  10.5 us
    ppermute x15, waiting for transfers between devices, shift_x(): return lax.ppermute(a, 'tm', pairs)  10.3 us
  transfers between devices with their start and end apart: 42, of which 14 were waited for; matrix products, arithmetic and copies ran while one was open for 2% of the time, Pallas kernels for 35%

commit v1 on v0

--- a/solution.py
+++ b/solution.py
@@ -404,17 +404,15 @@
         outs[d][chunk:, :] = tail
 
 
-def spread_small_body(in_ref, small_ref, out_ref):
-    members, _, width = in_ref.shape
+def spread_body(in_ref, out_ref):
+    members = in_ref.shape[0]
     total = sum(in_ref[i].astype(F32) for i in range(members)).astype(BF16)
-    small = small_ref[...]
     for i in range(members):
-        out_ref[i, :, :width] = total
-        out_ref[i, :, width:] = small
-
-
-def finish_body(heads, all_ref, qkv_out, proj_out, small_out):
-    members, each, _ = all_ref.shape
+        out_ref[i] = total
+
+
+def finish_body(heads, all_ref, qkv_out, proj_out):
+    _, each, _ = all_ref.shape
     width = qkv_out.shape[2]
     step = 8
 
@@ -429,7 +427,6 @@
                 qkv_out[j, at : at + step, :] = rows_of((h * 3 + j) * HEAD_DIM + i)
     for i in range(0, heads * HEAD_DIM, step):
         proj_out[i : i + step, :] = rows_of(3 * heads * HEAD_DIM + i)
-    small_out[...] = sum(all_ref[m, :, width:].astype(F32) for m in range(members))
 
 
 def tie(value, *others):
@@ -554,17 +551,38 @@
     dkv_terms = ring(shift_z, dkv, -1)
     dq_terms = ring(shift_x, dq, -1)
 
-    mixed = sum(t.astype(F32) for t in [tie(proj_terms[0], dq[0])] + proj_terms[1:])
-    residual = (frames.astype(F32) + mixed).astype(BF16)
-    res_left, res_right = halos(residual)
     (out_part,) = call(
         out_weights_body, [((head_cols, width), BF16)],
         [tie(attended, dq[0]), back_full], flops=2 * head_cols * width * rows,
     )
+    all_gp, part = call(
+        functools.partial(weights_body, heads),
+        [((3 * head_cols, rows), BF16), ((4 * head_cols, width), BF16)],
+        [*dq_terms, *dkv_terms, normed, out_part],
+        flops=2 * 3 * head_cols * width * rows,
+    )
+    each = part.shape[0] // members
+    got = lax.all_to_all(part.reshape(members, each, width), "tm", 0, 0, tiled=True)
+
+    gn_own, gn_other = call(
+        functools.partial(grads_body, heads, width),
+        [((half + 8, rows), F32), ((half + PAD, rows), BF16)],
+        [tie(all_gp, part), queries, keys_values, wq_rel],
+        flops=2 * 3 * head_cols * width * rows,
+    )
+    gn_got = swap_core(gn_other)
+    gn_blocks = call(grads_pair_body, [((own_width + PAD, rows), BF16)] * SIDE, [gn_own, gn_got])
+    gn_terms = ring(shift_y, gn_blocks, 1)
+
+    mixed = sum(t.astype(F32) for t in [tie(proj_terms[0], *gn_blocks)] + proj_terms[1:])
+    residual = (frames.astype(F32) + mixed).astype(BF16)
+    res_left, res_right = halos(residual)
+    (spread,) = call(spread_body, [((members, each, width), BF16)], [tie(got, res_left, res_right)])
+    everything = lax.all_to_all(spread, "tm", 0, 0, tiled=True)
     block_out, kernel_part = call(
         conv_body,
         [((own_width, rows), BF16), ((taps, own_width), F32)],
-        [res_left, residual, res_right, grad_out, conv_kernel], None,
+        [tie(res_left, spread), residual, res_right, grad_out, conv_kernel], None,
         [
             pltpu.VMEM((rows + 2 * PAD, own_width), F32),
             pltpu.VMEM((rows, own_width), F32),
@@ -574,25 +592,7 @@
         flops=16 * own_width * rows * taps,
     )
 
-    all_gp, part = call(
-        functools.partial(weights_body, heads),
-        [((3 * head_cols, rows), BF16), ((4 * head_cols, width), BF16)],
-        [*dq_terms, *dkv_terms, normed, tie(out_part, kernel_part)],
-        flops=2 * 3 * head_cols * width * rows,
-    )
-    each = part.shape[0] // members
-    got = lax.all_to_all(part.reshape(members, each, width), "tm", 0, 0, tiled=True)
-
-    gn_own, gn_other = call(
-        functools.partial(grads_body, heads, width),
-        [((half + 8, rows), F32), ((half + PAD, rows), BF16)],
-        [tie(all_gp, part), queries, keys_values, wq_rel],
-        flops=2 * 3 * head_cols * width * rows,
-    )
-    gn_got = swap_core(gn_other)
-    gn_blocks = call(grads_pair_body, [((own_width + PAD, rows), BF16)] * SIDE, [gn_own, gn_got])
-    gn_terms = ring(shift_y, gn_blocks, 1)
-    summed = sum(t.astype(F32) for t in gn_terms)
+    summed = sum(t.astype(F32) for t in [tie(gn_terms[0], spread)] + gn_terms[1:])
     grad_own = summed[:own_width]
     dots = summed[own_width : own_width + 1] + summed[own_width + 1 : own_width + 2]
     column_start = lax.axis_index("mp") * own_width
@@ -603,18 +603,13 @@
     ).astype(BF16)
     gain_part = jnp.sum(grad_own * normed_own, axis=1)
     small = jnp.concatenate([kernel_part.astype(BF16), gain_part.astype(BF16)[None]], axis=0)
-    small_cols = small.size // each
-    (spread,) = call(
-        spread_small_body, [((members, each, width + small_cols), BF16)],
-        [got, small.reshape(each, small_cols)],
-    )
-    everything = lax.all_to_all(spread, "tm", 0, 0, tiled=True)
-    qkv_grads, out_grads, small_sum = call(
+    for shift in (shift_x, shift_z):
+        small = sum(t.astype(F32) for t in ring(shift, [small] * SIDE, 1)).astype(BF16)
+    small_sum = small.astype(F32)
+    qkv_grads, out_grads = call(
         functools.partial(finish_body, heads),
-        [((3, head_cols, width), F32), ((head_cols, width), F32), ((each, small_cols), F32)],
-        [everything],
-    )
-    small_sum = small_sum.reshape(taps + 1, own_width)
+        [((3, head_cols, width), F32), ((head_cols, width), F32)], [everything],
+    )
     return block_out, grad_frames, small_sum[taps], qkv_grads, out_grads, small_sum[:taps]
 
 

time: 285 us -> 286 us (level)
  blocking collectives: 37.9 us -> 0 us
  waiting for transfers between devices: 34.8 us -> 62.5 us
  starting transfers between devices: 69.2 us -> 78.6 us
    all_to_all x1 -> x0, blocking collectives: 37.9 us -> none  [shards(): everything = lax.all_to_all(spread, 'tm', 0, 0, tiled=True)]
    ppermute x15 -> x18, waiting for transfers between devices: 10.3 us -> 19 us  [shift_x(): return lax.ppermute(a, 'tm', pairs)]
    ppermute x6 -> x9, waiting for transfers between devices: 0.02 us -> 7.52 us  [shift_z(): return lax.ppermute(a, 'tm', pairs)]
    ppermute x2, waiting for transfers between devices: 0.43 us -> 7.22 us  [halos(): lax.ppermute(a[:, a.shape[1] - slab:], 'tm', [(i, i + 1) for i in range(e...]
    ppermute x6 -> x9, starting transfers between devices: 11.6 us -> 17.1 us  [shift_z(): return lax.ppermute(a, 'tm', pairs)]
    ppermute x12, waiting for transfers between devices: 11.7 us -> 16.7 us  [shift_y(): return lax.ppermute(a, 'mp', pairs)]
    all_to_all x1, starting transfers between devices: 8 us -> 3.99 us  [shards(): lax.all_to_all(part.reshape(members, each, width), 'tm', 0, 0, tiled=True)]
    all_to_all x0 -> x1, starting transfers between devices: none -> 3.87 us  [shards(): everything = lax.all_to_all(spread, 'tm', 0, 0, tiled=True)]
  transfers between devices with their start and end apart: 42 -> 49, of which waited for: 14 -> 23; matrix products, arithmetic and copies ran while one was open for 2% -> 3% of each run, Pallas kernels for 35% -> 25%
where the time goes in v1:
time: 286 us; the launch traced here: 285 us
  Pallas kernels  121 us (42%)
  starting transfers between devices  78.6 us (27%)
  waiting for transfers between devices  62.5 us (22%)
  local copies, waits for them, and re-layouts  16.3 us (6%)
  other arithmetic  5.64 us (2%)
    pallas_call x18, Pallas kernels, call(): pl.pallas_call(body, out_shape=out_shape, in_specs=specs or [VM] * len(ar...  121 us
    ppermute x18, starting transfers between devices, shift_x(): return lax.ppermute(a, 'tm', pairs)  26 us
    ppermute x18, waiting for transfers between devices, shift_x(): return lax.ppermute(a, 'tm', pairs)  19 us
    ppermute x12, starting transfers between devices, shift_y(): return lax.ppermute(a, 'mp', pairs)  17.7 us
    ppermute x9, starting transfers between devices, shift_z(): return lax.ppermute(a, 'tm', pairs)  17.1 us
    ppermute x12, waiting for transfers between devices, shift_y(): return lax.ppermute(a, 'mp', pairs)  16.7 us
    unnamed x92, local copies, waits for them, and re-layouts  11.8 us
    ppermute x9, waiting for transfers between devices, shift_z(): return lax.ppermute(a, 'tm', pairs)  7.52 us
  transfers between devices with their start and end apart: 49, of which 23 were waited for; matrix products, arithmetic and copies ran while one was open for 3% of the time, Pallas kernels for 25%

profile of v1, /device:TPU:0, one launch (start us, length us, event | category | flops | bytes accessed | tf_op | source)
XLA Modules:
  0.0 285.3 jit_solution(7527519460903953031)
XLA Ops:
  12.6 4.2 %collective-permute-done.4.right_ref = bf16[192,128]{1,0:T(8,128)(2,1)S(1)} collective-permute-done((bf16[192,128]{1,0:T(8,128)(2,1)S(1)}, bf16[192,128]{1,0:T(8,128)(2,1)S(1)}, u32[]{:S(2)}, u32[]{:S(2)}) %collective-permute-start.4) | collective-permute-done | bytes 49184 | tf_op jit(solution)/shard_map/ppermute | solution.py:108
  17.5 4.3 %shard_map.109 = (f32[192,512]{1,0:T(8,128)}, bf16[192,512]{1,0:T(8,128)(2,1)}) custom-call(bf16[192,128]{1,0:T(8,128)(2,1)} %copy-done.35, bf16[192,512]{1,0:T(8,128)(2,1)} %up_ref.1, bf16[192,128]{1,0:T(8,128)(2,1)} %copy-done.36, f32[31,192]{1,0:T(8,128)} %taps_ref.3), custom_call_target="tpu_custom_call" | custom-call | flops 24379392 | bytes 908544 | tf_op jit(solution)/shard_map/pallas_call | solution.py:130
  29.5 4.6 %shard_map.110 = (bf16[1536,512]{1,0:T(8,128)(2,1)}, f32[1,512]{1,0:T(1,128)}, bf16[192,512]{1,0:T(8,128)(2,1)}, bf16[384,512]{1,0:T(8,128)(2,1)}) custom-call(s32[8]{0:T(128)} %add.124.pos_ref, bf16[192,512]{1,0:T(8,128)(2,1)} %b0, bf16[192,512]{1,0:T(8,128)(2,1)} %copy-done.5, bf16[192,512]{1,0:T(8,128)(2,1)} %copy-done.6, bf16[192,512]{1,0:T(8,128)(2,1)} %copy-done.7, ...), custom_call_target="tpu_custom_call" | custom-call | flops 905969664 | bytes 5513248 | tf_op jit(solution)/shard_map/pallas_call | solution.py:130
  40.3 3.6 %collective-permute-start.14 = (bf16[384,512]{1,0:T(8,128)(2,1)S(1)}, bf16[384,512]{1,0:T(8,128)(2,1)S(1)}, u32[]{:S(2)}, u32[]{:S(2)}) collective-permute-start(bf16[384,512]{1,0:T(8,128)(2,1)S(1)} %copy-done.40), channel_id=1, source_target_pairs={{0,64},{8,72},{16,80},{24,88},{32,96},{40,104},{48,112},{56,120},{... | collective-permute-start | bytes 1179656 | tf_op jit(solution)/shard_map/ppermute | solution.py:101
  62.5 23.0 %shard_map.112 = (bf16[192,2048]{1,0:T(8,128)(2,1)}, f32[3,2048]{1,0:T(4,128)}) custom-call(bf16[192,512]{1,0:T(8,128)(2,1)} %get-tuple-element.92.refs_0_.q_ref, bf16[192,512]{1,0:T(8,128)(2,1)} %copy-done.44, bf16[192,512]{1,0:T(8,128)(2,1)} %collective-permute-done.11.refs_2_, bf16[192,512]{1,0:T(8,128)(2,1)} %copy-done.45, ...), custom_call_target="tpu_custom_call" | custom-call | flops 12884901888 | bytes 3170304 | tf_op jit(solution)/shard_map/pallas_call | solution.py:130
  95.1 3.9 %shard_map.114 = (bf16[1536,576]{1,0:T(8,128)(2,1)}, bf16[1536,192]{1,0:T(8,128)(2,1)}) custom-call(s32[8]{0:T(128)} %add.129.pos_ref, bf16[3,192,1536]{2,1,0:T(8,128)(2,1)} %w_ref.3, bf16[192,1536]{1,0:T(8,128)(2,1)} %wo_ref.3), custom_call_target="tpu_custom_call" | custom-call | bytes 4718624 | tf_op jit(solution)/shard_map/pallas_call | solution.py:130
  104.6 15.2 %shard_map.116 = (bf16[64,512]{1,0:T(8,128)(2,1)}, bf16[64,512]{1,0:T(8,128)(2,1)}, bf16[64,512]{1,0:T(8,128)(2,1)}, bf16[64,512]{1,0:T(8,128)(2,1)}, bf16[128,5...) custom-call(bf16[192,512]{1,0:T(8,128)(2,1)} %get-tuple-element.92.refs_0_.q_ref, ...), custom_call_target="tpu_custom_call" | custom-call | flops 10737418240 | bytes 4063232 | tf_op jit(solution)/shard_map/pallas_call | solution.py:130
  130.7 27.5 %shard_map.119 = (bf16[192,512]{1,0:T(8,128)(2,1)}, bf16[192,512]{1,0:T(8,128)(2,1)}, bf16[192,512]{1,0:T(8,128)(2,1)}, bf16[192,512]{1,0:T(8,128)(2,1)}, bf16[3...) custom-call(bf16[192,512]{1,0:T(8,128)(2,1)} %get-tuple-element.92.refs_0_.q, ...), custom_call_target="tpu_custom_call" | custom-call | flops 21474836480 | bytes 6422528 | tf_op jit(solution)/shard_map/pallas_call | solution.py:130
  171.2 4.4 %collective-permute-done.27.refs_2_ = bf16[192,512]{1,0:T(8,128)(2,1)S(1)} collective-permute-done((bf16[192,512]{1,0:T(8,128)(2,1)}, bf16[192,512]{1,0:T(8,128)(2,1)S(1)}, u32[]{:S(2)}, u32[]{:S(2)}) %collective-permute-start.27) | collective-permute-done | bytes 196640 | tf_op jit(solution)/shard_map/ppermute | solution.py:94
  180.4 3.6 %collective-permute-done.31.refs_7_ = bf16[384,512]{1,0:T(8,128)(2,1)S(1)} collective-permute-done((bf16[384,512]{1,0:T(8,128)(2,1)}, bf16[384,512]{1,0:T(8,128)(2,1)S(1)}, u32[]{:S(2)}, u32[]{:S(2)}) %collective-permute-start.31) | collective-permute-done | bytes 393248 | tf_op jit(solution)/shard_map/ppermute | solution.py:101
  184.7 4.9 %shard_map.121 = (bf16[576,512]{1,0:T(8,128)(2,1)}, bf16[768,1536]{1,0:T(8,128)(2,1)}) custom-call(bf16[192,512]{1,0:T(8,128)(2,1)} %get-tuple-element.120.refs_0_, bf16[192,512]{1,0:T(8,128)(2,1)} %copy-done.20, bf16[192,512]{1,0:T(8,128)(2,1)} %copy-done.21, bf16[192,512]{1,0:T(8,128)(2,1)} %copy-done.22, bf16[384,512]{1,0:T(8,128)(2,1)} %get-tuple-element.124.refs_4_, ...), custom_call_target="tpu_custom_call" | custom-call | flops 905969664 | bytes 7471104 | tf_op jit(solution)/shard_map/pallas_call | solution.py:130
  189.6 4.0 %all-to-all-start = ((bf16[16,48,1536]{2,1,0:T(8,128)(2,1)}), bf16[16,48,1536]{2,1,0:T(8,128)(2,1)S(1)}, u32[]{:S(2)}, u32[]{:S(2)}) async-start(bf16[16,48,1536]{2,1,0:T(8,128)(2,1)} %bitcast.7), calls=%async_computation | async-start | bytes 4718592 | tf_op jit(solution)/shard_map/all_to_all | solution.py:565
  193.5 4.8 %shard_map.122 = (f32[776,512]{1,0:T(8,128)}, bf16[784,512]{1,0:T(8,128)(2,1)}) custom-call(bf16[576,512]{1,0:T(8,128)(2,1)} %get-tuple-element.132.all_gp, bf16[192,512]{1,0:T(8,128)(2,1)} %get-tuple-element.92.refs_0_.q_ref, bf16[384,512]{1,0:T(8,128)(2,1)} %get-tuple-element.86.refs_4_.kv_ref, bf16[1536,576]{1,0:T(8,128)(2,1)} %get-tuple-element.133.wq_ref), custom_call_target="tpu_custom_call" | custom-call | flops 905969664 | bytes 5341184 | tf_op jit(solution)/shard_map/pallas_call | solution.py:130
  198.8 3.6 %collective-permute-start.34 = (bf16[192,512]{1,0:T(8,128)(2,1)}, bf16[192,512]{1,0:T(8,128)(2,1)}, u32[]{:S(2)}, u32[]{:S(2)}) collective-permute-start(bf16[192,512]{1,0:T(8,128)(2,1)} %get-tuple-element.110), channel_id=1, source_target_pairs={{0,4},{1,5},{2,6},{3,7},{4,0},{5,1},{6,2},{7,3},{8,12},{9,13},{10,... | collective-permute-start | bytes 589832 | tf_op jit(solution)/shard_map/ppermute | solution.py:118
  207.2 5.0 %collective-permute-done.34 = bf16[192,512]{1,0:T(8,128)(2,1)} collective-permute-done((bf16[192,512]{1,0:T(8,128)(2,1)}, bf16[192,512]{1,0:T(8,128)(2,1)}, u32[]{:S(2)}, u32[]{:S(2)}) %collective-permute-start.34) | collective-permute-done | bytes 196640 | tf_op jit(solution)/shard_map/ppermute | solution.py:118
  213.4 3.8 %collective-permute-start.36 = (bf16[192,128]{1,0:T(8,128)(2,1)S(1)}, bf16[192,128]{1,0:T(8,128)(2,1)S(1)}, u32[]{:S(2)}, u32[]{:S(2)}) collective-permute-start(bf16[192,128]{1,0:T(8,128)(2,1)S(1)} %get-tuple-element.154), channel_id=1, source_target_pairs={{0,8},{8,16},{16,24},{24,32},{32,40},{40,48},{48,56},{56,64},{64,7... | collective-permute-start | bytes 147464 | tf_op jit(solution)/shard_map/ppermute | solution.py:107
  218.6 6.8 %collective-permute-done.36.left_ref = bf16[192,128]{1,0:T(8,128)(2,1)S(1)} collective-permute-done((bf16[192,128]{1,0:T(8,128)(2,1)S(1)}, bf16[192,128]{1,0:T(8,128)(2,1)S(1)}, u32[]{:S(2)}, u32[]{:S(2)}) %collective-permute-start.36) | collective-permute-done | bytes 49184 | tf_op jit(solution)/shard_map/ppermute | solution.py:107
  235.6 3.9 %all-to-all-start.1 = ((bf16[16,48,1536]{2,1,0:T(8,128)(2,1)}), bf16[16,48,1536]{2,1,0:T(8,128)(2,1)S(1)}, u32[]{:S(2)}, u32[]{:S(2)}) async-start(bf16[16,48,1536]{2,1,0:T(8,128)(2,1)} %shard_map.124), calls=%async_computation.1 | async-start | bytes 4718592 | tf_op jit(solution)/shard_map/all_to_all | solution.py:581
  240.0 3.6 %collective-permute-start.39 = (bf16[208,512]{1,0:T(8,128)(2,1)}, bf16[208,512]{1,0:T(8,128)(2,1)}, u32[]{:S(2)}, u32[]{:S(2)}) collective-permute-start(bf16[208,512]{1,0:T(8,128)(2,1)} %get-tuple-element.138), channel_id=1, source_target_pairs={{0,4},{1,5},{2,6},{3,7},{4,0},{5,1},{6,2},{7,3},{8,12},{9,13},{10,... | collective-permute-start | bytes 638984 | tf_op jit(solution)/shard_map/ppermute | solution.py:118
  244.4 4.2 %collective-permute-done.38 = bf16[208,512]{1,0:T(8,128)(2,1)} collective-permute-done((bf16[208,512]{1,0:T(8,128)(2,1)}, bf16[208,512]{1,0:T(8,128)(2,1)}, u32[]{:S(2)}, u32[]{:S(2)}) %collective-permute-start.38) | collective-permute-done | bytes 213024 | tf_op jit(solution)/shard_map/ppermute | solution.py:118
  248.6 3.7 %collective-permute-done.39 = bf16[208,512]{1,0:T(8,128)(2,1)} collective-permute-done((bf16[208,512]{1,0:T(8,128)(2,1)}, bf16[208,512]{1,0:T(8,128)(2,1)}, u32[]{:S(2)}, u32[]{:S(2)}) %collective-permute-start.39) | collective-permute-done | bytes 213024 | tf_op jit(solution)/shard_map/ppermute | solution.py:118
  254.4 6.4 %shard_map.125 = (bf16[192,512]{1,0:T(8,128)(2,1)}, f32[31,192]{1,0:T(8,128)}) custom-call(bf16[192,128]{1,0:T(8,128)(2,1)} %copy-done.33, bf16[192,512]{1,0:T(8,128)(2,1)} %copy-done.3, bf16[192,128]{1,0:T(8,128)(2,1)} %copy-done.34, bf16[192,512]{1,0:T(8,128)(2,1)} %up_ref.1, f32[31,192]{1,0:T(8,128)} %taps_ref.3), custom_call_target="tpu_custom_call" | custom-call | flops 48758784 | bytes 735744 | tf_op jit(solution)/shard_map/pallas_call | solution.py:130
  268.4 3.6 %collective-permute-done.42 = bf16[32,192]{1,0:T(8,128)(2,1)S(1)} collective-permute-done((bf16[32,192]{1,0:T(8,128)(2,1)S(1)}, bf16[32,192]{1,0:T(8,128)(2,1)S(1)}, u32[]{:S(2)}, u32[]{:S(2)}) %collective-permute-start.42) | collective-permute-done | bytes 12320 | tf_op jit(solution)/shard_map/ppermute | solution.py:94
  281.2 4.1 %shard_map.126 = (f32[3,192,1536]{2,1,0:T(8,128)}, f32[192,1536]{1,0:T(8,128)}) custom-call(bf16[16,48,1536]{2,1,0:T(8,128)(2,1)} %copy-done), custom_call_target="tpu_custom_call" | custom-call | bytes 7077888 | tf_op jit(solution)/shard_map/pallas_call | solution.py:130
  (205 shorter events, 127.7 us)
Async XLA Ops:
  0.6 21.2 %collective-permute-start = (bf16[192,512]{1,0:T(8,128)(2,1)}, bf16[192,512]{1,0:T(8,128)(2,1)S(1)}, u32[]{:S(2)}, u32[]{:S(2)}) collective-permute-start(bf16[192,512]{1,0:T(8,128)(2,1)} %b0), channel_id=1, source_target_pairs={{0,2},{1,3},{2,4},{3,5},{4,6},{5,7},{6,0},{7,1},{8,10},{9,11},{10,... | collective-permute-start | bytes 589832 | tf_op jit(solution)/shard_map/ppermute | solution.py:118
  2.4 19.4 %collective-permute-start.1 = (bf16[192,512]{1,0:T(8,128)(2,1)}, bf16[192,512]{1,0:T(8,128)(2,1)S(1)}, u32[]{:S(2)}, u32[]{:S(2)}) collective-permute-start(bf16[192,512]{1,0:T(8,128)(2,1)} %b0), channel_id=1, source_target_pairs={{0,4},{1,5},{2,6},{3,7},{4,0},{5,1},{6,2},{7,3},{8,12},{9,13},{10,... | collective-permute-start | bytes 589832 | tf_op jit(solution)/shard_map/ppermute | solution.py:118
  5.3 16.5 %collective-permute-start.2 = (bf16[192,512]{1,0:T(8,128)(2,1)}, bf16[192,512]{1,0:T(8,128)(2,1)S(1)}, u32[]{:S(2)}, u32[]{:S(2)}) collective-permute-start(bf16[192,512]{1,0:T(8,128)(2,1)} %b0), channel_id=1, source_target_pairs={{0,6},{1,7},{2,0},{3,1},{4,2},{5,3},{6,4},{7,5},{8,14},{9,15},{10,... | collective-permute-start | bytes 589832 | tf_op jit(solution)/shard_map/ppermute | solution.py:118
  23.3 12.8 %collective-permute-start.6 = (bf16[192,512]{1,0:T(8,128)(2,1)S(1)}, bf16[192,512]{1,0:T(8,128)(2,1)S(1)}, u32[]{:S(2)}, u32[]{:S(2)}) collective-permute-start(bf16[192,512]{1,0:T(8,128)(2,1)S(1)} %copy-done.9), channel_id=1, source_target_pairs={{0,2},{1,3},{2,4},{3,5},{4,6},{5,7},{6,0},{7,1},{8,10},{9,11},{10,... | collective-permute-start | bytes 589832 | tf_op jit(solution)/shard_map/ppermute | solution.py:118
  24.1 12.0 %collective-permute-start.7 = (bf16[192,512]{1,0:T(8,128)(2,1)S(1)}, bf16[192,512]{1,0:T(8,128)(2,1)S(1)}, u32[]{:S(2)}, u32[]{:S(2)}) collective-permute-start(bf16[192,512]{1,0:T(8,128)(2,1)S(1)} %copy-done.9), channel_id=1, source_target_pairs={{0,4},{1,5},{2,6},{3,7},{4,0},{5,1},{6,2},{7,3},{8,12},{9,13},{10,... | collective-permute-start | bytes 589832 | tf_op jit(solution)/shard_map/ppermute | solution.py:118
  24.8 11.9 %collective-permute-start.8 = (bf16[192,512]{1,0:T(8,128)(2,1)S(1)}, bf16[192,512]{1,0:T(8,128)(2,1)S(1)}, u32[]{:S(2)}, u32[]{:S(2)}) collective-permute-start(bf16[192,512]{1,0:T(8,128)(2,1)S(1)} %copy-done.9), channel_id=1, source_target_pairs={{0,6},{1,7},{2,0},{3,1},{4,2},{5,3},{6,4},{7,5},{8,14},{9,15},{10,... | collective-permute-start | bytes 589832 | tf_op jit(solution)/shard_map/ppermute | solution.py:118
  36.8 13.1 %collective-permute-start.9 = (bf16[768,512]{1,0:T(8,128)(2,1)S(1)}, bf16[768,512]{1,0:T(8,128)(2,1)S(1)}, u32[]{:S(2)}, u32[]{:S(2)}) collective-permute-start(bf16[768,512]{1,0:T(8,128)(2,1)S(1)} %pad_maximum_fusion.1), channel_id=1, source_target_pairs={{0,1},{1,0},{2,3},{3,2},{4,5},{5,4},{6,7},{7,6},{8,9},{9,8},{10,11... | collective-permute-start | bytes 2359304 | tf_op jit(solution)/shard_map/ppermute | solution.py:123
  38.4 21.8 %collective-permute-start.13 = (bf16[384,512]{1,0:T(8,128)(2,1)S(1)}, bf16[384,512]{1,0:T(8,128)(2,1)S(1)}, u32[]{:S(2)}, u32[]{:S(2)}) collective-permute-start(bf16[384,512]{1,0:T(8,128)(2,1)S(1)} %copy-done.40), channel_id=1, source_target_pairs={{0,32},{8,40},{16,48},{24,56},{32,64},{40,72},{48,80},{56,88},{64,... | collective-permute-start | bytes 1179656 | tf_op jit(solution)/shard_map/ppermute | solution.py:101
  40.3 21.4 %collective-permute-start.14 = (bf16[384,512]{1,0:T(8,128)(2,1)S(1)}, bf16[384,512]{1,0:T(8,128)(2,1)S(1)}, u32[]{:S(2)}, u32[]{:S(2)}) collective-permute-start(bf16[384,512]{1,0:T(8,128)(2,1)S(1)} %copy-done.40), channel_id=1, source_target_pairs={{0,64},{8,72},{16,80},{24,88},{32,96},{40,104},{48,112},{56,120},{... | collective-permute-start | bytes 1179656 | tf_op jit(solution)/shard_map/ppermute | solution.py:101
  43.9 17.8 %collective-permute-start.15 = (bf16[384,512]{1,0:T(8,128)(2,1)S(1)}, bf16[384,512]{1,0:T(8,128)(2,1)}, u32[]{:S(2)}, u32[]{:S(2)}) collective-permute-start(bf16[384,512]{1,0:T(8,128)(2,1)S(1)} %copy-done.40), channel_id=1, source_target_pairs={{0,96},{8,104},{16,112},{24,120},{32,0},{40,8},{48,16},{56,24},{64... | collective-permute-start | bytes 1179656 | tf_op jit(solution)/shard_map/ppermute | solution.py:101
  55.9 29.7 %collective-permute-start.16 = (bf16[192,512]{1,0:T(8,128)(2,1)}, bf16[192,512]{1,0:T(8,128)(2,1)S(1)}, u32[]{:S(2)}, u32[]{:S(2)}) collective-permute-start(bf16[192,512]{1,0:T(8,128)(2,1)} %get-tuple-element.91.refs_0_.refs_8_), channel_id=1, source_target_pairs={{0,8},{8,16},{16,24},{24,0},{32,40},{40,48},{48,56},{56,32},{64,72... | collective-permute-start | bytes 589832 | tf_op jit(solution)/shard_map/ppermute | solution.py:94
  58.8 26.7 %collective-permute-start.17 = (bf16[192,512]{1,0:T(8,128)(2,1)}, bf16[192,512]{1,0:T(8,128)(2,1)S(1)}, u32[]{:S(2)}, u32[]{:S(2)}) collective-permute-start(bf16[192,512]{1,0:T(8,128)(2,1)} %get-tuple-element.91.refs_0_.refs_8_), channel_id=1, source_target_pairs={{0,16},{8,24},{16,0},{24,8},{32,48},{40,56},{48,32},{56,40},{64,80... | collective-permute-start | bytes 589832 | tf_op jit(solution)/shard_map/ppermute | solution.py:94
  60.3 25.3 %collective-permute-start.18 = (bf16[192,512]{1,0:T(8,128)(2,1)}, bf16[192,512]{1,0:T(8,128)(2,1)S(1)}, u32[]{:S(2)}, u32[]{:S(2)}) collective-permute-start(bf16[192,512]{1,0:T(8,128)(2,1)} %get-tuple-element.91.refs_0_.refs_8_), channel_id=1, source_target_pairs={{0,24},{8,0},{16,8},{24,16},{32,56},{40,32},{48,40},{56,48},{64,88... | collective-permute-start | bytes 589832 | tf_op jit(solution)/shard_map/ppermute | solution.py:94
  102.5 17.2 %collective-permute-start.22 = (bf16[192,512]{1,0:T(8,128)(2,1)}, bf16[192,512]{1,0:T(8,128)(2,1)S(1)}, u32[]{:S(2)}, u32[]{:S(2)}) collective-permute-start(bf16[192,512]{1,0:T(8,128)(2,1)} %get-tuple-element.103), channel_id=1, source_target_pairs={{0,24},{8,0},{16,8},{24,16},{32,56},{40,32},{48,40},{56,48},{64,88... | collective-permute-start | bytes 589832 | tf_op jit(solution)/shard_map/ppermute | solution.py:94
  103.1 16.7 %collective-permute-start.23 = (bf16[192,512]{1,0:T(8,128)(2,1)}, bf16[192,512]{1,0:T(8,128)(2,1)S(1)}, u32[]{:S(2)}, u32[]{:S(2)}) collective-permute-start(bf16[192,512]{1,0:T(8,128)(2,1)} %get-tuple-element.104), channel_id=1, source_target_pairs={{0,16},{8,24},{16,0},{24,8},{32,48},{40,56},{48,32},{56,40},{64,80... | collective-permute-start | bytes 589832 | tf_op jit(solution)/shard_map/ppermute | solution.py:94
  104.4 15.4 %collective-permute-start.24 = (bf16[192,512]{1,0:T(8,128)(2,1)}, bf16[192,512]{1,0:T(8,128)(2,1)S(1)}, u32[]{:S(2)}, u32[]{:S(2)}) collective-permute-start(bf16[192,512]{1,0:T(8,128)(2,1)} %get-tuple-element.105), channel_id=1, source_target_pairs={{0,8},{8,16},{16,24},{24,0},{32,40},{40,48},{48,56},{56,32},{64,72... | collective-permute-start | bytes 589832 | tf_op jit(solution)/shard_map/ppermute | solution.py:94
  161.2 19.1 %collective-permute-start.29 = (bf16[384,512]{1,0:T(8,128)(2,1)}, bf16[384,512]{1,0:T(8,128)(2,1)S(1)}, u32[]{:S(2)}, u32[]{:S(2)}) collective-permute-start(bf16[384,512]{1,0:T(8,128)(2,1)} %get-tuple-element.125), channel_id=1, source_target_pairs={{0,96},{8,104},{16,112},{24,120},{32,0},{40,8},{48,16},{56,24},{64... | collective-permute-start | bytes 1179656 | tf_op jit(solution)/shard_map/ppermute | solution.py:101
  163.2 17.2 %collective-permute-start.30 = (bf16[384,512]{1,0:T(8,128)(2,1)}, bf16[384,512]{1,0:T(8,128)(2,1)S(1)}, u32[]{:S(2)}, u32[]{:S(2)}) collective-permute-start(bf16[384,512]{1,0:T(8,128)(2,1)} %get-tuple-element.126), channel_id=1, source_target_pairs={{0,64},{8,72},{16,80},{24,88},{32,96},{40,104},{48,112},{56,120},{... | collective-permute-start | bytes 1179656 | tf_op jit(solution)/shard_map/ppermute | solution.py:101
  164.7 19.3 %collective-permute-start.31 = (bf16[384,512]{1,0:T(8,128)(2,1)}, bf16[384,512]{1,0:T(8,128)(2,1)S(1)}, u32[]{:S(2)}, u32[]{:S(2)}) collective-permute-start(bf16[384,512]{1,0:T(8,128)(2,1)} %get-tuple-element.127), channel_id=1, source_target_pairs={{0,32},{8,40},{16,48},{24,56},{32,64},{40,72},{48,80},{56,88},{64,... | collective-permute-start | bytes 1179656 | tf_op jit(solution)/shard_map/ppermute | solution.py:101
  189.6 41.1 %all-to-all-start = ((bf16[16,48,1536]{2,1,0:T(8,128)(2,1)}), bf16[16,48,1536]{2,1,0:T(8,128)(2,1)S(1)}, u32[]{:S(2)}, u32[]{:S(2)}) async-start(bf16[16,48,1536]{2,1,0:T(8,128)(2,1)} %bitcast.7), calls=%async_computation | async-start | bytes 4718592 | tf_op jit(solution)/shard_map/all_to_all | solution.py:565
  198.8 13.3 %collective-permute-start.34 = (bf16[192,512]{1,0:T(8,128)(2,1)}, bf16[192,512]{1,0:T(8,128)(2,1)}, u32[]{:S(2)}, u32[]{:S(2)}) collective-permute-start(bf16[192,512]{1,0:T(8,128)(2,1)} %get-tuple-element.110), channel_id=1, source_target_pairs={{0,4},{1,5},{2,6},{3,7},{4,0},{5,1},{6,2},{7,3},{8,12},{9,13},{10,... | collective-permute-start | bytes 589832 | tf_op jit(solution)/shard_map/ppermute | solution.py:118
  213.4 11.9 %collective-permute-start.36 = (bf16[192,128]{1,0:T(8,128)(2,1)S(1)}, bf16[192,128]{1,0:T(8,128)(2,1)S(1)}, u32[]{:S(2)}, u32[]{:S(2)}) collective-permute-start(bf16[192,128]{1,0:T(8,128)(2,1)S(1)} %get-tuple-element.154), channel_id=1, source_target_pairs={{0,8},{8,16},{16,24},{24,32},{32,40},{40,48},{48,56},{56,64},{64,7... | collective-permute-start | bytes 147464 | tf_op jit(solution)/shard_map/ppermute | solution.py:107
  235.6 44.2 %all-to-all-start.1 = ((bf16[16,48,1536]{2,1,0:T(8,128)(2,1)}), bf16[16,48,1536]{2,1,0:T(8,128)(2,1)S(1)}, u32[]{:S(2)}, u32[]{:S(2)}) async-start(bf16[16,48,1536]{2,1,0:T(8,128)(2,1)} %shard_map.124), calls=%async_computation.1 | async-start | bytes 4718592 | tf_op jit(solution)/shard_map/all_to_all | solution.py:581
  240.0 12.2 %collective-permute-start.39 = (bf16[208,512]{1,0:T(8,128)(2,1)}, bf16[208,512]{1,0:T(8,128)(2,1)}, u32[]{:S(2)}, u32[]{:S(2)}) collective-permute-start(bf16[208,512]{1,0:T(8,128)(2,1)} %get-tuple-element.138), channel_id=1, source_target_pairs={{0,4},{1,5},{2,6},{3,7},{4,0},{5,1},{6,2},{7,3},{8,12},{9,13},{10,... | collective-permute-start | bytes 638984 | tf_op jit(solution)/shard_map/ppermute | solution.py:118
  (71 other events, 478.2 us)

commit v2 on v1

--- a/solution.py
+++ b/solution.py
@@ -152,8 +152,15 @@
         for j in range(3):
             at = (h * 3 + j) * HEAD_DIM
             mixed[at : at + HEAD_DIM, :] = w_ref[j, head_rows(h), :]
-    turned[...] = mixed[...].T
-    turned_out[...] = wo_ref[...].T
+    lanes = 128
+
+    def turn(i, carry):
+        cols = pl.ds(pl.multiple_of(i * lanes, lanes), lanes)
+        turned[cols, :] = mixed[:, cols].T
+        turned_out[cols, :] = wo_ref[:, cols].T
+        return carry
+
+    lax.fori_loop(0, width // lanes, turn, 0)
     chunk = width // 8
     for r in range(8):
         rows = pl.ds(pl.multiple_of(pos_ref[r] * chunk, chunk), chunk)
@@ -331,8 +338,16 @@
     att_out, own_out, other_out = refs[SIDE + 1 :]
     attended = sum_terms(terms).astype(BF16)
     half = own_out.shape[0]
-    other_out[...] = nn(wo_ref[half:, :], attended).astype(BF16)
-    own_out[...] = nn(wo_ref[:half, :], attended)
+    chunk = half // SIDE
+
+    def step(d, carry):
+        at = pl.multiple_of(d * chunk, chunk)
+        rows = pl.ds(at, chunk)
+        other_out[rows, :] = nn(wo_ref[pl.ds(half + at, chunk), :], attended).astype(BF16)
+        own_out[rows, :] = nn(wo_ref[rows, :], attended)
+        return carry
+
+    lax.fori_loop(0, SIDE, step, 0)
     att_out[...] = attended
 
 
@@ -358,7 +373,13 @@
         gp_out[at : at + HEAD_DIM, :] = grad_q[head_rows(h)]
         gp_out[at + HEAD_DIM : at + 2 * HEAD_DIM, :] = grad_kv[head_rows(h)]
         gp_out[at + 2 * HEAD_DIM : at + 3 * HEAD_DIM, :] = grad_kv[head_rows(heads + h)]
-    part_out[: 3 * width, :] = nt(gp_out[...], normed_ref[...]).astype(BF16)
+
+    def step(h, carry):
+        rows = pl.ds(pl.multiple_of(h * 3 * HEAD_DIM, 3 * HEAD_DIM), 3 * HEAD_DIM)
+        part_out[rows, :] = nt(gp_out[rows, :], normed_ref[...]).astype(BF16)
+        return carry
+
+    lax.fori_loop(0, heads, step, 0)
     part_out[3 * width :, :] = out_part_ref[...]
 
 
@@ -382,12 +403,20 @@
             )
     dots = dots / width
     half = wq_ref.shape[0] // 2
-    other_out[:half, :] = nn(wq_ref[half:, :], all_gp[...]).astype(BF16)
+    chunk = half // SIDE
+
+    def step(d, carry):
+        at = pl.multiple_of(d * chunk, chunk)
+        rows = pl.ds(at, chunk)
+        other_out[rows, :] = nn(wq_ref[pl.ds(half + at, chunk), :], all_gp[...]).astype(BF16)
+        own_out[rows, :] = nn(wq_ref[rows, :], all_gp[...])
+        return carry
+
+    lax.fori_loop(0, SIDE, step, 0)
     high, low = split(dots)
     other_out[half:, :] = jnp.concatenate(
         [high, low, jnp.zeros((PAD - 2, dots.shape[1]), BF16)], axis=0
     )
-    own_out[:half, :] = nn(wq_ref[:half, :], all_gp[...])
     own_out[half:, :] = jnp.broadcast_to(dots, (8, dots.shape[1]))
 
 
@@ -404,29 +433,59 @@
         outs[d][chunk:, :] = tail
 
 
-def spread_body(in_ref, out_ref):
-    members = in_ref.shape[0]
-    total = sum(in_ref[i].astype(F32) for i in range(members)).astype(BF16)
-    for i in range(members):
-        out_ref[i] = total
-
-
-def finish_body(heads, all_ref, qkv_out, proj_out):
-    _, each, _ = all_ref.shape
+def reduce_body(in_ref, small_ref, first_out, second_out):
+    members, rows, width = in_ref.shape
+    half = rows // 2
+    lanes = 256
+
+    def step(i, carry):
+        cols = pl.ds(pl.multiple_of(i * lanes, lanes), lanes)
+        total = sum(in_ref[m, :, cols].astype(F32) for m in range(members)).astype(BF16)
+        first_out[:, cols] = total[:half]
+        second_out[:, cols] = total[half:]
+        return carry
+
+    lax.fori_loop(0, width // lanes, step, 0)
+    first_out[:, width:] = small_ref[:half, :]
+    second_out[:, width:] = small_ref[half:, :]
+
+
+def finish_body(heads, pos_ref, *refs):
+    firsts, seconds = refs[:SIDE], refs[SIDE : 2 * SIDE]
+    qkv_out, proj_out, small_out, held = refs[2 * SIDE :]
+    half = firsts[0].shape[1]
+    each = 2 * half
     width = qkv_out.shape[2]
     step = 8
+    small_out[...] = jnp.zeros_like(small_out)
+    for d in range(SIDE):
+
+        def place(e, carry):
+            held[pos_ref[d * SIDE + e], :half, :] = firsts[d][e, :, :width].astype(F32)
+            held[pos_ref[e * SIDE + d], half:, :] = seconds[d][e, :, :width].astype(F32)
+            small_out[:half, :] += firsts[d][e, :, width:].astype(F32)
+            small_out[half:, :] += seconds[d][e, :, width:].astype(F32)
+            return carry
+
+        lax.fori_loop(0, SIDE, place, 0)
 
     def rows_of(row):
-        m, k = divmod(row, each)
-        return all_ref[m, k : k + step, :width].astype(F32)
-
-    for i in range(0, HEAD_DIM, step):
-        for h in range(heads):
-            for j in range(3):
-                at = h * HEAD_DIM + i
-                qkv_out[j, at : at + step, :] = rows_of((h * 3 + j) * HEAD_DIM + i)
-    for i in range(0, heads * HEAD_DIM, step):
-        proj_out[i : i + step, :] = rows_of(3 * heads * HEAD_DIM + i)
+        return held[lax.div(row, each), pl.ds(pl.multiple_of(lax.rem(row, each), step), step), :]
+
+    def write_qkv(g, carry):
+        row = g * step
+        block = lax.div(row, HEAD_DIM)
+        at = lax.div(block, 3) * HEAD_DIM + lax.rem(row, HEAD_DIM)
+        qkv_out[lax.rem(block, 3), pl.ds(pl.multiple_of(at, step), step), :] = rows_of(row)
+        return carry
+
+    def write_proj(g, carry):
+        row = g * step
+        proj_out[pl.ds(pl.multiple_of(row, step), step), :] = rows_of(row + 3 * heads * HEAD_DIM)
+        return carry
+
+    lax.fori_loop(0, 3 * heads * HEAD_DIM // step, write_qkv, 0)
+    lax.fori_loop(0, heads * HEAD_DIM // step, write_proj, 0)
 
 
 def tie(value, *others):
@@ -518,7 +577,7 @@
     )
     out_terms = ring(shift_x, out_blocks, -1)
 
-    q_block, k_block = min(1024, span), min(512, span)
+    q_block, k_block = min(256, span), min(2048, span)
 
     def head_grads(first, last, logsum, carried):
         count = last - first
@@ -551,6 +610,9 @@
     dkv_terms = ring(shift_z, dkv, -1)
     dq_terms = ring(shift_x, dq, -1)
 
+    mixed = sum(t.astype(F32) for t in [tie(proj_terms[0], dq[0])] + proj_terms[1:])
+    residual = (frames.astype(F32) + mixed).astype(BF16)
+    res_left, res_right = halos(residual)
     (out_part,) = call(
         out_weights_body, [((head_cols, width), BF16)],
         [tie(attended, dq[0]), back_full], flops=2 * head_cols * width * rows,
@@ -558,7 +620,7 @@
     all_gp, part = call(
         functools.partial(weights_body, heads),
         [((3 * head_cols, rows), BF16), ((4 * head_cols, width), BF16)],
-        [*dq_terms, *dkv_terms, normed, out_part],
+        [*dq_terms, *dkv_terms, normed, tie(out_part, res_left, res_right)],
         flops=2 * 3 * head_cols * width * rows,
     )
     each = part.shape[0] // members
@@ -573,16 +635,10 @@
     gn_got = swap_core(gn_other)
     gn_blocks = call(grads_pair_body, [((own_width + PAD, rows), BF16)] * SIDE, [gn_own, gn_got])
     gn_terms = ring(shift_y, gn_blocks, 1)
-
-    mixed = sum(t.astype(F32) for t in [tie(proj_terms[0], *gn_blocks)] + proj_terms[1:])
-    residual = (frames.astype(F32) + mixed).astype(BF16)
-    res_left, res_right = halos(residual)
-    (spread,) = call(spread_body, [((members, each, width), BF16)], [tie(got, res_left, res_right)])
-    everything = lax.all_to_all(spread, "tm", 0, 0, tiled=True)
     block_out, kernel_part = call(
         conv_body,
         [((own_width, rows), BF16), ((taps, own_width), F32)],
-        [tie(res_left, spread), residual, res_right, grad_out, conv_kernel], None,
+        [tie(res_left, *gn_blocks), residual, res_right, grad_out, conv_kernel], None,
         [
             pltpu.VMEM((rows + 2 * PAD, own_width), F32),
             pltpu.VMEM((rows, own_width), F32),
@@ -592,7 +648,7 @@
         flops=16 * own_width * rows * taps,
     )
 
-    summed = sum(t.astype(F32) for t in [tie(gn_terms[0], spread)] + gn_terms[1:])
+    summed = sum(t.astype(F32) for t in [tie(gn_terms[0], kernel_part)] + gn_terms[1:])
     grad_own = summed[:own_width]
     dots = summed[own_width : own_width + 1] + summed[own_width + 1 : own_width + 2]
     column_start = lax.axis_index("mp") * own_width
@@ -603,13 +659,24 @@
     ).astype(BF16)
     gain_part = jnp.sum(grad_own * normed_own, axis=1)
     small = jnp.concatenate([kernel_part.astype(BF16), gain_part.astype(BF16)[None]], axis=0)
-    for shift in (shift_x, shift_z):
-        small = sum(t.astype(F32) for t in ring(shift, [small] * SIDE, 1)).astype(BF16)
-    small_sum = small.astype(F32)
-    qkv_grads, out_grads = call(
+    small_cols = small.size // each
+    first, second = call(
+        reduce_body, [((each // 2, width + small_cols), BF16)] * 2,
+        [got, small.reshape(each, small_cols)],
+    )
+    first_row = jnp.stack(ring(shift_x, [first] * SIDE, 1))
+    second_row = jnp.stack(ring(shift_z, [second] * SIDE, 1))
+    first_all = ring(shift_z, [first_row] * SIDE, 1)
+    second_all = ring(shift_x, [second_row] * SIDE, 1)
+    z, x = lax.axis_index("tm") // SIDE, lax.axis_index("tm") % SIDE
+    held_at = ((z - steps + SIDE) % SIDE * SIDE)[:, None] + ((x - steps + SIDE) % SIDE)[None, :]
+    qkv_grads, out_grads, small_sum = call(
         functools.partial(finish_body, heads),
-        [((3, head_cols, width), F32), ((head_cols, width), F32)], [everything],
-    )
+        [((3, head_cols, width), F32), ((head_cols, width), F32), ((each, small_cols), F32)],
+        [held_at.reshape(-1).astype(jnp.int32), *first_all, *second_all], [SM] + [VM] * 2 * SIDE,
+        [pltpu.VMEM((members, each, width), F32)],
+    )
+    small_sum = small_sum.reshape(taps + 1, own_width)
     return block_out, grad_frames, small_sum[taps], qkv_grads, out_grads, small_sum[:taps]
 
 

time: 286 us -> 286 us (level)
  waiting for transfers between devices: 62.5 us -> 49 us
  starting transfers between devices: 78.6 us -> 84.2 us
  Pallas kernels: 121 us -> 124 us
    ppermute x12, waiting for transfers between devices: 16.7 us -> 4.51 us  [shift_y(): return lax.ppermute(a, 'mp', pairs)]
    ppermute x18 -> x21, starting transfers between devices: 26 us -> 34.5 us  [shift_x(): return lax.ppermute(a, 'tm', pairs)]
    ppermute x2, waiting for transfers between devices: 7.22 us -> 0.43 us  [halos(): lax.ppermute(a[:, a.shape[1] - slab:], 'tm', [(i, i + 1) for i in range(e...]
    all_to_all x1 -> x0, starting transfers between devices: 3.87 us -> none  [shards(): everything = lax.all_to_all(spread, 'tm', 0, 0, tiled=True)]
    pallas_call x18, Pallas kernels: 121 us -> 124 us  [call(): pl.pallas_call(body, out_shape=out_shape, in_specs=specs or [VM] * len(ar...]
    ppermute x9 -> x12, starting transfers between devices: 17.1 us -> 20.3 us  [shift_z(): return lax.ppermute(a, 'tm', pairs)]
    ppermute x9 -> x12, waiting for transfers between devices: 7.52 us -> 10.7 us  [shift_z(): return lax.ppermute(a, 'tm', pairs)]
    ppermute x18 -> x21, waiting for transfers between devices: 19 us -> 21.1 us  [shift_x(): return lax.ppermute(a, 'tm', pairs)]
  transfers between devices with their start and end apart: 49 -> 54, of which waited for: 23 -> 21; matrix products, arithmetic and copies ran while one was open for 3% -> 3% of each run, Pallas kernels for 25% -> 35%
where the time goes in v2:
time: 286 us; the launch traced here: 283 us
  Pallas kernels  124 us (43%)
  starting transfers between devices  84.2 us (29%)
  waiting for transfers between devices  49 us (17%)
  local copies, waits for them, and re-layouts  18 us (6%)
  other arithmetic  6.35 us (2%)
    pallas_call x18, Pallas kernels, call(): pl.pallas_call(body, out_shape=out_shape, in_specs=specs or [VM] * len(ar...  124 us
    ppermute x21, starting transfers between devices, shift_x(): return lax.ppermute(a, 'tm', pairs)  34.5 us
    ppermute x21, waiting for transfers between devices, shift_x(): return lax.ppermute(a, 'tm', pairs)  21.1 us
    ppermute x12, starting transfers between devices, shift_z(): return lax.ppermute(a, 'tm', pairs)  20.3 us
    ppermute x12, starting transfers between devices, shift_y(): return lax.ppermute(a, 'mp', pairs)  18.3 us
    unnamed x104, local copies, waits for them, and re-layouts  12.1 us
    ppermute x12, waiting for transfers between devices, shift_z(): return lax.ppermute(a, 'tm', pairs)  10.7 us
  transfers between devices with their start and end apart: 54, of which 21 were waited for; matrix products, arithmetic and copies ran while one was open for 3% of the time, Pallas kernels for 35%

profile of v2, /device:TPU:0, one launch (start us, length us, event | category | flops | bytes accessed | tf_op | source)
XLA Modules:
  0.0 283.2 jit_solution(475367767687815022)
XLA Ops:
  7.5 3.4 %collective-permute-start.3 = (bf16[192,128]{1,0:T(8,128)(2,1)S(1)}, bf16[192,128]{1,0:T(8,128)(2,1)S(1)}, u32[]{:S(2)}, u32[]{:S(2)}) collective-permute-start(bf16[192,128]{1,0:T(8,128)(2,1)S(1)} %get-tuple-element.162), channel_id=1, source_target_pairs={{0,8},{8,16},{16,24},{24,32},{32,40},{40,48},{48,56},{56,64},{64,7... | collective-permute-start | bytes 147464 | tf_op jit(solution)/shard_map/ppermute | solution.py:107
  12.6 4.2 %collective-permute-done.4.right_ref = bf16[192,128]{1,0:T(8,128)(2,1)S(1)} collective-permute-done((bf16[192,128]{1,0:T(8,128)(2,1)S(1)}, bf16[192,128]{1,0:T(8,128)(2,1)S(1)}, u32[]{:S(2)}, u32[]{:S(2)}) %collective-permute-start.4) | collective-permute-done | bytes 49184 | tf_op jit(solution)/shard_map/ppermute | solution.py:108
  17.5 4.4 %shard_map.109 = (f32[192,512]{1,0:T(8,128)}, bf16[192,512]{1,0:T(8,128)(2,1)}) custom-call(bf16[192,128]{1,0:T(8,128)(2,1)} %copy-done.41, bf16[192,512]{1,0:T(8,128)(2,1)} %up_ref.1, bf16[192,128]{1,0:T(8,128)(2,1)} %copy-done.42, f32[31,192]{1,0:T(8,128)} %taps_ref.3), custom_call_target="tpu_custom_call" | custom-call | flops 24379392 | bytes 908544 | tf_op jit(solution)/shard_map/pallas_call | solution.py:130
  29.6 4.6 %shard_map.110 = (bf16[1536,512]{1,0:T(8,128)(2,1)}, f32[1,512]{1,0:T(1,128)}, bf16[192,512]{1,0:T(8,128)(2,1)}, bf16[384,512]{1,0:T(8,128)(2,1)}) custom-call(s32[8]{0:T(128)} %add.157.pos_ref, bf16[192,512]{1,0:T(8,128)(2,1)} %b0, bf16[192,512]{1,0:T(8,128)(2,1)} %copy-done.6, bf16[192,512]{1,0:T(8,128)(2,1)} %copy-done.7, bf16[192,512]{1,0:T(8,128)(2,1)} %copy-done.8, ...), custom_call_target="tpu_custom_call" | custom-call | flops 905969664 | bytes 5513248 | tf_op jit(solution)/shard_map/pallas_call | solution.py:130
  40.4 3.6 %collective-permute-start.14 = (bf16[384,512]{1,0:T(8,128)(2,1)S(1)}, bf16[384,512]{1,0:T(8,128)(2,1)S(1)}, u32[]{:S(2)}, u32[]{:S(2)}) collective-permute-start(bf16[384,512]{1,0:T(8,128)(2,1)S(1)} %copy-done.46), channel_id=1, source_target_pairs={{0,64},{8,72},{16,80},{24,88},{32,96},{40,104},{48,112},{56,120},{... | collective-permute-start | bytes 1179656 | tf_op jit(solution)/shard_map/ppermute | solution.py:101
  50.7 3.0 %shard_map.111 = (bf16[1536,512]{1,0:T(8,128)(2,1)}, bf16[192,512]{1,0:T(8,128)(2,1)}) custom-call(s32[8]{0:T(128)} %add.157.pos_ref, bf16[192,512]{1,0:T(8,128)(2,1)} %get-tuple-element.90.b0, bf16[192,512]{1,0:T(8,128)(2,1)} %copy-done.11, bf16[192,512]{1,0:T(8,128)(2,1)} %copy-done.12, bf16[192,512]{1,0:T(8,128)(2,1)} %copy-done.13, ...), custom_call_target="tpu_custom_call" | custom-call | flops 301989888 | bytes 3932192 | tf_op jit(solution)/shard_map/pallas_call | solution.py:130
  62.5 23.0 %shard_map.112 = (bf16[192,2048]{1,0:T(8,128)(2,1)}, f32[3,2048]{1,0:T(4,128)}) custom-call(bf16[192,512]{1,0:T(8,128)(2,1)} %get-tuple-element.95.refs_0_.q_ref, bf16[192,512]{1,0:T(8,128)(2,1)} %copy-done.50, bf16[192,512]{1,0:T(8,128)(2,1)} %collective-permute-done.11.refs_2_, bf16[192,512]{1,0:T(8,128)(2,1)} %copy-done.51, ...), custom_call_target="tpu_custom_call" | custom-call | flops 12884901888 | bytes 3170304 | tf_op jit(solution)/shard_map/pallas_call | solution.py:130
  95.0 4.9 %shard_map.114 = (bf16[1536,576]{1,0:T(8,128)(2,1)}, bf16[1536,192]{1,0:T(8,128)(2,1)}) custom-call(s32[8]{0:T(128)} %add.162.pos_ref, bf16[3,192,1536]{2,1,0:T(8,128)(2,1)} %w_ref.3, bf16[192,1536]{1,0:T(8,128)(2,1)} %wo_ref.3), custom_call_target="tpu_custom_call" | custom-call | bytes 4718624 | tf_op jit(solution)/shard_map/pallas_call | solution.py:130
  105.5 14.7 %shard_map.116 = (bf16[64,512]{1,0:T(8,128)(2,1)}, bf16[64,512]{1,0:T(8,128)(2,1)}, bf16[64,512]{1,0:T(8,128)(2,1)}, bf16[64,512]{1,0:T(8,128)(2,1)}, bf16[128,5...) custom-call(bf16[192,512]{1,0:T(8,128)(2,1)} %get-tuple-element.95.refs_0_.q_ref, ...), custom_call_target="tpu_custom_call" | custom-call | flops 10737418240 | bytes 4063232 | tf_op jit(solution)/shard_map/pallas_call | solution.py:130
  121.7 4.1 %shard_map.117 = (bf16[192,512]{1,0:T(8,128)(2,1)}, f32[768,512]{1,0:T(8,128)}, bf16[768,512]{1,0:T(8,128)(2,1)}) custom-call(bf16[192,512]{1,0:T(8,128)(2,1)} %get-tuple-element.105.refs_0_, bf16[192,512]{1,0:T(8,128)(2,1)} %copy-done.33, bf16[192,512]{1,0:T(8,128)(2,1)} %copy-done.34, bf16[192,512]{1,0:T(8,128)(2,1)} %copy-done.35, ...), custom_call_target="tpu_custom_call" | custom-call | flops 301989888 | bytes 3932160 | tf_op jit(solution)/shard_map/pallas_call | solution.py:130
  132.2 3.6 %collective-permute-start.27 = (bf16[192,512]{1,0:T(8,128)(2,1)}, bf16[192,512]{1,0:T(8,128)(2,1)S(1)}, u32[]{:S(2)}, u32[]{:S(2)}) collective-permute-start(bf16[192,512]{1,0:T(8,128)(2,1)} %get-tuple-element.113), channel_id=1, source_target_pairs={{0,4},{1,5},{2,6},{3,7},{4,0},{5,1},{6,2},{7,3},{8,12},{9,13},{10,... | collective-permute-start | bytes 589832 | tf_op jit(solution)/shard_map/ppermute | solution.py:118
  135.7 26.5 %shard_map.119 = (bf16[192,512]{1,0:T(8,128)(2,1)}, bf16[192,512]{1,0:T(8,128)(2,1)}, bf16[192,512]{1,0:T(8,128)(2,1)}, bf16[192,512]{1,0:T(8,128)(2,1)}, bf16[3...) custom-call(bf16[192,512]{1,0:T(8,128)(2,1)} %get-tuple-element.95.refs_0_.q, ...), custom_call_target="tpu_custom_call" | custom-call | flops 21474836480 | bytes 6422528 | tf_op jit(solution)/shard_map/pallas_call | solution.py:130
  175.1 3.9 %collective-permute-start.31 = (bf16[192,512]{1,0:T(8,128)(2,1)}, bf16[192,512]{1,0:T(8,128)(2,1)S(1)}, u32[]{:S(2)}, u32[]{:S(2)}) collective-permute-start(bf16[192,512]{1,0:T(8,128)(2,1)} %get-tuple-element.126), channel_id=1, source_target_pairs={{0,16},{8,24},{16,0},{24,8},{32,48},{40,56},{48,32},{56,40},{64,80... | collective-permute-start | bytes 589832 | tf_op jit(solution)/shard_map/ppermute | solution.py:94
  182.3 3.0 %shard_map.120.refs_9_ = bf16[192,1536]{1,0:T(8,128)(2,1)} custom-call(bf16[192,512]{1,0:T(8,128)(2,1)} %get-tuple-element.134.att_ref, bf16[1536,512]{1,0:T(8,128)(2,1)} %get-tuple-element.135.full_ref), custom_call_target="tpu_custom_call" | custom-call | flops 301989888 | bytes 2359296 | tf_op jit(solution)/shard_map/pallas_call | solution.py:130
  185.3 6.0 %collective-permute-done.32.refs_3_ = bf16[192,512]{1,0:T(8,128)(2,1)S(1)} collective-permute-done((bf16[192,512]{1,0:T(8,128)(2,1)}, bf16[192,512]{1,0:T(8,128)(2,1)S(1)}, u32[]{:S(2)}, u32[]{:S(2)}) %collective-permute-start.32) | collective-permute-done | bytes 196640 | tf_op jit(solution)/shard_map/ppermute | solution.py:94
  192.5 6.1 %shard_map.121 = (bf16[576,512]{1,0:T(8,128)(2,1)}, bf16[768,1536]{1,0:T(8,128)(2,1)}) custom-call(bf16[192,512]{1,0:T(8,128)(2,1)} %get-tuple-element.123.refs_0_, bf16[192,512]{1,0:T(8,128)(2,1)} %copy-done.26, bf16[192,512]{1,0:T(8,128)(2,1)} %copy-done.27, bf16[192,512]{1,0:T(8,128)(2,1)} %copy-done.28, bf16[384,512]{1,0:T(8,128)(2,1)} %get-tuple-element.128.refs_4_, ...), custom_call_target="tpu_custom_call" | custom-call | flops 905969664 | bytes 7471104 | tf_op jit(solution)/shard_map/pallas_call | solution.py:130
  198.6 3.7 %all-to-all-start = ((bf16[16,48,1536]{2,1,0:T(8,128)(2,1)}), bf16[16,48,1536]{2,1,0:T(8,128)(2,1)S(1)}, u32[]{:S(2)}, u32[]{:S(2)}) async-start(bf16[16,48,1536]{2,1,0:T(8,128)(2,1)} %bitcast.15), calls=%async_computation | async-start | bytes 4718592 | tf_op jit(solution)/shard_map/all_to_all | solution.py:627
  202.3 5.4 %shard_map.122 = (f32[776,512]{1,0:T(8,128)}, bf16[784,512]{1,0:T(8,128)(2,1)}) custom-call(bf16[576,512]{1,0:T(8,128)(2,1)} %get-tuple-element.137.all_gp, bf16[192,512]{1,0:T(8,128)(2,1)} %get-tuple-element.95.refs_0_.q_ref, bf16[384,512]{1,0:T(8,128)(2,1)} %get-tuple-element.89.refs_4_.kv_ref, bf16[1536,576]{1,0:T(8,128)(2,1)} %get-tuple-element.138.wq_ref), custom_call_target="tpu_custom_call" | custom-call | flops 905969664 | bytes 5341184 | tf_op jit(solution)/shard_map/pallas_call | solution.py:130
  218.6 6.4 %shard_map.124 = (bf16[192,512]{1,0:T(8,128)(2,1)}, f32[31,192]{1,0:T(8,128)}) custom-call(bf16[192,128]{1,0:T(8,128)(2,1)} %copy-done.39, bf16[192,512]{1,0:T(8,128)(2,1)} %copy-done.4, bf16[192,128]{1,0:T(8,128)(2,1)} %copy-done.40, bf16[192,512]{1,0:T(8,128)(2,1)} %up_ref.1, f32[31,192]{1,0:T(8,128)} %taps_ref.3), custom_call_target="tpu_custom_call" | custom-call | flops 48758784 | bytes 735744 | tf_op jit(solution)/shard_map/pallas_call | solution.py:130
  252.5 4.3 %collective-permute-done.41 = bf16[24,1664]{1,0:T(8,128)(2,1)S(1)} collective-permute-done((bf16[24,1664]{1,0:T(8,128)(2,1)}, bf16[24,1664]{1,0:T(8,128)(2,1)S(1)}, u32[]{:S(2)}, u32[]{:S(2)}) %collective-permute-start.41) | collective-permute-done | bytes 79904 | tf_op jit(solution)/shard_map/ppermute | solution.py:94
  262.3 3.6 %collective-permute-start.45 = (bf16[4,24,1664]{2,1,0:T(8,128)(2,1)S(1)}, bf16[4,24,1664]{2,1,0:T(8,128)(2,1)S(1)}, u32[]{:S(2)}, u32[]{:S(2)}) collective-permute-start(bf16[4,24,1664]{2,1,0:T(8,128)(2,1)S(1)} %pad_maximum_fusion.2.refs_0_), channel_id=1, source_target_pairs={{0,64},{8,72},{16,80},{24,88},{32,96},{40,104},{48,112},{56,120},{... | collective-permute-start | bytes 958472 | tf_op jit(solution)/shard_map/ppermute | solution.py:101
  266.9 3.7 %collective-permute-done.44.refs_1_ = bf16[4,24,1664]{2,1,0:T(8,128)(2,1)S(1)} collective-permute-done((bf16[4,24,1664]{2,1,0:T(8,128)(2,1)S(1)}, bf16[4,24,1664]{2,1,0:T(8,128)(2,1)S(1)}, u32[]{:S(2)}, u32[]{:S(2)}) %collective-permute-start.44) | collective-permute-done | bytes 319520 | tf_op jit(solution)/shard_map/ppermute | solution.py:101
  270.6 3.7 %collective-permute-done.45.refs_2_ = bf16[4,24,1664]{2,1,0:T(8,128)(2,1)S(1)} collective-permute-done((bf16[4,24,1664]{2,1,0:T(8,128)(2,1)S(1)}, bf16[4,24,1664]{2,1,0:T(8,128)(2,1)S(1)}, u32[]{:S(2)}, u32[]{:S(2)}) %collective-permute-start.45) | collective-permute-done | bytes 319520 | tf_op jit(solution)/shard_map/ppermute | solution.py:101
  275.8 6.0 %shard_map.126 = (f32[3,192,1536]{2,1,0:T(8,128)}, f32[192,1536]{1,0:T(8,128)}, f32[48,128]{1,0:T(8,128)}) custom-call(s32[16]{0:T(128)} %add.181.pos_ref, bf16[4,24,1664]{2,1,0:T(8,128)(2,1)} %copy-done.3, bf16[4,24,1664]{2,1,0:T(8,128)(2,1)} %copy-done.23, bf16[4,24,1664]{2,1,0:T(8,128)(2,1)} %copy-done.24, bf16[4,24,1664]{2,1,0:T(8,128)(2,1)} %copy-done.25, ...), custom_call_target="tpu_custom_call" | custom-call | bytes 7299136 | tf_op jit(solution)/shard_map/pallas_call | solution.py:130
  (232 shorter events, 126.1 us)
Async XLA Ops:
  0.6 21.2 %collective-permute-start = (bf16[192,512]{1,0:T(8,128)(2,1)}, bf16[192,512]{1,0:T(8,128)(2,1)S(1)}, u32[]{:S(2)}, u32[]{:S(2)}) collective-permute-start(bf16[192,512]{1,0:T(8,128)(2,1)} %b0), channel_id=1, source_target_pairs={{0,2},{1,3},{2,4},{3,5},{4,6},{5,7},{6,0},{7,1},{8,10},{9,11},{10,... | collective-permute-start | bytes 589832 | tf_op jit(solution)/shard_map/ppermute | solution.py:118
  2.4 19.4 %collective-permute-start.1 = (bf16[192,512]{1,0:T(8,128)(2,1)}, bf16[192,512]{1,0:T(8,128)(2,1)S(1)}, u32[]{:S(2)}, u32[]{:S(2)}) collective-permute-start(bf16[192,512]{1,0:T(8,128)(2,1)} %b0), channel_id=1, source_target_pairs={{0,4},{1,5},{2,6},{3,7},{4,0},{5,1},{6,2},{7,3},{8,12},{9,13},{10,... | collective-permute-start | bytes 589832 | tf_op jit(solution)/shard_map/ppermute | solution.py:118
  5.3 16.6 %collective-permute-start.2 = (bf16[192,512]{1,0:T(8,128)(2,1)}, bf16[192,512]{1,0:T(8,128)(2,1)S(1)}, u32[]{:S(2)}, u32[]{:S(2)}) collective-permute-start(bf16[192,512]{1,0:T(8,128)(2,1)} %b0), channel_id=1, source_target_pairs={{0,6},{1,7},{2,0},{3,1},{4,2},{5,3},{6,4},{7,5},{8,14},{9,15},{10,... | collective-permute-start | bytes 589832 | tf_op jit(solution)/shard_map/ppermute | solution.py:118
  36.8 13.1 %collective-permute-start.9 = (bf16[768,512]{1,0:T(8,128)(2,1)S(1)}, bf16[768,512]{1,0:T(8,128)(2,1)S(1)}, u32[]{:S(2)}, u32[]{:S(2)}) collective-permute-start(bf16[768,512]{1,0:T(8,128)(2,1)S(1)} %pad_maximum_fusion.1), channel_id=1, source_target_pairs={{0,1},{1,0},{2,3},{3,2},{4,5},{5,4},{6,7},{7,6},{8,9},{9,8},{10,11... | collective-permute-start | bytes 2359304 | tf_op jit(solution)/shard_map/ppermute | solution.py:123
  38.5 21.8 %collective-permute-start.13 = (bf16[384,512]{1,0:T(8,128)(2,1)S(1)}, bf16[384,512]{1,0:T(8,128)(2,1)S(1)}, u32[]{:S(2)}, u32[]{:S(2)}) collective-permute-start(bf16[384,512]{1,0:T(8,128)(2,1)S(1)} %copy-done.46), channel_id=1, source_target_pairs={{0,32},{8,40},{16,48},{24,56},{32,64},{40,72},{48,80},{56,88},{64,... | collective-permute-start | bytes 1179656 | tf_op jit(solution)/shard_map/ppermute | solution.py:101
  40.4 21.4 %collective-permute-start.14 = (bf16[384,512]{1,0:T(8,128)(2,1)S(1)}, bf16[384,512]{1,0:T(8,128)(2,1)S(1)}, u32[]{:S(2)}, u32[]{:S(2)}) collective-permute-start(bf16[384,512]{1,0:T(8,128)(2,1)S(1)} %copy-done.46), channel_id=1, source_target_pairs={{0,64},{8,72},{16,80},{24,88},{32,96},{40,104},{48,112},{56,120},{... | collective-permute-start | bytes 1179656 | tf_op jit(solution)/shard_map/ppermute | solution.py:101
  44.0 17.8 %collective-permute-start.15 = (bf16[384,512]{1,0:T(8,128)(2,1)S(1)}, bf16[384,512]{1,0:T(8,128)(2,1)}, u32[]{:S(2)}, u32[]{:S(2)}) collective-permute-start(bf16[384,512]{1,0:T(8,128)(2,1)S(1)} %copy-done.46), channel_id=1, source_target_pairs={{0,96},{8,104},{16,112},{24,120},{32,0},{40,8},{48,16},{56,24},{64... | collective-permute-start | bytes 1179656 | tf_op jit(solution)/shard_map/ppermute | solution.py:101
  55.9 29.6 %collective-permute-start.16 = (bf16[192,512]{1,0:T(8,128)(2,1)}, bf16[192,512]{1,0:T(8,128)(2,1)S(1)}, u32[]{:S(2)}, u32[]{:S(2)}) collective-permute-start(bf16[192,512]{1,0:T(8,128)(2,1)} %get-tuple-element.94.refs_0_.refs_8_), channel_id=1, source_target_pairs={{0,8},{8,16},{16,24},{24,0},{32,40},{40,48},{48,56},{56,32},{64,72... | collective-permute-start | bytes 589832 | tf_op jit(solution)/shard_map/ppermute | solution.py:94
  58.9 26.7 %collective-permute-start.17 = (bf16[192,512]{1,0:T(8,128)(2,1)}, bf16[192,512]{1,0:T(8,128)(2,1)S(1)}, u32[]{:S(2)}, u32[]{:S(2)}) collective-permute-start(bf16[192,512]{1,0:T(8,128)(2,1)} %get-tuple-element.94.refs_0_.refs_8_), channel_id=1, source_target_pairs={{0,16},{8,24},{16,0},{24,8},{32,48},{40,56},{48,32},{56,40},{64,80... | collective-permute-start | bytes 589832 | tf_op jit(solution)/shard_map/ppermute | solution.py:94
  60.3 25.3 %collective-permute-start.18 = (bf16[192,512]{1,0:T(8,128)(2,1)}, bf16[192,512]{1,0:T(8,128)(2,1)S(1)}, u32[]{:S(2)}, u32[]{:S(2)}) collective-permute-start(bf16[192,512]{1,0:T(8,128)(2,1)} %get-tuple-element.94.refs_0_.refs_8_), channel_id=1, source_target_pairs={{0,24},{8,0},{16,8},{24,16},{32,56},{40,32},{48,40},{56,48},{64,88... | collective-permute-start | bytes 589832 | tf_op jit(solution)/shard_map/ppermute | solution.py:94
  103.5 16.8 %collective-permute-start.22 = (bf16[192,512]{1,0:T(8,128)(2,1)}, bf16[192,512]{1,0:T(8,128)(2,1)S(1)}, u32[]{:S(2)}, u32[]{:S(2)}) collective-permute-start(bf16[192,512]{1,0:T(8,128)(2,1)} %get-tuple-element.106), channel_id=1, source_target_pairs={{0,24},{8,0},{16,8},{24,16},{32,56},{40,32},{48,40},{56,48},{64,88... | collective-permute-start | bytes 589832 | tf_op jit(solution)/shard_map/ppermute | solution.py:94
  103.5 16.8 %collective-permute-start.23 = (bf16[192,512]{1,0:T(8,128)(2,1)}, bf16[192,512]{1,0:T(8,128)(2,1)S(1)}, u32[]{:S(2)}, u32[]{:S(2)}) collective-permute-start(bf16[192,512]{1,0:T(8,128)(2,1)} %get-tuple-element.107), channel_id=1, source_target_pairs={{0,16},{8,24},{16,0},{24,8},{32,48},{40,56},{48,32},{56,40},{64,80... | collective-permute-start | bytes 589832 | tf_op jit(solution)/shard_map/ppermute | solution.py:94
  105.3 15.0 %collective-permute-start.24 = (bf16[192,512]{1,0:T(8,128)(2,1)}, bf16[192,512]{1,0:T(8,128)(2,1)S(1)}, u32[]{:S(2)}, u32[]{:S(2)}) collective-permute-start(bf16[192,512]{1,0:T(8,128)(2,1)} %get-tuple-element.108), channel_id=1, source_target_pairs={{0,8},{8,16},{16,24},{24,0},{32,40},{40,48},{48,56},{56,32},{64,72... | collective-permute-start | bytes 589832 | tf_op jit(solution)/shard_map/ppermute | solution.py:94
  131.7 34.4 %collective-permute-start.26 = (bf16[192,512]{1,0:T(8,128)(2,1)}, bf16[192,512]{1,0:T(8,128)(2,1)S(1)}, u32[]{:S(2)}, u32[]{:S(2)}) collective-permute-start(bf16[192,512]{1,0:T(8,128)(2,1)} %get-tuple-element.112), channel_id=1, source_target_pairs={{0,2},{1,3},{2,4},{3,5},{4,6},{5,7},{6,0},{7,1},{8,10},{9,11},{10,... | collective-permute-start | bytes 589832 | tf_op jit(solution)/shard_map/ppermute | solution.py:118
  132.2 35.2 %collective-permute-start.27 = (bf16[192,512]{1,0:T(8,128)(2,1)}, bf16[192,512]{1,0:T(8,128)(2,1)S(1)}, u32[]{:S(2)}, u32[]{:S(2)}) collective-permute-start(bf16[192,512]{1,0:T(8,128)(2,1)} %get-tuple-element.113), channel_id=1, source_target_pairs={{0,4},{1,5},{2,6},{3,7},{4,0},{5,1},{6,2},{7,3},{8,12},{9,13},{10,... | collective-permute-start | bytes 589832 | tf_op jit(solution)/shard_map/ppermute | solution.py:118
  135.7 34.5 %collective-permute-start.28 = (bf16[192,512]{1,0:T(8,128)(2,1)}, bf16[192,512]{1,0:T(8,128)(2,1)S(1)}, u32[]{:S(2)}, u32[]{:S(2)}) collective-permute-start(bf16[192,512]{1,0:T(8,128)(2,1)} %get-tuple-element.114), channel_id=1, source_target_pairs={{0,6},{1,7},{2,0},{3,1},{4,2},{5,3},{6,4},{7,5},{8,14},{9,15},{10,... | collective-permute-start | bytes 589832 | tf_op jit(solution)/shard_map/ppermute | solution.py:118
  162.3 29.1 %collective-permute-start.33 = (bf16[384,512]{1,0:T(8,128)(2,1)}, bf16[384,512]{1,0:T(8,128)(2,1)S(1)}, u32[]{:S(2)}, u32[]{:S(2)}) collective-permute-start(bf16[384,512]{1,0:T(8,128)(2,1)} %get-tuple-element.129), channel_id=1, source_target_pairs={{0,96},{8,104},{16,112},{24,120},{32,0},{40,8},{48,16},{56,24},{64... | collective-permute-start | bytes 1179656 | tf_op jit(solution)/shard_map/ppermute | solution.py:101
  164.7 26.7 %collective-permute-start.34 = (bf16[384,512]{1,0:T(8,128)(2,1)}, bf16[384,512]{1,0:T(8,128)(2,1)S(1)}, u32[]{:S(2)}, u32[]{:S(2)}) collective-permute-start(bf16[384,512]{1,0:T(8,128)(2,1)} %get-tuple-element.130), channel_id=1, source_target_pairs={{0,64},{8,72},{16,80},{24,88},{32,96},{40,104},{48,112},{56,120},{... | collective-permute-start | bytes 1179656 | tf_op jit(solution)/shard_map/ppermute | solution.py:101
  166.1 25.3 %collective-permute-start.35 = (bf16[384,512]{1,0:T(8,128)(2,1)}, bf16[384,512]{1,0:T(8,128)(2,1)S(1)}, u32[]{:S(2)}, u32[]{:S(2)}) collective-permute-start(bf16[384,512]{1,0:T(8,128)(2,1)} %get-tuple-element.131), channel_id=1, source_target_pairs={{0,32},{8,40},{16,48},{24,56},{32,64},{40,72},{48,80},{56,88},{64,... | collective-permute-start | bytes 1179656 | tf_op jit(solution)/shard_map/ppermute | solution.py:101
  198.6 33.7 %all-to-all-start = ((bf16[16,48,1536]{2,1,0:T(8,128)(2,1)}), bf16[16,48,1536]{2,1,0:T(8,128)(2,1)S(1)}, u32[]{:S(2)}, u32[]{:S(2)}) async-start(bf16[16,48,1536]{2,1,0:T(8,128)(2,1)} %bitcast.15), calls=%async_computation | async-start | bytes 4718592 | tf_op jit(solution)/shard_map/all_to_all | solution.py:627
  213.8 13.3 %collective-permute-start.38 = (bf16[208,512]{1,0:T(8,128)(2,1)}, bf16[208,512]{1,0:T(8,128)(2,1)S(1)}, u32[]{:S(2)}, u32[]{:S(2)}) collective-permute-start(bf16[208,512]{1,0:T(8,128)(2,1)} %get-tuple-element.142), channel_id=1, source_target_pairs={{0,2},{1,3},{2,4},{3,5},{4,6},{5,7},{6,0},{7,1},{8,10},{9,11},{10,... | collective-permute-start | bytes 638984 | tf_op jit(solution)/shard_map/ppermute | solution.py:118
  244.8 21.1 %collective-permute-start.50 = (bf16[4,24,1664]{2,1,0:T(8,128)(2,1)S(1)}, bf16[4,24,1664]{2,1,0:T(8,128)(2,1)S(1)}, u32[]{:S(2)}, u32[]{:S(2)}) collective-permute-start(bf16[4,24,1664]{2,1,0:T(8,128)(2,1)S(1)} %pad_maximum_fusion.3.refs_4_), channel_id=1, source_target_pairs={{0,8},{8,16},{16,24},{24,0},{32,40},{40,48},{48,56},{56,32},{64,72... | collective-permute-start | bytes 958472 | tf_op jit(solution)/shard_map/ppermute | solution.py:94
  247.8 13.0 %collective-permute-start.42 = (bf16[24,1664]{1,0:T(8,128)(2,1)}, bf16[24,1664]{1,0:T(8,128)(2,1)S(1)}, u32[]{:S(2)}, u32[]{:S(2)}) collective-permute-start(bf16[24,1664]{1,0:T(8,128)(2,1)} %get-tuple-element.152), channel_id=1, source_target_pairs={{0,16},{8,24},{16,0},{24,8},{32,48},{40,56},{48,32},{56,40},{64,80... | collective-permute-start | bytes 239624 | tf_op jit(solution)/shard_map/ppermute | solution.py:94
  251.6 15.3 %collective-permute-start.51 = (bf16[4,24,1664]{2,1,0:T(8,128)(2,1)S(1)}, bf16[4,24,1664]{2,1,0:T(8,128)(2,1)S(1)}, u32[]{:S(2)}, u32[]{:S(2)}) collective-permute-start(bf16[4,24,1664]{2,1,0:T(8,128)(2,1)S(1)} %pad_maximum_fusion.3.refs_4_), channel_id=1, source_target_pairs={{0,16},{8,24},{16,0},{24,8},{32,48},{40,56},{48,32},{56,40},{64,80... | collective-permute-start | bytes 958472 | tf_op jit(solution)/shard_map/ppermute | solution.py:94
  (82 other events, 648.1 us)

commit v3 on v2

--- a/solution.py
+++ b/solution.py
@@ -109,7 +109,17 @@
     return left, right
 
 
-SM = pl.BlockSpec(memory_space=pltpu.SMEM)
+def place_mp(step, core_step):
+    index = lax.axis_index("mp")
+    y, core = lax.div(index, 2), lax.rem(index, 2)
+    core = 1 - core if core_step else core
+    return lax.rem(y + step + SIDE, SIDE) * 2 + core
+
+
+def place_tm(dz, dx):
+    index = lax.axis_index("tm")
+    z, x = lax.div(index, SIDE), lax.rem(index, SIDE)
+    return lax.rem(z - dz + SIDE, SIDE) * SIDE + lax.rem(x - dx + SIDE, SIDE)
 
 
 def shift_y(a, by):
@@ -145,7 +155,7 @@
     return slice(h * HEAD_DIM, (h + 1) * HEAD_DIM)
 
 
-def prep_body(pos_ref, w_ref, wo_ref, wq_out, wo_out, mixed, turned, turned_out):
+def prep_body(after_ref, w_ref, wo_ref, wq_out, wo_out, mixed, turned, turned_out):
     head_cols, width = wo_ref.shape
     heads = head_cols // HEAD_DIM
     for h in range(heads):
@@ -163,12 +173,13 @@
     lax.fori_loop(0, width // lanes, turn, 0)
     chunk = width // 8
     for r in range(8):
-        rows = pl.ds(pl.multiple_of(pos_ref[r] * chunk, chunk), chunk)
+        at = place_mp(r % SIDE, r // SIDE)
+        rows = pl.ds(pl.multiple_of(at * chunk, chunk), chunk)
         wq_out[r * chunk : (r + 1) * chunk, :] = turned[rows, :]
         wo_out[r * chunk : (r + 1) * chunk, :] = turned_out[rows, :]
 
 
-def norm_body(pos_ref, b0, b1, b2, b3, other, gain_ref, w_ref, normed_out, inv_out, q_out, kv_out):
+def norm_body(b0, b1, b2, b3, other, gain_ref, w_ref, normed_out, inv_out, q_out, kv_out, gain):
     own = [b0, b1, b2, b3]
     chunk, rows = b0.shape
     width = normed_out.shape[0]
@@ -177,6 +188,7 @@
         part = own[r][...] if r < 4 else other[(r - 4) * chunk : (r - 3) * chunk, :]
         return part.astype(F32)
 
+    gain[...] = jnp.broadcast_to(gain_ref[...], (8, width)).T
     total = jnp.zeros((1, rows), F32)
     for r in range(8):
         x = block(r)
@@ -184,20 +196,25 @@
     inverse = lax.rsqrt(total / width + 1e-06)
     inv_out[...] = inverse
     for r in range(8):
-        at = pl.ds(pl.multiple_of(pos_ref[r] * chunk, chunk), chunk)
-        normed_out[at, :] = (block(r) * inverse * gain_ref[at, :]).astype(BF16)
+        at = pl.ds(pl.multiple_of(place_mp(-(r % SIDE), r // SIDE) * chunk, chunk), chunk)
+        normed_out[at, :] = (block(r) * inverse * gain[at, :1]).astype(BF16)
     normed = normed_out[...]
     q_out[...] = nn(w_ref[0], normed).astype(BF16) * jnp.asarray(HEAD_DIM ** (-0.5), BF16)
     head_cols = q_out.shape[0]
-    for j in (1, 2):
-        kv_out[(j - 1) * head_cols : j * head_cols, :] = nn(w_ref[j], normed).astype(BF16)
-
-
-def back_arrange_body(pos_ref, b0, b1, b2, b3, other, wo_ref, full_out, grad_out):
+
+    def step(j, carry):
+        at = pl.ds(pl.multiple_of((j - 1) * head_cols, head_cols), head_cols)
+        kv_out[at, :] = nn(w_ref[j], normed_out[...]).astype(BF16)
+        return carry
+
+    lax.fori_loop(1, 3, step, 0)
+
+
+def back_arrange_body(b0, b1, b2, b3, other, wo_ref, full_out, grad_out):
     own = [b0, b1, b2, b3]
     chunk = b0.shape[0]
     for r in range(8):
-        at = pl.ds(pl.multiple_of(pos_ref[r] * chunk, chunk), chunk)
+        at = pl.ds(pl.multiple_of(place_mp(-(r % SIDE), r // SIDE) * chunk, chunk), chunk)
         full_out[at, :] = own[r][...] if r < 4 else other[(r - 4) * chunk : (r - 3) * chunk, :]
     grad_out[...] = nn(wo_ref[...], full_out[...]).astype(BF16)
 
@@ -352,7 +369,14 @@
 
 
 def out_weights_body(att_ref, full_ref, part_out):
-    part_out[...] = nt(att_ref[...], full_ref[...]).astype(BF16)
+    chunk = full_ref.shape[0] // SIDE
+
+    def step(d, carry):
+        cols = pl.ds(pl.multiple_of(d * chunk, chunk), chunk)
+        part_out[:, cols] = nt(att_ref[...], full_ref[cols, :]).astype(BF16)
+        return carry
+
+    lax.fori_loop(0, SIDE, step, 0)
 
 
 def pair_body(own_ref, got_ref, *outs):
@@ -436,7 +460,7 @@
 def reduce_body(in_ref, small_ref, first_out, second_out):
     members, rows, width = in_ref.shape
     half = rows // 2
-    lanes = 256
+    lanes = 128
 
     def step(i, carry):
         cols = pl.ds(pl.multiple_of(i * lanes, lanes), lanes)
@@ -450,42 +474,43 @@
     second_out[:, width:] = small_ref[half:, :]
 
 
-def finish_body(heads, pos_ref, *refs):
+def finish_body(heads, *refs):
     firsts, seconds = refs[:SIDE], refs[SIDE : 2 * SIDE]
-    qkv_out, proj_out, small_out, held = refs[2 * SIDE :]
+    qkv_out, proj_out, small_out = refs[2 * SIDE :]
     half = firsts[0].shape[1]
     each = 2 * half
     width = qkv_out.shape[2]
     step = 8
+    qkv_rows = 3 * heads * HEAD_DIM
+    qkv_members = qkv_rows // each
     small_out[...] = jnp.zeros_like(small_out)
+
+    def place(ref, e, m, start):
+        @pl.when(m < qkv_members)
+        def _():
+            for i in range(0, half, step):
+                row = m * each + (start + i)
+                block = lax.div(row, HEAD_DIM)
+                at = lax.div(block, 3) * HEAD_DIM + lax.rem(row, HEAD_DIM)
+                at = pl.ds(pl.multiple_of(at, step), step)
+                qkv_out[lax.rem(block, 3), at, :] = ref[e, i : i + step, :width].astype(F32)
+
+        @pl.when(m >= qkv_members)
+        def _():
+            for i in range(0, half, step):
+                at = pl.ds(pl.multiple_of(m * each + (start + i) - qkv_rows, step), step)
+                proj_out[at, :] = ref[e, i : i + step, :width].astype(F32)
+
     for d in range(SIDE):
 
-        def place(e, carry):
-            held[pos_ref[d * SIDE + e], :half, :] = firsts[d][e, :, :width].astype(F32)
-            held[pos_ref[e * SIDE + d], half:, :] = seconds[d][e, :, :width].astype(F32)
+        def spread(e, carry):
+            place(firsts[d], e, place_tm(d, e), 0)
+            place(seconds[d], e, place_tm(e, d), half)
             small_out[:half, :] += firsts[d][e, :, width:].astype(F32)
             small_out[half:, :] += seconds[d][e, :, width:].astype(F32)
             return carry
 
-        lax.fori_loop(0, SIDE, place, 0)
-
-    def rows_of(row):
-        return held[lax.div(row, each), pl.ds(pl.multiple_of(lax.rem(row, each), step), step), :]
-
-    def write_qkv(g, carry):
-        row = g * step
-        block = lax.div(row, HEAD_DIM)
-        at = lax.div(block, 3) * HEAD_DIM + lax.rem(row, HEAD_DIM)
-        qkv_out[lax.rem(block, 3), pl.ds(pl.multiple_of(at, step), step), :] = rows_of(row)
-        return carry
-
-    def write_proj(g, carry):
-        row = g * step
-        proj_out[pl.ds(pl.multiple_of(row, step), step), :] = rows_of(row + 3 * heads * HEAD_DIM)
-        return carry
-
-    lax.fori_loop(0, 3 * heads * HEAD_DIM // step, write_qkv, 0)
-    lax.fori_loop(0, heads * HEAD_DIM // step, write_proj, 0)
+        lax.fori_loop(0, SIDE, spread, 0)
 
 
 def tie(value, *others):
@@ -499,11 +524,6 @@
     members = lax.axis_size("tm")
     taps = conv_kernel.shape[0]
     span = SIDE * rows
-    y, core = lax.axis_index("mp") // 2, lax.axis_index("mp") % 2
-    steps = jnp.arange(SIDE, dtype=jnp.int32)
-    cores = jnp.stack([core, 1 - core]).astype(jnp.int32)
-    came = ((((y - steps + SIDE) % SIDE) * 2)[None, :] + cores[:, None]).reshape(-1)
-    goes = ((((y + steps) % SIDE) * 2)[None, :] + cores[:, None]).reshape(-1)
 
     def with_swap(blocks):
         return blocks + [swap_core(jnp.concatenate(blocks, axis=0))]
@@ -521,14 +541,12 @@
         ],
         flops=8 * own_width * rows * taps,
     )
-    in_blocks = list(lax.optimization_barrier((*in_blocks, back_cast)))
-    back_cast = in_blocks.pop()
     in_blocks = with_swap(in_blocks)
     back_blocks = ring(shift_y, [back_cast] * SIDE, 1)
     normed, inverse, queries, keys_values = call(
         norm_body,
         [((width, rows), BF16), ((1, rows), F32), ((head_cols, rows), BF16), ((2 * head_cols, rows), BF16)],
-        [came, *in_blocks, norm_gain[:, None], w_qkv], [SM] + [VM] * 7,
+        [*in_blocks, norm_gain[None], w_qkv], None, [pltpu.VMEM((width, 8), F32)],
         flops=2 * 3 * head_cols * width * rows,
     )
     group_kv = ring(shift_z, [keys_values] * SIDE, 1)
@@ -539,7 +557,7 @@
     back_full, grad_attn = call(
         back_arrange_body,
         [((width, rows), BF16), ((head_cols, rows), BF16)],
-        [came, *back_blocks, w_out], [SM] + [VM] * 6,
+        [*back_blocks, w_out],
         flops=2 * head_cols * width * rows,
     )
     group_g = ring(shift_x, [grad_attn] * SIDE, 1)
@@ -563,7 +581,7 @@
     wq_rel, wo_rel = call(
         prep_body,
         [((width, 3 * head_cols), BF16), ((width, head_cols), BF16)],
-        [tie(goes, stats), w_qkv, w_out], [SM, VM, VM],
+        [stats[:, :128], w_qkv, w_out], None,
         [
             pltpu.VMEM((3 * head_cols, width), BF16),
             pltpu.VMEM((width, 3 * head_cols), BF16),
@@ -668,13 +686,10 @@
     second_row = jnp.stack(ring(shift_z, [second] * SIDE, 1))
     first_all = ring(shift_z, [first_row] * SIDE, 1)
     second_all = ring(shift_x, [second_row] * SIDE, 1)
-    z, x = lax.axis_index("tm") // SIDE, lax.axis_index("tm") % SIDE
-    held_at = ((z - steps + SIDE) % SIDE * SIDE)[:, None] + ((x - steps + SIDE) % SIDE)[None, :]
     qkv_grads, out_grads, small_sum = call(
         functools.partial(finish_body, heads),
         [((3, head_cols, width), F32), ((head_cols, width), F32), ((each, small_cols), F32)],
-        [held_at.reshape(-1).astype(jnp.int32), *first_all, *second_all], [SM] + [VM] * 2 * SIDE,
-        [pltpu.VMEM((members, each, width), F32)],
+        [*first_all, *second_all],
     )
     small_sum = small_sum.reshape(taps + 1, own_width)
     return block_out, grad_frames, small_sum[taps], qkv_grads, out_grads, small_sum[:taps]

time: 286 us -> 292 us (1.021)
  waiting for transfers between devices: 49 us -> 54.5 us
    ppermute x12, waiting for transfers between devices: 4.51 us -> 10.9 us  [shift_y(): return lax.ppermute(a, 'mp', pairs)]
    unnamed x104 -> x108, local copies, waits for them, and re-layouts: 12.1 us -> 12.8 us
  transfers between devices with their start and end apart: 54 -> 54, of which waited for: 21 -> 23; matrix products, arithmetic and copies ran while one was open for 3% -> 2% of each run, Pallas kernels for 35% -> 34%
where the time goes in v3:
time: 292 us; the launch traced here: 290 us
  Pallas kernels  125 us (43%)
  starting transfers between devices  86.7 us (30%)
  waiting for transfers between devices  54.5 us (19%)
  local copies, waits for them, and re-layouts  16.8 us (6%)
  other arithmetic  6 us (2%)
    pallas_call x18, Pallas kernels, call(): pl.pallas_call(body, out_shape=out_shape, in_specs=specs or [VM] * len(ar...  125 us
    ppermute x21, starting transfers between devices, shift_x(): return lax.ppermute(a, 'tm', pairs)  35.4 us
    ppermute x12, starting transfers between devices, shift_z(): return lax.ppermute(a, 'tm', pairs)  20.1 us
    ppermute x12, starting transfers between devices, shift_y(): return lax.ppermute(a, 'mp', pairs)  20 us
    ppermute x21, waiting for transfers between devices, shift_x(): return lax.ppermute(a, 'tm', pairs)  18.6 us
    unnamed x108, local copies, waits for them, and re-layouts  12.8 us
    ppermute x12, waiting for transfers between devices, shift_z(): return lax.ppermute(a, 'tm', pairs)  12.5 us
    ppermute x12, waiting for transfers between devices, shift_y(): return lax.ppermute(a, 'mp', pairs)  10.9 us
  transfers between devices with their start and end apart: 54, of which 23 were waited for; matrix products, arithmetic and copies ran while one was open for 2% of the time, Pallas kernels for 34%

profile of v3, /device:TPU:0, one launch (start us, length us, event | category | flops | bytes accessed | tf_op | source)
XLA Modules:
  0.0 290.2 jit_solution(1438876447905591061)
XLA Ops:
  9.0 5.4 %collective-permute-done.1.b2 = bf16[192,512]{1,0:T(8,128)(2,1)S(1)} collective-permute-done((bf16[192,512]{1,0:T(8,128)(2,1)}, bf16[192,512]{1,0:T(8,128)(2,1)S(1)}, u32[]{:S(2)}, u32[]{:S(2)}) %collective-permute-start.1) | collective-permute-done | bytes 196640 | tf_op jit(solution)/shard_map/ppermute | solution.py:128
  15.6 3.4 %collective-permute-start.4 = (bf16[192,128]{1,0:T(8,128)(2,1)S(1)}, bf16[192,128]{1,0:T(8,128)(2,1)S(1)}, u32[]{:S(2)}, u32[]{:S(2)}) collective-permute-start(bf16[192,128]{1,0:T(8,128)(2,1)S(1)} %get-tuple-element.150), channel_id=1, source_target_pairs={{0,8},{8,16},{16,24},{24,32},{32,40},{40,48},{48,56},{56,64},{64,7... | collective-permute-start | bytes 147464 | tf_op jit(solution)/shard_map/ppermute | solution.py:107
  20.7 4.2 %collective-permute-done.5.right_ref = bf16[192,128]{1,0:T(8,128)(2,1)S(1)} collective-permute-done((bf16[192,128]{1,0:T(8,128)(2,1)S(1)}, bf16[192,128]{1,0:T(8,128)(2,1)S(1)}, u32[]{:S(2)}, u32[]{:S(2)}) %collective-permute-start.5) | collective-permute-done | bytes 49184 | tf_op jit(solution)/shard_map/ppermute | solution.py:108
  25.6 4.3 %shard_map.110 = (f32[192,512]{1,0:T(8,128)}, bf16[192,512]{1,0:T(8,128)(2,1)}) custom-call(bf16[192,128]{1,0:T(8,128)(2,1)} %copy-done.41, bf16[192,512]{1,0:T(8,128)(2,1)} %up_ref.1, bf16[192,128]{1,0:T(8,128)(2,1)} %copy-done.42, f32[31,192]{1,0:T(8,128)} %taps_ref.3), custom_call_target="tpu_custom_call" | custom-call | flops 24379392 | bytes 908544 | tf_op jit(solution)/shard_map/pallas_call | solution.py:140
  36.6 5.2 %shard_map.109 = (bf16[1536,512]{1,0:T(8,128)(2,1)}, f32[1,512]{1,0:T(1,128)}, bf16[192,512]{1,0:T(8,128)(2,1)}, bf16[384,512]{1,0:T(8,128)(2,1)}) custom-call(bf16[192,512]{1,0:T(8,128)(2,1)} %b0.1, bf16[192,512]{1,0:T(8,128)(2,1)} %copy-done.30, bf16[192,512]{1,0:T(8,128)(2,1)} %copy-done.31, bf16[192,512]{1,0:T(8,128)(2,1)} %copy-done.32, ...), custom_call_target="tpu_custom_call" | custom-call | flops 905969664 | bytes 5513216 | tf_op jit(solution)/shard_map/pallas_call | solution.py:140
  46.4 3.6 %collective-permute-start.14 = (bf16[384,512]{1,0:T(8,128)(2,1)S(1)}, bf16[384,512]{1,0:T(8,128)(2,1)S(1)}, u32[]{:S(2)}, u32[]{:S(2)}) collective-permute-start(bf16[384,512]{1,0:T(8,128)(2,1)S(1)} %copy-done.47), channel_id=1, source_target_pairs={{0,64},{8,72},{16,80},{24,88},{32,96},{40,104},{48,112},{56,120},{... | collective-permute-start | bytes 1179656 | tf_op jit(solution)/shard_map/ppermute | solution.py:101
  67.6 23.0 %shard_map.112 = (bf16[192,2048]{1,0:T(8,128)(2,1)}, f32[3,2048]{1,0:T(4,128)}) custom-call(bf16[192,512]{1,0:T(8,128)(2,1)} %get-tuple-element.84.refs_0_.q_ref, bf16[192,512]{1,0:T(8,128)(2,1)} %copy-done.51, bf16[192,512]{1,0:T(8,128)(2,1)} %copy-done.52, bf16[192,512]{1,0:T(8,128)(2,1)} %copy-done.53, bf16[384,512]{1,0:T(8,128)(2,1)} %get-tuple-element.78.refs_4_.kv_ref, ...), custom_call_target="tpu_custom_call" | custom-call | flops 12884901888 | bytes 3170304 | tf_op jit(solution)/shard_map/pallas_call | solution.py:140
  101.0 4.9 %shard_map.114 = (bf16[1536,576]{1,0:T(8,128)(2,1)}, bf16[1536,192]{1,0:T(8,128)(2,1)}) custom-call(f32[8,128]{1,0:T(8,128)} %slice.40.after_ref, bf16[3,192,1536]{2,1,0:T(8,128)(2,1)} %w_ref.3, bf16[192,1536]{1,0:T(8,128)(2,1)} %wo_ref.3), custom_call_target="tpu_custom_call" | custom-call | bytes 4722688 | tf_op jit(solution)/shard_map/pallas_call | solution.py:140
  111.5 14.7 %shard_map.116 = (bf16[64,512]{1,0:T(8,128)(2,1)}, bf16[64,512]{1,0:T(8,128)(2,1)}, bf16[64,512]{1,0:T(8,128)(2,1)}, bf16[64,512]{1,0:T(8,128)(2,1)}, bf16[128,5...) custom-call(bf16[192,512]{1,0:T(8,128)(2,1)} %get-tuple-element.84.refs_0_.q_ref, ...), custom_call_target="tpu_custom_call" | custom-call | flops 10737418240 | bytes 4063232 | tf_op jit(solution)/shard_map/pallas_call | solution.py:140
  127.7 4.1 %shard_map.117 = (bf16[192,512]{1,0:T(8,128)(2,1)}, f32[768,512]{1,0:T(8,128)}, bf16[768,512]{1,0:T(8,128)(2,1)}) custom-call(bf16[192,512]{1,0:T(8,128)(2,1)} %get-tuple-element.93.refs_0_, bf16[192,512]{1,0:T(8,128)(2,1)} %copy-done.33, bf16[192,512]{1,0:T(8,128)(2,1)} %copy-done.34, bf16[192,512]{1,0:T(8,128)(2,1)} %copy-done.35, ...), custom_call_target="tpu_custom_call" | custom-call | flops 301989888 | bytes 3932160 | tf_op jit(solution)/shard_map/pallas_call | solution.py:140
  142.9 26.5 %shard_map.119 = (bf16[192,512]{1,0:T(8,128)(2,1)}, bf16[192,512]{1,0:T(8,128)(2,1)}, bf16[192,512]{1,0:T(8,128)(2,1)}, bf16[192,512]{1,0:T(8,128)(2,1)}, bf16[3...) custom-call(bf16[192,512]{1,0:T(8,128)(2,1)} %get-tuple-element.84.refs_0_.q, ...), custom_call_target="tpu_custom_call" | custom-call | flops 21474836480 | bytes 6422528 | tf_op jit(solution)/shard_map/pallas_call | solution.py:140
  182.1 3.8 %collective-permute-start.31 = (bf16[192,512]{1,0:T(8,128)(2,1)}, bf16[192,512]{1,0:T(8,128)(2,1)S(1)}, u32[]{:S(2)}, u32[]{:S(2)}) collective-permute-start(bf16[192,512]{1,0:T(8,128)(2,1)} %get-tuple-element.114), channel_id=1, source_target_pairs={{0,16},{8,24},{16,0},{24,8},{32,48},{40,56},{48,32},{56,40},{64,80... | collective-permute-start | bytes 589832 | tf_op jit(solution)/shard_map/ppermute | solution.py:94
  189.1 3.6 %shard_map.120.refs_9_ = bf16[192,1536]{1,0:T(8,128)(2,1)} custom-call(bf16[192,512]{1,0:T(8,128)(2,1)} %get-tuple-element.122.att_ref, bf16[1536,512]{1,0:T(8,128)(2,1)} %get-tuple-element.123.full_ref), custom_call_target="tpu_custom_call" | custom-call | flops 301989888 | bytes 2359296 | tf_op jit(solution)/shard_map/pallas_call | solution.py:140
  192.7 5.8 %collective-permute-done.32.refs_3_ = bf16[192,512]{1,0:T(8,128)(2,1)S(1)} collective-permute-done((bf16[192,512]{1,0:T(8,128)(2,1)}, bf16[192,512]{1,0:T(8,128)(2,1)S(1)}, u32[]{:S(2)}, u32[]{:S(2)}) %collective-permute-start.32) | collective-permute-done | bytes 196640 | tf_op jit(solution)/shard_map/ppermute | solution.py:94
  199.6 6.1 %shard_map.121 = (bf16[576,512]{1,0:T(8,128)(2,1)}, bf16[768,1536]{1,0:T(8,128)(2,1)}) custom-call(bf16[192,512]{1,0:T(8,128)(2,1)} %get-tuple-element.111.refs_0_, bf16[192,512]{1,0:T(8,128)(2,1)} %copy-done.23, bf16[192,512]{1,0:T(8,128)(2,1)} %copy-done.24, bf16[192,512]{1,0:T(8,128)(2,1)} %copy-done.25, bf16[384,512]{1,0:T(8,128)(2,1)} %get-tuple-element.116.refs_4_, ...), custom_call_target="tpu_custom_call" | custom-call | flops 905969664 | bytes 7471104 | tf_op jit(solution)/shard_map/pallas_call | solution.py:140
  205.6 3.8 %all-to-all-start = ((bf16[16,48,1536]{2,1,0:T(8,128)(2,1)}), bf16[16,48,1536]{2,1,0:T(8,128)(2,1)S(1)}, u32[]{:S(2)}, u32[]{:S(2)}) async-start(bf16[16,48,1536]{2,1,0:T(8,128)(2,1)} %bitcast.13), calls=%async_computation | async-start | bytes 4718592 | tf_op jit(solution)/shard_map/all_to_all | solution.py:645
  209.4 5.4 %shard_map.122 = (f32[776,512]{1,0:T(8,128)}, bf16[784,512]{1,0:T(8,128)(2,1)}) custom-call(bf16[576,512]{1,0:T(8,128)(2,1)} %get-tuple-element.125.all_gp, bf16[192,512]{1,0:T(8,128)(2,1)} %get-tuple-element.84.refs_0_.q_ref, bf16[384,512]{1,0:T(8,128)(2,1)} %get-tuple-element.78.refs_4_.kv_ref, bf16[1536,576]{1,0:T(8,128)(2,1)} %get-tuple-element.126.wq_ref), custom_call_target="tpu_custom_call" | custom-call | flops 905969664 | bytes 5341184 | tf_op jit(solution)/shard_map/pallas_call | solution.py:140
  224.6 6.4 %shard_map.124 = (bf16[192,512]{1,0:T(8,128)(2,1)}, f32[31,192]{1,0:T(8,128)}) custom-call(bf16[192,128]{1,0:T(8,128)(2,1)} %copy-done.39, bf16[192,512]{1,0:T(8,128)(2,1)} %copy-done.4, bf16[192,128]{1,0:T(8,128)(2,1)} %copy-done.40, bf16[192,512]{1,0:T(8,128)(2,1)} %up_ref.1, f32[31,192]{1,0:T(8,128)} %taps_ref.3), custom_call_target="tpu_custom_call" | custom-call | flops 48758784 | bytes 735744 | tf_op jit(solution)/shard_map/pallas_call | solution.py:140
  247.9 3.8 %collective-permute-done.47 = bf16[24,1664]{1,0:T(8,128)(2,1)S(1)} collective-permute-done((bf16[24,1664]{1,0:T(8,128)(2,1)}, bf16[24,1664]{1,0:T(8,128)(2,1)S(1)}, u32[]{:S(2)}, u32[]{:S(2)}) %collective-permute-start.47) | collective-permute-done | bytes 79904 | tf_op jit(solution)/shard_map/ppermute | solution.py:101
  260.3 4.8 %collective-permute-done.41 = bf16[24,1664]{1,0:T(8,128)(2,1)S(1)} collective-permute-done((bf16[24,1664]{1,0:T(8,128)(2,1)}, bf16[24,1664]{1,0:T(8,128)(2,1)S(1)}, u32[]{:S(2)}, u32[]{:S(2)}) %collective-permute-start.41) | collective-permute-done | bytes 79904 | tf_op jit(solution)/shard_map/ppermute | solution.py:94
  269.9 3.6 %collective-permute-start.45 = (bf16[4,24,1664]{2,1,0:T(8,128)(2,1)S(1)}, bf16[4,24,1664]{2,1,0:T(8,128)(2,1)S(1)}, u32[]{:S(2)}, u32[]{:S(2)}) collective-permute-start(bf16[4,24,1664]{2,1,0:T(8,128)(2,1)S(1)} %pad_maximum_fusion.2.refs_0_), channel_id=1, source_target_pairs={{0,64},{8,72},{16,80},{24,88},{32,96},{40,104},{48,112},{56,120},{... | collective-permute-start | bytes 958472 | tf_op jit(solution)/shard_map/ppermute | solution.py:101
  274.1 3.8 %collective-permute-done.44.refs_1_ = bf16[4,24,1664]{2,1,0:T(8,128)(2,1)S(1)} collective-permute-done((bf16[4,24,1664]{2,1,0:T(8,128)(2,1)S(1)}, bf16[4,24,1664]{2,1,0:T(8,128)(2,1)S(1)}, u32[]{:S(2)}, u32[]{:S(2)}) %collective-permute-start.44) | collective-permute-done | bytes 319520 | tf_op jit(solution)/shard_map/ppermute | solution.py:101
  277.9 4.0 %collective-permute-done.45.refs_2_ = bf16[4,24,1664]{2,1,0:T(8,128)(2,1)S(1)} collective-permute-done((bf16[4,24,1664]{2,1,0:T(8,128)(2,1)S(1)}, bf16[4,24,1664]{2,1,0:T(8,128)(2,1)S(1)}, u32[]{:S(2)}, u32[]{:S(2)}) %collective-permute-start.45) | collective-permute-done | bytes 319520 | tf_op jit(solution)/shard_map/ppermute | solution.py:101
  283.4 5.3 %shard_map.126 = (f32[3,192,1536]{2,1,0:T(8,128)}, f32[192,1536]{1,0:T(8,128)}, f32[48,128]{1,0:T(8,128)}) custom-call(bf16[4,24,1664]{2,1,0:T(8,128)(2,1)} %copy-done.3, bf16[4,24,1664]{2,1,0:T(8,128)(2,1)} %copy-done.20, bf16[4,24,1664]{2,1,0:T(8,128)(2,1)} %copy-done.21, bf16[4,24,1664]{2,1,0:T(8,128)(2,1)} %copy-done.22, bf16[4,24,1664]{2,1,0:T(8,128)(2,1)} %copy-done.2, ...), custom_call_target="tpu_custom_call" | custom-call | bytes 7299072 | tf_op jit(solution)/shard_map/pallas_call | solution.py:140
  (229 shorter events, 129.3 us)
Async XLA Ops:
  15.5 20.2 %collective-permute-start.3 = (bf16[768,512]{1,0:T(8,128)(2,1)S(1)}, bf16[768,512]{1,0:T(8,128)(2,1)S(1)}, u32[]{:S(2)}, u32[]{:S(2)}) collective-permute-start(bf16[768,512]{1,0:T(8,128)(2,1)S(1)} %pad_maximum_fusion), channel_id=1, source_target_pairs={{0,1},{1,0},{2,3},{3,2},{4,5},{5,4},{6,7},{7,6},{8,9},{9,8},{10,11... | collective-permute-start | bytes 2359304 | tf_op jit(solution)/shard_map/ppermute | solution.py:133
  42.1 13.7 %collective-permute-start.9 = (bf16[768,512]{1,0:T(8,128)(2,1)S(1)}, bf16[768,512]{1,0:T(8,128)(2,1)S(1)}, u32[]{:S(2)}, u32[]{:S(2)}) collective-permute-start(bf16[768,512]{1,0:T(8,128)(2,1)S(1)} %pad_maximum_fusion.1), channel_id=1, source_target_pairs={{0,1},{1,0},{2,3},{3,2},{4,5},{5,4},{6,7},{7,6},{8,9},{9,8},{10,11... | collective-permute-start | bytes 2359304 | tf_op jit(solution)/shard_map/ppermute | solution.py:133
  44.4 21.0 %collective-permute-start.13 = (bf16[384,512]{1,0:T(8,128)(2,1)S(1)}, bf16[384,512]{1,0:T(8,128)(2,1)S(1)}, u32[]{:S(2)}, u32[]{:S(2)}) collective-permute-start(bf16[384,512]{1,0:T(8,128)(2,1)S(1)} %copy-done.47), channel_id=1, source_target_pairs={{0,32},{8,40},{16,48},{24,56},{32,64},{40,72},{48,80},{56,88},{64,... | collective-permute-start | bytes 1179656 | tf_op jit(solution)/shard_map/ppermute | solution.py:101
  46.4 20.5 %collective-permute-start.14 = (bf16[384,512]{1,0:T(8,128)(2,1)S(1)}, bf16[384,512]{1,0:T(8,128)(2,1)S(1)}, u32[]{:S(2)}, u32[]{:S(2)}) collective-permute-start(bf16[384,512]{1,0:T(8,128)(2,1)S(1)} %copy-done.47), channel_id=1, source_target_pairs={{0,64},{8,72},{16,80},{24,88},{32,96},{40,104},{48,112},{56,120},{... | collective-permute-start | bytes 1179656 | tf_op jit(solution)/shard_map/ppermute | solution.py:101
  49.9 16.9 %collective-permute-start.15 = (bf16[384,512]{1,0:T(8,128)(2,1)S(1)}, bf16[384,512]{1,0:T(8,128)(2,1)}, u32[]{:S(2)}, u32[]{:S(2)}) collective-permute-start(bf16[384,512]{1,0:T(8,128)(2,1)S(1)} %copy-done.47), channel_id=1, source_target_pairs={{0,96},{8,104},{16,112},{24,120},{32,0},{40,8},{48,16},{56,24},{64... | collective-permute-start | bytes 1179656 | tf_op jit(solution)/shard_map/ppermute | solution.py:101
  60.4 30.1 %collective-permute-start.16 = (bf16[192,512]{1,0:T(8,128)(2,1)}, bf16[192,512]{1,0:T(8,128)(2,1)S(1)}, u32[]{:S(2)}, u32[]{:S(2)}) collective-permute-start(bf16[192,512]{1,0:T(8,128)(2,1)} %get-tuple-element.83.refs_0_.refs_8_), channel_id=1, source_target_pairs={{0,8},{8,16},{16,24},{24,0},{32,40},{40,48},{48,56},{56,32},{64,72... | collective-permute-start | bytes 589832 | tf_op jit(solution)/shard_map/ppermute | solution.py:94
  63.4 27.1 %collective-permute-start.17 = (bf16[192,512]{1,0:T(8,128)(2,1)}, bf16[192,512]{1,0:T(8,128)(2,1)S(1)}, u32[]{:S(2)}, u32[]{:S(2)}) collective-permute-start(bf16[192,512]{1,0:T(8,128)(2,1)} %get-tuple-element.83.refs_0_.refs_8_), channel_id=1, source_target_pairs={{0,16},{8,24},{16,0},{24,8},{32,48},{40,56},{48,32},{56,40},{64,80... | collective-permute-start | bytes 589832 | tf_op jit(solution)/shard_map/ppermute | solution.py:94
  65.5 25.1 %collective-permute-start.18 = (bf16[192,512]{1,0:T(8,128)(2,1)}, bf16[192,512]{1,0:T(8,128)(2,1)S(1)}, u32[]{:S(2)}, u32[]{:S(2)}) collective-permute-start(bf16[192,512]{1,0:T(8,128)(2,1)} %get-tuple-element.83.refs_0_.refs_8_), channel_id=1, source_target_pairs={{0,24},{8,0},{16,8},{24,16},{32,56},{40,32},{48,40},{56,48},{64,88... | collective-permute-start | bytes 589832 | tf_op jit(solution)/shard_map/ppermute | solution.py:94
  93.5 12.4 %collective-permute-start.19 = (f32[8,2048]{1,0:T(8,128)}, f32[8,2048]{1,0:T(8,128)S(1)}, u32[]{:S(2)}, u32[]{:S(2)}) collective-permute-start(f32[8,2048]{1,0:T(8,128)} %shard_map.113.refs_0_), channel_id=1, source_target_pairs={{0,8},{8,16},{16,24},{24,0},{32,40},{40,48},{48,56},{56,32},{64,72... | collective-permute-start | bytes 196616 | tf_op jit(solution)/shard_map/ppermute | solution.py:94
  109.5 16.8 %collective-permute-start.22 = (bf16[192,512]{1,0:T(8,128)(2,1)}, bf16[192,512]{1,0:T(8,128)(2,1)S(1)}, u32[]{:S(2)}, u32[]{:S(2)}) collective-permute-start(bf16[192,512]{1,0:T(8,128)(2,1)} %get-tuple-element.94), channel_id=1, source_target_pairs={{0,24},{8,0},{16,8},{24,16},{32,56},{40,32},{48,40},{56,48},{64,88... | collective-permute-start | bytes 589832 | tf_op jit(solution)/shard_map/ppermute | solution.py:94
  109.5 16.7 %collective-permute-start.23 = (bf16[192,512]{1,0:T(8,128)(2,1)}, bf16[192,512]{1,0:T(8,128)(2,1)S(1)}, u32[]{:S(2)}, u32[]{:S(2)}) collective-permute-start(bf16[192,512]{1,0:T(8,128)(2,1)} %get-tuple-element.95), channel_id=1, source_target_pairs={{0,16},{8,24},{16,0},{24,8},{32,48},{40,56},{48,32},{56,40},{64,80... | collective-permute-start | bytes 589832 | tf_op jit(solution)/shard_map/ppermute | solution.py:94
  111.3 15.0 %collective-permute-start.24 = (bf16[192,512]{1,0:T(8,128)(2,1)}, bf16[192,512]{1,0:T(8,128)(2,1)S(1)}, u32[]{:S(2)}, u32[]{:S(2)}) collective-permute-start(bf16[192,512]{1,0:T(8,128)(2,1)} %get-tuple-element.96), channel_id=1, source_target_pairs={{0,8},{8,16},{16,24},{24,0},{32,40},{40,48},{48,56},{56,32},{64,72... | collective-permute-start | bytes 589832 | tf_op jit(solution)/shard_map/ppermute | solution.py:94
  137.7 35.7 %collective-permute-start.26 = (bf16[192,512]{1,0:T(8,128)(2,1)}, bf16[192,512]{1,0:T(8,128)(2,1)S(1)}, u32[]{:S(2)}, u32[]{:S(2)}) collective-permute-start(bf16[192,512]{1,0:T(8,128)(2,1)} %get-tuple-element.100), channel_id=1, source_target_pairs={{0,2},{1,3},{2,4},{3,5},{4,6},{5,7},{6,0},{7,1},{8,10},{9,11},{10,... | collective-permute-start | bytes 589832 | tf_op jit(solution)/shard_map/ppermute | solution.py:128
  139.5 35.0 %collective-permute-start.27 = (bf16[192,512]{1,0:T(8,128)(2,1)}, bf16[192,512]{1,0:T(8,128)(2,1)S(1)}, u32[]{:S(2)}, u32[]{:S(2)}) collective-permute-start(bf16[192,512]{1,0:T(8,128)(2,1)} %get-tuple-element.101), channel_id=1, source_target_pairs={{0,4},{1,5},{2,6},{3,7},{4,0},{5,1},{6,2},{7,3},{8,12},{9,13},{10,... | collective-permute-start | bytes 589832 | tf_op jit(solution)/shard_map/ppermute | solution.py:128
  141.8 35.5 %collective-permute-start.28 = (bf16[192,512]{1,0:T(8,128)(2,1)}, bf16[192,512]{1,0:T(8,128)(2,1)S(1)}, u32[]{:S(2)}, u32[]{:S(2)}) collective-permute-start(bf16[192,512]{1,0:T(8,128)(2,1)} %get-tuple-element.102), channel_id=1, source_target_pairs={{0,6},{1,7},{2,0},{3,1},{4,2},{5,3},{6,4},{7,5},{8,14},{9,15},{10,... | collective-permute-start | bytes 589832 | tf_op jit(solution)/shard_map/ppermute | solution.py:128
  169.4 29.1 %collective-permute-start.33 = (bf16[384,512]{1,0:T(8,128)(2,1)}, bf16[384,512]{1,0:T(8,128)(2,1)S(1)}, u32[]{:S(2)}, u32[]{:S(2)}) collective-permute-start(bf16[384,512]{1,0:T(8,128)(2,1)} %get-tuple-element.117), channel_id=1, source_target_pairs={{0,96},{8,104},{16,112},{24,120},{32,0},{40,8},{48,16},{56,24},{64... | collective-permute-start | bytes 1179656 | tf_op jit(solution)/shard_map/ppermute | solution.py:101
  172.1 26.4 %collective-permute-start.34 = (bf16[384,512]{1,0:T(8,128)(2,1)}, bf16[384,512]{1,0:T(8,128)(2,1)S(1)}, u32[]{:S(2)}, u32[]{:S(2)}) collective-permute-start(bf16[384,512]{1,0:T(8,128)(2,1)} %get-tuple-element.118), channel_id=1, source_target_pairs={{0,64},{8,72},{16,80},{24,88},{32,96},{40,104},{48,112},{56,120},{... | collective-permute-start | bytes 1179656 | tf_op jit(solution)/shard_map/ppermute | solution.py:101
  173.4 25.1 %collective-permute-start.35 = (bf16[384,512]{1,0:T(8,128)(2,1)}, bf16[384,512]{1,0:T(8,128)(2,1)S(1)}, u32[]{:S(2)}, u32[]{:S(2)}) collective-permute-start(bf16[384,512]{1,0:T(8,128)(2,1)} %get-tuple-element.119), channel_id=1, source_target_pairs={{0,32},{8,40},{16,48},{24,56},{32,64},{40,72},{48,80},{56,88},{64,... | collective-permute-start | bytes 1179656 | tf_op jit(solution)/shard_map/ppermute | solution.py:101
  205.6 33.4 %all-to-all-start = ((bf16[16,48,1536]{2,1,0:T(8,128)(2,1)}), bf16[16,48,1536]{2,1,0:T(8,128)(2,1)S(1)}, u32[]{:S(2)}, u32[]{:S(2)}) async-start(bf16[16,48,1536]{2,1,0:T(8,128)(2,1)} %bitcast.13), calls=%async_computation | async-start | bytes 4718592 | tf_op jit(solution)/shard_map/all_to_all | solution.py:645
  220.8 13.3 %collective-permute-start.38 = (bf16[208,512]{1,0:T(8,128)(2,1)}, bf16[208,512]{1,0:T(8,128)(2,1)S(1)}, u32[]{:S(2)}, u32[]{:S(2)}) collective-permute-start(bf16[208,512]{1,0:T(8,128)(2,1)} %get-tuple-element.130), channel_id=1, source_target_pairs={{0,2},{1,3},{2,4},{3,5},{4,6},{5,7},{6,0},{7,1},{8,10},{9,11},{10,... | collective-permute-start | bytes 638984 | tf_op jit(solution)/shard_map/ppermute | solution.py:128
  221.8 12.3 %collective-permute-start.39 = (bf16[208,512]{1,0:T(8,128)(2,1)}, bf16[208,512]{1,0:T(8,128)(2,1)S(1)}, u32[]{:S(2)}, u32[]{:S(2)}) collective-permute-start(bf16[208,512]{1,0:T(8,128)(2,1)} %get-tuple-element.131), channel_id=1, source_target_pairs={{0,4},{1,5},{2,6},{3,7},{4,0},{5,1},{6,2},{7,3},{8,12},{9,13},{10,... | collective-permute-start | bytes 638984 | tf_op jit(solution)/shard_map/ppermute | solution.py:128
  252.7 20.9 %collective-permute-start.50 = (bf16[4,24,1664]{2,1,0:T(8,128)(2,1)S(1)}, bf16[4,24,1664]{2,1,0:T(8,128)(2,1)S(1)}, u32[]{:S(2)}, u32[]{:S(2)}) collective-permute-start(bf16[4,24,1664]{2,1,0:T(8,128)(2,1)S(1)} %pad_maximum_fusion.3.refs_4_), channel_id=1, source_target_pairs={{0,8},{8,16},{16,24},{24,0},{32,40},{40,48},{48,56},{56,32},{64,72... | collective-permute-start | bytes 958472 | tf_op jit(solution)/shard_map/ppermute | solution.py:94
  255.6 13.0 %collective-permute-start.42 = (bf16[24,1664]{1,0:T(8,128)(2,1)}, bf16[24,1664]{1,0:T(8,128)(2,1)S(1)}, u32[]{:S(2)}, u32[]{:S(2)}) collective-permute-start(bf16[24,1664]{1,0:T(8,128)(2,1)} %get-tuple-element.140), channel_id=1, source_target_pairs={{0,16},{8,24},{16,0},{24,8},{32,48},{40,56},{48,32},{56,40},{64,80... | collective-permute-start | bytes 239624 | tf_op jit(solution)/shard_map/ppermute | solution.py:94
  259.5 14.6 %collective-permute-start.51 = (bf16[4,24,1664]{2,1,0:T(8,128)(2,1)S(1)}, bf16[4,24,1664]{2,1,0:T(8,128)(2,1)S(1)}, u32[]{:S(2)}, u32[]{:S(2)}) collective-permute-start(bf16[4,24,1664]{2,1,0:T(8,128)(2,1)S(1)} %pad_maximum_fusion.3.refs_4_), channel_id=1, source_target_pairs={{0,16},{8,24},{16,0},{24,8},{32,48},{40,56},{48,32},{56,40},{64,80... | collective-permute-start | bytes 958472 | tf_op jit(solution)/shard_map/ppermute | solution.py:94
  (84 other events, 733.7 us)

commit v4 on v3

--- a/solution.py
+++ b/solution.py
@@ -133,7 +133,7 @@
     return lax.ppermute(a, "mp", [(i, i ^ 1) for i in range(count)])
 
 
-def call(body, outs, args, specs=None, scratch=(), flops=0, exps=0):
+def call(body, outs, args, specs=None, scratch=(), flops=0, exps=0, limit=20):
     out_shape = tuple(jax.ShapeDtypeStruct(s, t) for s, t in outs)
     moved = sum(a.size * a.dtype.itemsize for a in args)
     moved += sum(o.size * o.dtype.itemsize for o in out_shape)
@@ -143,6 +143,7 @@
         in_specs=specs or [VM] * len(args),
         out_specs=[VM] * len(outs),
         scratch_shapes=list(scratch),
+        compiler_params=pltpu.CompilerParams(vmem_limit_bytes=limit * 2**20),
         cost_estimate=pl.CostEstimate(flops=flops, bytes_accessed=moved, transcendentals=exps),
     )(*args)
 
@@ -541,6 +542,8 @@
         ],
         flops=8 * own_width * rows * taps,
     )
+    in_blocks = list(lax.optimization_barrier((*in_blocks, back_cast)))
+    back_cast = in_blocks.pop()
     in_blocks = with_swap(in_blocks)
     back_blocks = ring(shift_y, [back_cast] * SIDE, 1)
     normed, inverse, queries, keys_values = call(
@@ -571,7 +574,7 @@
             pltpu.VMEM((head_cols, span), BF16),
             pltpu.VMEM((head_cols, span), BF16),
         ],
-        flops=16 * head_cols * span * span, exps=heads * span * span,
+        flops=16 * head_cols * span * span, exps=heads * span * span, limit=40,
     )
     (stats,) = call(
         functools.partial(stats_body, heads),
@@ -608,7 +611,7 @@
             + [pltpu.VMEM((size, span), BF16)] * 3
             + [pltpu.VMEM((8, span), F32)]
             + [pltpu.VMEM((size, span), F32)] * 3,
-            flops=40 * size * span * span, exps=count * span * span,
+            flops=40 * size * span * span, exps=count * span * span, limit=40,
         )
 
     early = head_grads(0, 1, logsum, ())

time: 292 us -> 253 us (0.87)
  Pallas kernels: 125 us -> 80.3 us
  waiting for transfers between devices: 54.5 us -> 71.7 us
  local copies, waits for them, and re-layouts: 16.8 us -> 12.3 us
  starting transfers between devices: 86.7 us -> 82.5 us
    pallas_call x18, Pallas kernels: 125 us -> 80.3 us  [call(): pl.pallas_call(body, out_shape=out_shape, in_specs=specs or [VM] * len(ar...]
    ppermute x21, waiting for transfers between devices: 18.6 us -> 33.5 us  [shift_x(): return lax.ppermute(a, 'tm', pairs)]
    all_to_all x1, waiting for transfers between devices: 1.41 us -> 9.12 us  [shards(): lax.all_to_all(part.reshape(members, each, width), 'tm', 0, 0, tiled=True)]
    ppermute x21, starting transfers between devices: 35.4 us -> 32.5 us  [shift_x(): return lax.ppermute(a, 'tm', pairs)]
    unnamed x108 -> x44, local copies, waits for them, and re-layouts: 12.8 us -> 9.95 us
  transfers between devices with their start and end apart: 54 -> 54, of which waited for: 23 -> 21; matrix products, arithmetic and copies ran while one was open for 2% -> 2% of each run, Pallas kernels for 34% -> 29%
where the time goes in v4:
time: 253 us; the launch traced here: 251 us
  starting transfers between devices  82.5 us (33%)
  Pallas kernels  80.3 us (32%)
  waiting for transfers between devices  71.7 us (28%)
  local copies, waits for them, and re-layouts  12.3 us (5%)
  other arithmetic  3.43 us (1%)
    pallas_call x18, Pallas kernels, call(): pl.pallas_call(body, out_shape=out_shape, in_specs=specs or [VM] * len(ar...  80.3 us
    ppermute x21, waiting for transfers between devices, shift_x(): return lax.ppermute(a, 'tm', pairs)  33.5 us
    ppermute x21, starting transfers between devices, shift_x(): return lax.ppermute(a, 'tm', pairs)  32.5 us
    ppermute x12, starting transfers between devices, shift_z(): return lax.ppermute(a, 'tm', pairs)  19.4 us
    ppermute x12, starting transfers between devices, shift_y(): return lax.ppermute(a, 'mp', pairs)  18.4 us
    ppermute x12, waiting for transfers between devices, shift_z(): return lax.ppermute(a, 'tm', pairs)  11 us
    unnamed x44, local copies, waits for them, and re-layouts  9.95 us
    all_to_all x1, waiting for transfers between devices, shards(): lax.all_to_all(part.reshape(members, each, width), 'tm', 0, 0, tiled=True)  9.12 us
  transfers between devices with their start and end apart: 54, of which 21 were waited for; matrix products, arithmetic and copies ran while one was open for 2% of the time, Pallas kernels for 29%

profile of v4, /device:TPU:0, one launch (start us, length us, event | category | flops | bytes accessed | tf_op | source)
XLA Modules:
  0.0 251.4 jit_solution(10743068313336587855)
XLA Ops:
  2.4 2.9 %collective-permute-start.1 = (bf16[192,512]{1,0:T(8,128)(2,1)}, bf16[192,512]{1,0:T(8,128)(2,1)S(1)}, u32[]{:S(2)}, u32[]{:S(2)}) collective-permute-start(bf16[192,512]{1,0:T(8,128)(2,1)} %b0), channel_id=1, source_target_pairs={{0,4},{1,5},{2,6},{3,7},{4,0},{5,1},{6,2},{7,3},{8,12},{9,13},{10,... | collective-permute-start | bytes 589832 | tf_op jit(solution)/shard_map/ppermute | solution.py:128
  7.5 3.4 %collective-permute-start.3 = (bf16[192,128]{1,0:T(8,128)(2,1)S(1)}, bf16[192,128]{1,0:T(8,128)(2,1)S(1)}, u32[]{:S(2)}, u32[]{:S(2)}) collective-permute-start(bf16[192,128]{1,0:T(8,128)(2,1)S(1)} %get-tuple-element.160), channel_id=1, source_target_pairs={{0,8},{8,16},{16,24},{24,32},{32,40},{40,48},{48,56},{56,64},{64,7... | collective-permute-start | bytes 147464 | tf_op jit(solution)/shard_map/ppermute | solution.py:107
  12.6 4.3 %collective-permute-done.4.right_ref = bf16[192,128]{1,0:T(8,128)(2,1)S(1)} collective-permute-done((bf16[192,128]{1,0:T(8,128)(2,1)S(1)}, bf16[192,128]{1,0:T(8,128)(2,1)S(1)}, u32[]{:S(2)}, u32[]{:S(2)}) %collective-permute-start.4) | collective-permute-done | bytes 49184 | tf_op jit(solution)/shard_map/ppermute | solution.py:108
  28.0 7.0 %collective-permute-done.6.b1 = bf16[192,512]{1,0:T(8,128)(2,1)S(1)} collective-permute-done((bf16[192,512]{1,0:T(8,128)(2,1)S(1)}, bf16[192,512]{1,0:T(8,128)(2,1)S(1)}, u32[]{:S(2)}, u32[]{:S(2)}) %collective-permute-start.6) | collective-permute-done | bytes 196640 | tf_op jit(solution)/shard_map/ppermute | solution.py:128
  39.2 3.6 %collective-permute-start.14 = (bf16[384,512]{1,0:T(8,128)(2,1)S(1)}, bf16[384,512]{1,0:T(8,128)(2,1)S(1)}, u32[]{:S(2)}, u32[]{:S(2)}) collective-permute-start(bf16[384,512]{1,0:T(8,128)(2,1)S(1)} %get-tuple-element.88.refs_4_.kv_ref), channel_id=1, source_target_pairs={{0,64},{8,72},{16,80},{24,88},{32,96},{40,104},{48,112},{56,120},{... | collective-permute-start | bytes 1179656 | tf_op jit(solution)/shard_map/ppermute | solution.py:101
  43.8 2.7 %collective-permute-done.10.refs_1_ = bf16[192,512]{1,0:T(8,128)(2,1)S(1)} collective-permute-done((bf16[192,512]{1,0:T(8,128)(2,1)S(1)}, bf16[192,512]{1,0:T(8,128)(2,1)S(1)}, u32[]{:S(2)}, u32[]{:S(2)}) %collective-permute-start.10) | collective-permute-done | bytes 196640 | tf_op jit(solution)/shard_map/ppermute | solution.py:94
  49.3 5.3 %collective-permute-done.11.refs_2_ = bf16[192,512]{1,0:T(8,128)(2,1)S(1)} collective-permute-done((bf16[192,512]{1,0:T(8,128)(2,1)S(1)}, bf16[192,512]{1,0:T(8,128)(2,1)S(1)}, u32[]{:S(2)}, u32[]{:S(2)}) %collective-permute-start.11) | collective-permute-done | bytes 196640 | tf_op jit(solution)/shard_map/ppermute | solution.py:94
  54.9 2.8 %collective-permute-done.12.refs_3_ = bf16[192,512]{1,0:T(8,128)(2,1)S(1)} collective-permute-done((bf16[192,512]{1,0:T(8,128)(2,1)S(1)}, bf16[192,512]{1,0:T(8,128)(2,1)S(1)}, u32[]{:S(2)}, u32[]{:S(2)}) %collective-permute-start.12) | collective-permute-done | bytes 196640 | tf_op jit(solution)/shard_map/ppermute | solution.py:94
  60.7 20.4 %shard_map.112 = (bf16[192,2048]{1,0:T(8,128)(2,1)S(1)}, f32[3,2048]{1,0:T(4,128)S(1)}) custom-call(bf16[192,512]{1,0:T(8,128)(2,1)S(1)} %get-tuple-element.94.refs_0_.q_ref, bf16[192,512]{1,0:T(8,128)(2,1)S(1)} %collective-permute-done.10.refs_1_, bf16[192,512]{1,0:T(8,128)(2,1)S(1)} %collective-permute-done.11.refs_2_, ...), custom_call_target="tpu_custom_call" | custom-call | flops 12884901888 | bytes 3170304 | tf_op jit(solution)/shard_map/pallas_call | solution.py:140
  89.4 3.6 %collective-permute-start.22 = (bf16[192,512]{1,0:T(8,128)(2,1)S(1)}, bf16[192,512]{1,0:T(8,128)(2,1)S(1)}, u32[]{:S(2)}, u32[]{:S(2)}) collective-permute-start(bf16[192,512]{1,0:T(8,128)(2,1)S(1)} %get-tuple-element.104), channel_id=1, source_target_pairs={{0,24},{8,0},{16,8},{24,16},{32,56},{40,32},{48,40},{56,48},{64,88... | collective-permute-start | bytes 589832 | tf_op jit(solution)/shard_map/ppermute | solution.py:94
  94.0 12.0 %shard_map.116 = (bf16[64,512]{1,0:T(8,128)(2,1)S(1)}, bf16[64,512]{1,0:T(8,128)(2,1)S(1)}, bf16[64,512]{1,0:T(8,128)(2,1)S(1)}, bf16[64,512]{1,0:T(8,128)(2,1)S...) custom-call(bf16[192,512]{1,0:T(8,128)(2,1)S(1)} %get-tuple-element., ...), custom_call_target="tpu_custom_call" | custom-call | flops 10737418240 | bytes 4063232 | tf_op jit(solution)/shard_map/pallas_call | solution.py:140
  110.2 3.6 %collective-permute-start.27 = (bf16[192,512]{1,0:T(8,128)(2,1)S(1)}, bf16[192,512]{1,0:T(8,128)(2,1)S(1)}, u32[]{:S(2)}, u32[]{:S(2)}) collective-permute-start(bf16[192,512]{1,0:T(8,128)(2,1)S(1)} %get-tuple-element.111), channel_id=1, source_target_pairs={{0,4},{1,5},{2,6},{3,7},{4,0},{5,1},{6,2},{7,3},{8,12},{9,13},{10,... | collective-permute-start | bytes 589832 | tf_op jit(solution)/shard_map/ppermute | solution.py:128
  113.7 23.0 %shard_map.119 = (bf16[192,512]{1,0:T(8,128)(2,1)S(1)}, bf16[192,512]{1,0:T(8,128)(2,1)S(1)}, bf16[192,512]{1,0:T(8,128)(2,1)S(1)}, bf16[192,512]{1,0:T(8,128)(2...) custom-call(bf16[192,512]{1,0:T(8,128)(2,1)S(1)} %get-tuple-element., ...), custom_call_target="tpu_custom_call" | custom-call | flops 21474836480 | bytes 6422528 | tf_op jit(solution)/shard_map/pallas_call | solution.py:140
  149.5 4.6 %collective-permute-start.31 = (bf16[192,512]{1,0:T(8,128)(2,1)S(1)}, bf16[192,512]{1,0:T(8,128)(2,1)S(1)}, u32[]{:S(2)}, u32[]{:S(2)}) collective-permute-start(bf16[192,512]{1,0:T(8,128)(2,1)S(1)} %get-tuple-element.124), channel_id=1, source_target_pairs={{0,16},{8,24},{16,0},{24,8},{32,48},{40,56},{48,32},{56,40},{64,80... | collective-permute-start | bytes 589832 | tf_op jit(solution)/shard_map/ppermute | solution.py:94
  158.2 6.6 %collective-permute-done.32.refs_3_ = bf16[192,512]{1,0:T(8,128)(2,1)S(1)} collective-permute-done((bf16[192,512]{1,0:T(8,128)(2,1)S(1)}, bf16[192,512]{1,0:T(8,128)(2,1)S(1)}, u32[]{:S(2)}, u32[]{:S(2)}) %collective-permute-start.32) | collective-permute-done | bytes 196640 | tf_op jit(solution)/shard_map/ppermute | solution.py:94
  169.5 3.7 %all-to-all-start = ((bf16[16,48,1536]{2,1,0:T(8,128)(2,1)}), bf16[16,48,1536]{2,1,0:T(8,128)(2,1)S(1)}, u32[]{:S(2)}, u32[]{:S(2)}) async-start(bf16[16,48,1536]{2,1,0:T(8,128)(2,1)} %bitcast.13), calls=%async_computation | async-start | bytes 4718592 | tf_op jit(solution)/shard_map/all_to_all | solution.py:648
  190.2 5.4 %shard_map.124 = (bf16[192,512]{1,0:T(8,128)(2,1)}, f32[31,192]{1,0:T(8,128)S(1)}) custom-call(bf16[192,128]{1,0:T(8,128)(2,1)S(1)} %copy-done.9, bf16[192,512]{1,0:T(8,128)(2,1)S(1)} %fusion.6.own_ref, bf16[192,128]{1,0:T(8,128)(2,1)S(1)} %copy-done.11, bf16[192,512]{1,0:T(8,128)(2,1)S(1)} %copy-done.5, f32[31,192]{1,0:T(8,128)S(1)} %copy-done.7), custom_call_target="tpu_custom_call" | custom-call | flops 48758784 | bytes 735744 | tf_op jit(solution)/shard_map/pallas_call | solution.py:140
  198.4 9.1 %all-to-all-done.in_ref = bf16[16,48,1536]{2,1,0:T(8,128)(2,1)S(1)} async-done(((bf16[16,48,1536]{2,1,0:T(8,128)(2,1)}), bf16[16,48,1536]{2,1,0:T(8,128)(2,1)S(1)}, u32[]{:S(2)}, u32[]{:S(2)}) %all-to-all-start) | async-done | bytes 2359328 | tf_op jit(solution)/shard_map/all_to_all | solution.py:648
  213.2 3.0 %collective-permute-done.47 = bf16[24,1664]{1,0:T(8,128)(2,1)S(1)} collective-permute-done((bf16[24,1664]{1,0:T(8,128)(2,1)S(1)}, bf16[24,1664]{1,0:T(8,128)(2,1)S(1)}, u32[]{:S(2)}, u32[]{:S(2)}) %collective-permute-start.47) | collective-permute-done | bytes 79904 | tf_op jit(solution)/shard_map/ppermute | solution.py:101
  216.6 4.5 %collective-permute-start.42 = (bf16[24,1664]{1,0:T(8,128)(2,1)S(1)}, bf16[24,1664]{1,0:T(8,128)(2,1)S(1)}, u32[]{:S(2)}, u32[]{:S(2)}) collective-permute-start(bf16[24,1664]{1,0:T(8,128)(2,1)S(1)} %get-tuple-element.150), channel_id=1, source_target_pairs={{0,16},{8,24},{16,0},{24,8},{32,48},{40,56},{48,32},{56,40},{64,80... | collective-permute-start | bytes 239624 | tf_op jit(solution)/shard_map/ppermute | solution.py:94
  222.6 11.4 %collective-permute-done.41 = bf16[24,1664]{1,0:T(8,128)(2,1)S(1)} collective-permute-done((bf16[24,1664]{1,0:T(8,128)(2,1)S(1)}, bf16[24,1664]{1,0:T(8,128)(2,1)S(1)}, u32[]{:S(2)}, u32[]{:S(2)}) %collective-permute-start.41) | collective-permute-done | bytes 79904 | tf_op jit(solution)/shard_map/ppermute | solution.py:94
  234.8 3.8 %collective-permute-start.45 = (bf16[4,24,1664]{2,1,0:T(8,128)(2,1)S(1)}, bf16[4,24,1664]{2,1,0:T(8,128)(2,1)S(1)}, u32[]{:S(2)}, u32[]{:S(2)}) collective-permute-start(bf16[4,24,1664]{2,1,0:T(8,128)(2,1)S(1)} %pad_maximum_fusion.2.refs_0_), channel_id=1, source_target_pairs={{0,64},{8,72},{16,80},{24,88},{32,96},{40,104},{48,112},{56,120},{... | collective-permute-start | bytes 958472 | tf_op jit(solution)/shard_map/ppermute | solution.py:101
  242.3 4.7 %collective-permute-done.45.refs_2_ = bf16[4,24,1664]{2,1,0:T(8,128)(2,1)S(1)} collective-permute-done((bf16[4,24,1664]{2,1,0:T(8,128)(2,1)S(1)}, bf16[4,24,1664]{2,1,0:T(8,128)(2,1)S(1)}, u32[]{:S(2)}, u32[]{:S(2)}) %collective-permute-start.45) | collective-permute-done | bytes 319520 | tf_op jit(solution)/shard_map/ppermute | solution.py:101
  247.0 3.7 %shard_map.126 = (f32[3,192,1536]{2,1,0:T(8,128)}, f32[192,1536]{1,0:T(8,128)}, f32[48,128]{1,0:T(8,128)S(1)}) custom-call(bf16[4,24,1664]{2,1,0:T(8,128)(2,1)S(1)} %pad_maximum_fusion.2.refs_0_, bf16[4,24,1664]{2,1,0:T(8,128)(2,1)S(1)} %collective-permute-done.44.refs_1_, bf16[4,24,1664]{2,1,0:T(8,128)(2,1)S(1)} %collective-permute-done.45.refs_2_, ...), custom_call_target="tpu_custom_call" | custom-call | bytes 7299072 | tf_op jit(solution)/shard_map/pallas_call | solution.py:140
  (165 shorter events, 95.1 us)
Async XLA Ops:
  0.7 20.5 %collective-permute-start = (bf16[192,512]{1,0:T(8,128)(2,1)}, bf16[192,512]{1,0:T(8,128)(2,1)S(1)}, u32[]{:S(2)}, u32[]{:S(2)}) collective-permute-start(bf16[192,512]{1,0:T(8,128)(2,1)} %b0), channel_id=1, source_target_pairs={{0,2},{1,3},{2,4},{3,5},{4,6},{5,7},{6,0},{7,1},{8,10},{9,11},{10,... | collective-permute-start | bytes 589832 | tf_op jit(solution)/shard_map/ppermute | solution.py:128
  2.4 18.7 %collective-permute-start.1 = (bf16[192,512]{1,0:T(8,128)(2,1)}, bf16[192,512]{1,0:T(8,128)(2,1)S(1)}, u32[]{:S(2)}, u32[]{:S(2)}) collective-permute-start(bf16[192,512]{1,0:T(8,128)(2,1)} %b0), channel_id=1, source_target_pairs={{0,4},{1,5},{2,6},{3,7},{4,0},{5,1},{6,2},{7,3},{8,12},{9,13},{10,... | collective-permute-start | bytes 589832 | tf_op jit(solution)/shard_map/ppermute | solution.py:128
  5.3 15.9 %collective-permute-start.2 = (bf16[192,512]{1,0:T(8,128)(2,1)}, bf16[192,512]{1,0:T(8,128)(2,1)S(1)}, u32[]{:S(2)}, u32[]{:S(2)}) collective-permute-start(bf16[192,512]{1,0:T(8,128)(2,1)} %b0), channel_id=1, source_target_pairs={{0,6},{1,7},{2,0},{3,1},{4,2},{5,3},{6,4},{7,5},{8,14},{9,15},{10,... | collective-permute-start | bytes 589832 | tf_op jit(solution)/shard_map/ppermute | solution.py:128
  35.7 13.1 %collective-permute-start.9 = (bf16[768,512]{1,0:T(8,128)(2,1)S(1)}, bf16[768,512]{1,0:T(8,128)(2,1)S(1)}, u32[]{:S(2)}, u32[]{:S(2)}) collective-permute-start(bf16[768,512]{1,0:T(8,128)(2,1)S(1)} %pad_maximum_fusion.1), channel_id=1, source_target_pairs={{0,1},{1,0},{2,3},{3,2},{4,5},{5,4},{6,7},{7,6},{8,9},{9,8},{10,11... | collective-permute-start | bytes 2359304 | tf_op jit(solution)/shard_map/ppermute | solution.py:133
  37.3 21.7 %collective-permute-start.13 = (bf16[384,512]{1,0:T(8,128)(2,1)S(1)}, bf16[384,512]{1,0:T(8,128)(2,1)S(1)}, u32[]{:S(2)}, u32[]{:S(2)}) collective-permute-start(bf16[384,512]{1,0:T(8,128)(2,1)S(1)} %get-tuple-element.88.refs_4_.kv_ref), channel_id=1, source_target_pairs={{0,32},{8,40},{16,48},{24,56},{32,64},{40,72},{48,80},{56,88},{64,... | collective-permute-start | bytes 1179656 | tf_op jit(solution)/shard_map/ppermute | solution.py:101
  39.2 21.4 %collective-permute-start.14 = (bf16[384,512]{1,0:T(8,128)(2,1)S(1)}, bf16[384,512]{1,0:T(8,128)(2,1)S(1)}, u32[]{:S(2)}, u32[]{:S(2)}) collective-permute-start(bf16[384,512]{1,0:T(8,128)(2,1)S(1)} %get-tuple-element.88.refs_4_.kv_ref), channel_id=1, source_target_pairs={{0,64},{8,72},{16,80},{24,88},{32,96},{40,104},{48,112},{56,120},{... | collective-permute-start | bytes 1179656 | tf_op jit(solution)/shard_map/ppermute | solution.py:101
  42.8 17.8 %collective-permute-start.15 = (bf16[384,512]{1,0:T(8,128)(2,1)S(1)}, bf16[384,512]{1,0:T(8,128)(2,1)S(1)}, u32[]{:S(2)}, u32[]{:S(2)}) collective-permute-start(bf16[384,512]{1,0:T(8,128)(2,1)S(1)} %get-tuple-element.88.refs_4_.kv_ref), channel_id=1, source_target_pairs={{0,96},{8,104},{16,112},{24,120},{32,0},{40,8},{48,16},{56,24},{64... | collective-permute-start | bytes 1179656 | tf_op jit(solution)/shard_map/ppermute | solution.py:101
  54.7 26.4 %collective-permute-start.16 = (bf16[192,512]{1,0:T(8,128)(2,1)S(1)}, bf16[192,512]{1,0:T(8,128)(2,1)S(1)}, u32[]{:S(2)}, u32[]{:S(2)}) collective-permute-start(bf16[192,512]{1,0:T(8,128)(2,1)S(1)} %get-tuple-element.93.refs_0_.refs_8_), channel_id=1, source_target_pairs={{0,8},{8,16},{16,24},{24,0},{32,40},{40,48},{48,56},{56,32},{64,72... | collective-permute-start | bytes 589832 | tf_op jit(solution)/shard_map/ppermute | solution.py:94
  57.7 23.3 %collective-permute-start.17 = (bf16[192,512]{1,0:T(8,128)(2,1)S(1)}, bf16[192,512]{1,0:T(8,128)(2,1)S(1)}, u32[]{:S(2)}, u32[]{:S(2)}) collective-permute-start(bf16[192,512]{1,0:T(8,128)(2,1)S(1)} %get-tuple-element.93.refs_0_.refs_8_), channel_id=1, source_target_pairs={{0,16},{8,24},{16,0},{24,8},{32,48},{40,56},{48,32},{56,40},{64,80... | collective-permute-start | bytes 589832 | tf_op jit(solution)/shard_map/ppermute | solution.py:94
  59.0 22.1 %collective-permute-start.18 = (bf16[192,512]{1,0:T(8,128)(2,1)S(1)}, bf16[192,512]{1,0:T(8,128)(2,1)S(1)}, u32[]{:S(2)}, u32[]{:S(2)}) collective-permute-start(bf16[192,512]{1,0:T(8,128)(2,1)S(1)} %get-tuple-element.93.refs_0_.refs_8_), channel_id=1, source_target_pairs={{0,24},{8,0},{16,8},{24,16},{32,56},{40,32},{48,40},{56,48},{64,88... | collective-permute-start | bytes 589832 | tf_op jit(solution)/shard_map/ppermute | solution.py:94
  89.4 16.6 %collective-permute-start.22 = (bf16[192,512]{1,0:T(8,128)(2,1)S(1)}, bf16[192,512]{1,0:T(8,128)(2,1)S(1)}, u32[]{:S(2)}, u32[]{:S(2)}) collective-permute-start(bf16[192,512]{1,0:T(8,128)(2,1)S(1)} %get-tuple-element.104), channel_id=1, source_target_pairs={{0,24},{8,0},{16,8},{24,16},{32,56},{40,32},{48,40},{56,48},{64,88... | collective-permute-start | bytes 589832 | tf_op jit(solution)/shard_map/ppermute | solution.py:94
  93.0 13.0 %collective-permute-start.24 = (bf16[192,512]{1,0:T(8,128)(2,1)S(1)}, bf16[192,512]{1,0:T(8,128)(2,1)S(1)}, u32[]{:S(2)}, u32[]{:S(2)}) collective-permute-start(bf16[192,512]{1,0:T(8,128)(2,1)S(1)} %get-tuple-element.106), channel_id=1, source_target_pairs={{0,8},{8,16},{16,24},{24,0},{32,40},{40,48},{48,56},{56,32},{64,72... | collective-permute-start | bytes 589832 | tf_op jit(solution)/shard_map/ppermute | solution.py:94
  109.8 30.9 %collective-permute-start.26 = (bf16[192,512]{1,0:T(8,128)(2,1)S(1)}, bf16[192,512]{1,0:T(8,128)(2,1)S(1)}, u32[]{:S(2)}, u32[]{:S(2)}) collective-permute-start(bf16[192,512]{1,0:T(8,128)(2,1)S(1)} %get-tuple-element.110), channel_id=1, source_target_pairs={{0,2},{1,3},{2,4},{3,5},{4,6},{5,7},{6,0},{7,1},{8,10},{9,11},{10,... | collective-permute-start | bytes 589832 | tf_op jit(solution)/shard_map/ppermute | solution.py:128
  110.2 31.7 %collective-permute-start.27 = (bf16[192,512]{1,0:T(8,128)(2,1)S(1)}, bf16[192,512]{1,0:T(8,128)(2,1)S(1)}, u32[]{:S(2)}, u32[]{:S(2)}) collective-permute-start(bf16[192,512]{1,0:T(8,128)(2,1)S(1)} %get-tuple-element.111), channel_id=1, source_target_pairs={{0,4},{1,5},{2,6},{3,7},{4,0},{5,1},{6,2},{7,3},{8,12},{9,13},{10,... | collective-permute-start | bytes 589832 | tf_op jit(solution)/shard_map/ppermute | solution.py:128
  113.7 30.4 %collective-permute-start.28 = (bf16[192,512]{1,0:T(8,128)(2,1)S(1)}, bf16[192,512]{1,0:T(8,128)(2,1)S(1)}, u32[]{:S(2)}, u32[]{:S(2)}) collective-permute-start(bf16[192,512]{1,0:T(8,128)(2,1)S(1)} %get-tuple-element.112), channel_id=1, source_target_pairs={{0,6},{1,7},{2,0},{3,1},{4,2},{5,3},{6,4},{7,5},{8,14},{9,15},{10,... | collective-permute-start | bytes 589832 | tf_op jit(solution)/shard_map/ppermute | solution.py:128
  136.8 28.1 %collective-permute-start.33 = (bf16[384,512]{1,0:T(8,128)(2,1)S(1)}, bf16[384,512]{1,0:T(8,128)(2,1)S(1)}, u32[]{:S(2)}, u32[]{:S(2)}) collective-permute-start(bf16[384,512]{1,0:T(8,128)(2,1)S(1)} %get-tuple-element.127), channel_id=1, source_target_pairs={{0,96},{8,104},{16,112},{24,120},{32,0},{40,8},{48,16},{56,24},{64... | collective-permute-start | bytes 1179656 | tf_op jit(solution)/shard_map/ppermute | solution.py:101
  139.5 25.4 %collective-permute-start.34 = (bf16[384,512]{1,0:T(8,128)(2,1)S(1)}, bf16[384,512]{1,0:T(8,128)(2,1)S(1)}, u32[]{:S(2)}, u32[]{:S(2)}) collective-permute-start(bf16[384,512]{1,0:T(8,128)(2,1)S(1)} %get-tuple-element.128), channel_id=1, source_target_pairs={{0,64},{8,72},{16,80},{24,88},{32,96},{40,104},{48,112},{56,120},{... | collective-permute-start | bytes 1179656 | tf_op jit(solution)/shard_map/ppermute | solution.py:101
  140.6 24.3 %collective-permute-start.35 = (bf16[384,512]{1,0:T(8,128)(2,1)S(1)}, bf16[384,512]{1,0:T(8,128)(2,1)S(1)}, u32[]{:S(2)}, u32[]{:S(2)}) collective-permute-start(bf16[384,512]{1,0:T(8,128)(2,1)S(1)} %get-tuple-element.129), channel_id=1, source_target_pairs={{0,32},{8,40},{16,48},{24,56},{32,64},{40,72},{48,80},{56,88},{64,... | collective-permute-start | bytes 1179656 | tf_op jit(solution)/shard_map/ppermute | solution.py:101
  169.5 38.1 %all-to-all-start = ((bf16[16,48,1536]{2,1,0:T(8,128)(2,1)}), bf16[16,48,1536]{2,1,0:T(8,128)(2,1)S(1)}, u32[]{:S(2)}, u32[]{:S(2)}) async-start(bf16[16,48,1536]{2,1,0:T(8,128)(2,1)} %bitcast.13), calls=%async_computation | async-start | bytes 4718592 | tf_op jit(solution)/shard_map/all_to_all | solution.py:648
  182.1 13.4 %collective-permute-start.38 = (bf16[208,512]{1,0:T(8,128)(2,1)}, bf16[208,512]{1,0:T(8,128)(2,1)}, u32[]{:S(2)}, u32[]{:S(2)}) collective-permute-start(bf16[208,512]{1,0:T(8,128)(2,1)} %get-tuple-element.140), channel_id=1, source_target_pairs={{0,2},{1,3},{2,4},{3,5},{4,6},{5,7},{6,0},{7,1},{8,10},{9,11},{10,... | collective-permute-start | bytes 638984 | tf_op jit(solution)/shard_map/ppermute | solution.py:128
  216.3 22.3 %collective-permute-start.50 = (bf16[4,24,1664]{2,1,0:T(8,128)(2,1)S(1)}, bf16[4,24,1664]{2,1,0:T(8,128)(2,1)S(1)}, u32[]{:S(2)}, u32[]{:S(2)}) collective-permute-start(bf16[4,24,1664]{2,1,0:T(8,128)(2,1)S(1)} %pad_maximum_fusion.3.refs_4_), channel_id=1, source_target_pairs={{0,8},{8,16},{16,24},{24,0},{32,40},{40,48},{48,56},{56,32},{64,72... | collective-permute-start | bytes 958472 | tf_op jit(solution)/shard_map/ppermute | solution.py:94
  216.4 17.6 %collective-permute-start.41 = (bf16[24,1664]{1,0:T(8,128)(2,1)S(1)}, bf16[24,1664]{1,0:T(8,128)(2,1)S(1)}, u32[]{:S(2)}, u32[]{:S(2)}) collective-permute-start(bf16[24,1664]{1,0:T(8,128)(2,1)S(1)} %get-tuple-element.150), channel_id=1, source_target_pairs={{0,8},{8,16},{16,24},{24,0},{32,40},{40,48},{48,56},{56,32},{64,72... | collective-permute-start | bytes 239624 | tf_op jit(solution)/shard_map/ppermute | solution.py:94
  216.6 17.4 %collective-permute-start.42 = (bf16[24,1664]{1,0:T(8,128)(2,1)S(1)}, bf16[24,1664]{1,0:T(8,128)(2,1)S(1)}, u32[]{:S(2)}, u32[]{:S(2)}) collective-permute-start(bf16[24,1664]{1,0:T(8,128)(2,1)S(1)} %get-tuple-element.150), channel_id=1, source_target_pairs={{0,16},{8,24},{16,0},{24,8},{32,48},{40,56},{48,32},{56,40},{64,80... | collective-permute-start | bytes 239624 | tf_op jit(solution)/shard_map/ppermute | solution.py:94
  221.1 17.6 %collective-permute-start.51 = (bf16[4,24,1664]{2,1,0:T(8,128)(2,1)S(1)}, bf16[4,24,1664]{2,1,0:T(8,128)(2,1)S(1)}, u32[]{:S(2)}, u32[]{:S(2)}) collective-permute-start(bf16[4,24,1664]{2,1,0:T(8,128)(2,1)S(1)} %pad_maximum_fusion.3.refs_4_), channel_id=1, source_target_pairs={{0,16},{8,24},{16,0},{24,8},{32,48},{40,56},{48,32},{56,40},{64,80... | collective-permute-start | bytes 958472 | tf_op jit(solution)/shard_map/ppermute | solution.py:94
  (52 other events, 504.9 us)
